TPU v7x, 32 devices: a whole 2x2x4 slice. The times are simulated.
32 devices in a mesh: particle: 8 (over y, x, core), slab: 4 (over z).
Axes of the slice: x: 2, y: 2, z: 4, core: 2. Of those that a mesh axis runs over, the one named last changes fastest.
Arguments:
- vel_coarse: float32 [8, 16, 8, 64], P('particle', 'slab'), may hold values from 1.5 to 3.5
- fwd_prev: float32 [8, 32, 16, 128], P('particle', 'slab'), may hold values from -6 to 6
- fwd_cur: float32 [8, 32, 16, 128], P('particle', 'slab'), may hold values from -6 to 6
- adj_far: float32 [8, 32, 16, 128], P('particle', 'slab'), may hold values from -6 to 6
- adj_near: float32 [8, 32, 16, 128], P('particle', 'slab'), may hold values from -6 to 6
- src_cell: int32 [8], P('particle'), may hold values from 0 to 65535
- src_step: int32 [8], P('particle'), may hold values from 0 to 61
- wavelet: float32 [64], replicated, may hold values from -24 to 24
- rec_cell: int32 [256], replicated, may hold values from 0 to 65535
- observed: float32 [2, 256], replicated, may hold values from -6 to 6
Outputs:
- update: float32 [8, 16, 8, 64], P('particle', 'slab')
- misfit: float32 [8, 2, 256], P('particle')
Inputs may be any that keep to these rules, and one draw needn't show every extreme that they name: `src_cell`: a flat index (x 16 + y) * 128 + z of the grid. The wavelet samples used are src_step + 1 and src_step + 2. `rec_cell`: flat indices as for src_cell; cells may repeat.
All inputs are finite; a program needn't handle non-finite values.
Results may differ from a plain program's by a relative error of at most 0.00028.
Values sent between devices are 32-bit elements; how exact they have to be, the bound alone decides.
No kernel may reach another device: no remote copies, remote signals or barrier semaphores. Data moves between devices by JAX's collectives and lax.ppermute only.
A program may use at most 64 MiB of HBM per device.

v0:
```python
import jax
import jax.numpy as jnp
from jax import lax
from jax.sharding import PartitionSpec as P

STENCIL_WEIGHTS = (-205.0 / 72.0, 8.0 / 5.0, -1.0 / 5.0, 8.0 / 315.0, -1.0 / 560.0)
COURANT_FACTOR = 0.1


def with_halo(block, sides, width):
    for axis, dim in sides:
        count = lax.axis_size(axis)
        forward = [(i, i + 1) for i in range(count - 1)]
        backward = [(target, source) for source, target in forward]
        low = lax.ppermute(
            lax.slice_in_dim(block, block.shape[dim] - width, None, axis=dim), axis, forward
        )
        high = lax.ppermute(lax.slice_in_dim(block, 0, width, axis=dim), axis, backward)
        block = jnp.concatenate([low, block, high], axis=dim)
    return block


def laplace(extended):
    length = extended.shape[0] - 8
    size_y = extended.shape[1]
    size_z = extended.shape[2]
    padded = jnp.pad(extended, ((0, 0), (4, 4), (4, 4)))

    def window(shift_x, shift_y, shift_z):
        return padded[
            4 + shift_x : 4 + shift_x + length,
            4 + shift_y : 4 + shift_y + size_y,
            4 + shift_z : 4 + shift_z + size_z,
        ]

    result = 3.0 * STENCIL_WEIGHTS[0] * window(0, 0, 0)
    for offset in range(1, 5):
        pairs = (
            window(offset, 0, 0)
            + window(-offset, 0, 0)
            + (window(0, offset, 0) + window(0, -offset, 0))
            + (window(0, 0, offset) + window(0, 0, -offset))
        )
        result = result + STENCIL_WEIGHTS[offset] * pairs
    return result


def refine(model):
    return jnp.repeat(jnp.repeat(jnp.repeat(model, 2, axis=0), 2, axis=1), 2, axis=2)


def locate(field, anchor, cells):
    plane = field.shape[1] * field.shape[2]
    extent = field.shape[0] * plane
    local_cells = cells - anchor * plane
    valid = (local_cells >= 0) & (local_cells < extent)
    placed = jnp.clip(local_cells, 0, extent - 1)
    return (valid, placed)


def inject(field, anchor, cells, values):
    valid, placed = locate(field, anchor, cells)
    flat = field.reshape(-1).at[placed].add(jnp.where(valid, values, 0.0))
    return flat.reshape(field.shape)


def sample(field, anchor, cells):
    valid, placed = locate(field, anchor, cells)
    return jnp.where(valid, field.reshape(-1)[placed], 0.0)


def advance_once(older, newer, courant_sq, anchor, cells, values):
    extended = with_halo(newer, (("slab", 0),), 4)
    result = 2.0 * newer - older + courant_sq * laplace(extended)
    return inject(result, anchor, cells, values)


def march_pair(older, newer, courant_sq, anchor, cells, values_one, values_two):
    first = advance_once(older, newer, courant_sq, anchor, cells, values_one)
    second = advance_once(newer, first, courant_sq, anchor, cells, values_two)
    return (first, second)


def on_device(
    vel_coarse,
    fwd_prev,
    fwd_cur,
    adj_far,
    adj_near,
    src_cell,
    src_step,
    wavelet,
    rec_cell,
    observed,
):
    model = vel_coarse[0]
    speed = refine(model)
    courant_sq = (COURANT_FACTOR * speed) ** 2
    width_x = fwd_prev.shape[1]
    anchor = lax.axis_index("slab") * width_x
    step_now = src_step[0]
    pulse_one = jnp.take(wavelet, step_now + 1)[None]
    pulse_two = jnp.take(wavelet, step_now + 2)[None]
    prev_field = fwd_prev[0]
    cur_field = fwd_cur[0]
    first, second = march_pair(
        prev_field, cur_field, courant_sq, anchor, src_cell, pulse_one, pulse_two
    )
    samples = jnp.stack([sample(first, anchor, rec_cell), sample(second, anchor, rec_cell)])
    traces = lax.psum(samples, "slab")
    residual = traces - observed
    adj_two, adj_one = march_pair(
        adj_far[0], adj_near[0], courant_sq, anchor, rec_cell, residual[1], residual[0]
    )
    image = adj_two * (second - 2.0 * first + cur_field) + adj_one * (
        first - 2.0 * cur_field + prev_field
    )
    fine_grad = -2.0 / (speed * speed * speed) * image
    size_x, size_y, size_z = model.shape
    grads = fine_grad.reshape(size_x, 2, size_y, 2, size_z, 2).sum(axis=(1, 3, 5))
    count = lax.axis_size("particle")
    cells_coarse = size_x * lax.axis_size("slab") * size_y * size_z
    stacked = jnp.stack([-grads, model])[None]
    gathered = lax.all_gather(stacked, "particle", axis=0, tiled=True)
    partial_rows = jnp.sum((gathered[:, 1] - model[None]) ** 2, axis=(1, 2, 3))
    dist_row = lax.psum(partial_rows, "slab")
    grand = lax.psum(jnp.sum(dist_row), "particle")
    band = grand / (count * (count - 1))
    kernel_row = jnp.exp(-dist_row / band)
    mixed = jnp.einsum("q,qsxyz->sxyz", kernel_row, gathered, precision=lax.Precision.HIGHEST)
    kernel_sum = jnp.sum(kernel_row)
    coef = 2.0 * cells_coarse / band
    update = (mixed[0] + coef * (model * kernel_sum - mixed[1])) / count
    return (update[None], residual[None])


def solution(mesh):
    in_specs = (
        P("particle", "slab", None, None),
        P("particle", "slab", None, None),
        P("particle", "slab", None, None),
        P("particle", "slab", None, None),
        P("particle", "slab", None, None),
        P("particle"),
        P("particle"),
        P(),
        P(),
        P(),
    )
    out_specs = (P("particle", "slab", None, None), P("particle", None, None))
    return jax.shard_map(
        on_device, mesh=mesh, in_specs=in_specs, out_specs=out_specs, check_vma=False
    )
```

profile of v0, /device:TPU:0, one launch (start us, length us, event | category | flops | bytes accessed | tf_op | source)
XLA Modules:
  0.0 127.2 jit_solution(15205556375967248762)
XLA Ops:
  2.8 5.6 %collective-permute-start.3 = (f32[4,16,128]{2,1,0:T(8,128)S(1)}, f32[4,16,128]{2,1,0:T(8,128)S(1)}, u32[]{:S(2)}, u32[]{:S(2)}) collective-permute-start(f32[4,16,128]{2,1,0:T(8,128)S(1)} %get-tuple-element.57), channel_id=1, source_target_pairs={{0,1},{1,2},{2,3},{4,5},{5,6},{6,7},{8,9},{9,10},{10,11},{12,13},{... | collective-permute-start | bytes 98312 | tf_op jit(solution)/shard_map/ppermute | solution.py:15
  10.5 4.6 %collective-permute-start.1 = (f32[4,16,128]{2,1,0:T(8,128)S(1)}, f32[4,16,128]{2,1,0:T(8,128)S(1)}, u32[]{:S(2)}, u32[]{:S(2)}) collective-permute-start(f32[4,16,128]{2,1,0:T(8,128)S(1)} %get-tuple-element.59), channel_id=1, source_target_pairs={{0,1},{1,2},{2,3},{4,5},{5,6},{6,7},{8,9},{9,10},{10,11},{12,13},{... | collective-permute-start | bytes 98312 | tf_op jit(solution)/shard_map/ppermute | solution.py:15
  19.8 1.5 %fusion.65 = f32[8,16,128]{2,1,0:T(8,128)S(1)} fusion(f32[8,16,128]{2,1,0:T(8,128)S(1)} %copy.248, f32[8,16,128]{2,1,0:T(8,128)} %bitcast.82, f32[4,16,128]{2,1,0:T(8,128)S(1)} %collective-permute-done.3, f32[4,16,128]{2,1,0:T(8,128)S(1)} %collective-permute-done.2, f32[16,24,136]{2,1,0:T(8,128)S(1)} %select_maximum_fusion.4, f32[1,8,16,128]{3,2,1,0:T(8,128)} %param.15), kind=kLoop, calls=%fused_computation.132 | loop fusion | flops 671744 | bytes 1376256 | tf_op jit(solution)/shard_map/add | solution.py:74
  21.4 1.5 %fusion.124 = f32[16384]{0:T(1024)S(1)} fusion(f32[16384]{0:T(1024)S(1)} %bitcast.68, s32[]{:T(128)} %bitcast.15, s32[1]{0:T(128)} %maximum_minimum_fusion, pred[1]{0:T(512)(128)(4,1)} %bitcast.18, f32[64]{0:T(128)S(1)} %copy-done.8, s32[]{:T(128)S(6)} %select_n.44, s32[1]{0:T(128)S(6)} %copy.273, s32[1]{0:T(128)} %bitcast.14), kind=kLoop, calls=%fused_computation.248 | loop fusion | flops 9 | bytes 1557 | tf_op jit(solution)/shard_map/scatter-add | solution.py:63
  24.2 4.7 %collective-permute-start.5 = (f32[4,16,128]{2,1,0:T(8,128)S(1)}, f32[4,16,128]{2,1,0:T(8,128)S(1)}, u32[]{:S(2)}, u32[]{:S(2)}) collective-permute-start(f32[4,16,128]{2,1,0:T(8,128)S(1)} %bitcast.91), channel_id=1, source_target_pairs={{0,1},{1,2},{2,3},{4,5},{5,6},{6,7},{8,9},{9,10},{10,11},{12,13},{... | collective-permute-start | bytes 98312 | tf_op jit(solution)/shard_map/ppermute | solution.py:15
  28.9 1.7 %gather_fusion = f32[256]{0:T(256)S(1)} fusion(f32[16384]{0:T(1024)S(1)} %fusion.124, s32[1024]{0:T(1024)S(1)} %pad_clamp_fusion), kind=kCustom, calls=%fused_computation | custom fusion | bytes 3072 | tf_op jit(solution)/shard_map/gather | solution.py:69
  31.7 1.5 %fusion.125 = f32[16384]{0:T(1024)S(1)} fusion(f32[16384]{0:T(1024)S(1)} %bitcast.74, s32[]{:T(128)} %bitcast.15, s32[1]{0:T(128)} %maximum_minimum_fusion, pred[1]{0:T(512)(128)(4,1)} %bitcast.26, f32[64]{0:T(128)S(1)} %copy-done.8, s32[]{:T(128)S(6)} %select_n.48, s32[1]{0:T(128)S(6)} %copy.273, s32[1]{0:T(128)} %bitcast.14), kind=kLoop, calls=%fused_computation.249 | loop fusion | flops 9 | bytes 1557 | tf_op jit(solution)/shard_map/scatter-add | solution.py:63
  33.2 1.7 %gather_fusion.1 = f32[256]{0:T(256)S(1)} fusion(f32[16384]{0:T(1024)S(1)} %fusion.125, s32[1024]{0:T(1024)S(1)} %pad_clamp_fusion), kind=kCustom, calls=%fused_computation.1 | custom fusion | bytes 3072 | tf_op jit(solution)/shard_map/gather | solution.py:69
  35.0 12.4 %psum.21 = f32[2,256]{1,0:T(2,128)S(1)} all-reduce(f32[2,256]{1,0:T(2,128)S(1)} %pad_maximum_fusion.9), channel_id=1, replica_groups=mesh['particle'=8,'slab'=4] {'slab'}, use_global_device_ids=true, to_apply=%region_0.1 | all-reduce | flops 512 | bytes 4096 | tf_op jit(solution)/shard_map/psum | solution.py:110
  47.4 2.1 %scatter_fusion = f32[16384]{0:T(1024)S(1)} fusion(f32[16384]{0:T(1024)S(1)} %bitcast.71, s32[256]{0:T(256)S(1)} %compare_select_fusion, f32[256]{0:T(256)S(1)} %get-tuple-element.63), kind=kCustom, calls=%fused_computation.2 | custom fusion | flops 256 | bytes 4096 | tf_op jit(solution)/shard_map/scatter-add | solution.py:63
  50.8 4.5 %collective-permute-start.7 = (f32[4,16,128]{2,1,0:T(8,128)S(1)}, f32[4,16,128]{2,1,0:T(8,128)S(1)}, u32[]{:S(2)}, u32[]{:S(2)}) collective-permute-start(f32[4,16,128]{2,1,0:T(8,128)S(1)} %bitcast.92), channel_id=1, source_target_pairs={{0,1},{1,2},{2,3},{4,5},{5,6},{6,7},{8,9},{9,10},{10,11},{12,13},{... | collective-permute-start | bytes 98312 | tf_op jit(solution)/shard_map/ppermute | solution.py:15
  56.3 5.5 %reshape.163 = f32[8,16,64,2]{3,2,1,0:T(8,128)} reshape(f32[16384]{0:T(1024)S(1)} %fusion.124) | data formatting | bytes 131072 | tf_op jit(solution)/shard_map/reshape | solution.py:64
  61.8 3.0 %copy.251 = f32[8,16,64,2]{2,1,3,0:T(8,128)S(1)} copy(f32[8,16,64,2]{3,2,1,0:T(8,128)} %reshape.163) | data formatting | bytes 131072 | tf_op jit(solution)/shard_map/reshape | solution.py:64
  64.8 5.5 %reshape.161 = f32[8,16,64,2]{3,2,1,0:T(8,128)} reshape(f32[16384]{0:T(1024)S(1)} %scatter_fusion) | data formatting | bytes 131072 | tf_op jit(solution)/shard_map/reshape | solution.py:64
  70.3 5.5 %reshape.162 = f32[8,16,64,2]{3,2,1,0:T(8,128)} reshape(f32[16384]{0:T(1024)S(1)} %fusion.125) | data formatting | bytes 131072 | tf_op jit(solution)/shard_map/reshape | solution.py:64
  75.8 3.0 %copy.255 = f32[8,16,64,2]{2,1,3,0:T(8,128)S(1)} copy(f32[8,16,64,2]{3,2,1,0:T(8,128)} %reshape.161) | data formatting | bytes 131072 | tf_op jit(solution)/shard_map/reshape | solution.py:64
  78.8 3.0 %copy.252 = f32[8,16,64,2]{2,1,3,0:T(8,128)S(1)} copy(f32[8,16,64,2]{3,2,1,0:T(8,128)} %reshape.162) | data formatting | bytes 131072 | tf_op jit(solution)/shard_map/reshape | solution.py:64
  82.3 2.2 %scatter_fusion.1 = f32[16384]{0:T(1024)S(1)} fusion(f32[16384]{0:T(1024)S(1)} %bitcast.75, s32[256]{0:T(256)S(1)} %compare_select_fusion, f32[256]{0:T(256)S(1)} %get-tuple-element.62), kind=kCustom, calls=%fused_computation.3 | custom fusion | flops 256 | bytes 4096 | tf_op jit(solution)/shard_map/scatter-add | solution.py:63
  84.5 5.5 %reshape.166 = f32[8,16,64,2]{3,2,1,0:T(8,128)} reshape(f32[16384]{0:T(1024)S(1)} %scatter_fusion.1) | data formatting | bytes 131072 | tf_op jit(solution)/shard_map/reshape | solution.py:64
  90.0 3.0 %copy.261 = f32[8,16,64,2]{2,1,3,0:T(8,128)S(1)} copy(f32[8,16,64,2]{3,2,1,0:T(8,128)} %reshape.166) | data formatting | bytes 131072 | tf_op jit(solution)/shard_map/reshape | solution.py:64
  93.2 9.3 %all-gather = f32[16,4,8,64]{3,2,1,0:T(8,128)S(1)} all-gather(f32[2,4,8,64]{3,2,1,0:T(8,128)S(1)} %pad_maximum_fusion.8), channel_id=2, replica_groups=mesh['particle'=8,'slab'=4] {'particle'}, dimensions={0}, use_global_device_ids=true | all-gather | bytes 147456 | tf_op jit(solution)/shard_map/all_gather | solution.py:124
  102.7 8.3 %psum.22 = f32[8]{0:T(128)S(1)} all-reduce(f32[8]{0:T(128)S(1)} %fusion.7), channel_id=1, replica_groups=mesh['particle'=8,'slab'=4] {'slab'}, use_global_device_ids=true, to_apply=%region_6.7 | all-reduce | flops 8 | bytes 64 | tf_op jit(solution)/shard_map/psum | solution.py:126
  111.6 12.4 %psum.23 = f32[]{:T(128)} all-reduce(f32[]{:T(128)} %reduce_sum.47), channel_id=1, replica_groups=mesh['particle'=8,'slab'=4] {'particle'}, use_global_device_ids=true, to_apply=%region_8.9 | all-reduce | flops 1 | bytes 8 | tf_op jit(solution)/shard_map/psum | solution.py:127
  125.9 1.3 %fusion.123 = f32[1,4,8,64]{3,2,1,0:T(8,128)} fusion(f32[2,4,8,64]{3,2,1,0:T(8,128)S(1)} %bitcast.89, f32[1,4,8,64]{3,2,1,0:T(8,128)S(1)} %copy-done.2, f32[]{:T(128)} %fusion.127, f32[]{:T(128)S(6)} %div.32), kind=kLoop, calls=%fused_computation.239 | loop fusion | flops 10240 | bytes 32776 | tf_op jit(solution)/shard_map/div | solution.py:133
  (67 shorter events, 14.3 us)
Async XLA Ops:
  0.6 30.7 %copy-start = (f32[1,8,16,128]{3,2,1,0:T(8,128)S(1)}, f32[1,8,16,128]{3,2,1,0:T(8,128)}, u32[]{:S(2)}) copy-start(f32[1,8,16,128]{3,2,1,0:T(8,128)} %param.16) | copy-start | bytes 196612
  0.6 30.0 %copy-start.1 = (f32[1,8,16,128]{3,2,1,0:T(8,128)S(1)}, f32[1,8,16,128]{3,2,1,0:T(8,128)}, u32[]{:S(2)}) copy-start(f32[1,8,16,128]{3,2,1,0:T(8,128)} %param.18) | copy-start | bytes 196612
  0.7 30.5 %copy-start.6 = (s32[256]{0:T(256)S(1)}, s32[256]{0:T(256)}, u32[]{:S(2)}) copy-start(s32[256]{0:T(256)} %param.22) | copy-start | bytes 3076
  0.7 20.7 %copy-start.8 = (f32[64]{0:T(128)S(1)}, f32[64]{0:T(128)}, u32[]{:S(2)}) copy-start(f32[64]{0:T(128)} %param.21) | copy-start | bytes 772
  0.7 30.1 %copy-start.4 = (f32[1,8,16,128]{3,2,1,0:T(8,128)S(1)}, f32[1,8,16,128]{3,2,1,0:T(8,128)}, u32[]{:S(2)}) copy-start(f32[1,8,16,128]{3,2,1,0:T(8,128)} %param.17) | copy-start | bytes 196612
  1.5 17.3 %collective-permute-start.2 = (f32[4,16,128]{2,1,0:T(8,128)S(1)}, f32[4,16,128]{2,1,0:T(8,128)S(1)}, u32[]{:S(2)}, u32[]{:S(2)}) collective-permute-start(f32[4,16,128]{2,1,0:T(8,128)S(1)} %get-tuple-element.56), channel_id=1, source_target_pairs={{1,0},{2,1},{3,2},{5,4},{6,5},{7,6},{9,8},{10,9},{11,10},{13,12},{... | collective-permute-start | bytes 98312 | tf_op jit(solution)/shard_map/ppermute | solution.py:18
  2.8 16.0 %collective-permute-start.3 = (f32[4,16,128]{2,1,0:T(8,128)S(1)}, f32[4,16,128]{2,1,0:T(8,128)S(1)}, u32[]{:S(2)}, u32[]{:S(2)}) collective-permute-start(f32[4,16,128]{2,1,0:T(8,128)S(1)} %get-tuple-element.57), channel_id=1, source_target_pairs={{0,1},{1,2},{2,3},{4,5},{5,6},{6,7},{8,9},{9,10},{10,11},{12,13},{... | collective-permute-start | bytes 98312 | tf_op jit(solution)/shard_map/ppermute | solution.py:15
  9.2 21.4 %collective-permute-start = (f32[4,16,128]{2,1,0:T(8,128)S(1)}, f32[4,16,128]{2,1,0:T(8,128)S(1)}, u32[]{:S(2)}, u32[]{:S(2)}) collective-permute-start(f32[4,16,128]{2,1,0:T(8,128)S(1)} %get-tuple-element.58), channel_id=1, source_target_pairs={{1,0},{2,1},{3,2},{5,4},{6,5},{7,6},{9,8},{10,9},{11,10},{13,12},{... | collective-permute-start | bytes 98312 | tf_op jit(solution)/shard_map/ppermute | solution.py:18
  10.5 20.1 %collective-permute-start.1 = (f32[4,16,128]{2,1,0:T(8,128)S(1)}, f32[4,16,128]{2,1,0:T(8,128)S(1)}, u32[]{:S(2)}, u32[]{:S(2)}) collective-permute-start(f32[4,16,128]{2,1,0:T(8,128)S(1)} %get-tuple-element.59), channel_id=1, source_target_pairs={{0,1},{1,2},{2,3},{4,5},{5,6},{6,7},{8,9},{9,10},{10,11},{12,13},{... | collective-permute-start | bytes 98312 | tf_op jit(solution)/shard_map/ppermute | solution.py:15
  17.4 29.9 %copy-start.7 = (f32[2,256]{1,0:T(2,128)S(1)}, f32[2,256]{1,0:T(2,128)}, u32[]{:S(2)}) copy-start(f32[2,256]{1,0:T(2,128)} %param.23) | copy-start | bytes 6148
  22.9 8.3 %collective-permute-start.4 = (f32[4,16,128]{2,1,0:T(8,128)S(1)}, f32[4,16,128]{2,1,0:T(8,128)S(1)}, u32[]{:S(2)}, u32[]{:S(2)}) collective-permute-start(f32[4,16,128]{2,1,0:T(8,128)S(1)} %bitcast.93), channel_id=1, source_target_pairs={{1,0},{2,1},{3,2},{5,4},{6,5},{7,6},{9,8},{10,9},{11,10},{13,12},{... | collective-permute-start | bytes 98312 | tf_op jit(solution)/shard_map/ppermute | solution.py:18
  24.2 31.4 %copy-start.3 = (f32[1,8,16,128]{3,2,1,0:T(8,128)S(1)}, f32[1,8,16,128]{3,2,1,0:T(8,128)}, u32[]{:S(2)}) copy-start(f32[1,8,16,128]{3,2,1,0:T(8,128)} %param.15) | copy-start | bytes 196612
  24.2 7.0 %collective-permute-start.5 = (f32[4,16,128]{2,1,0:T(8,128)S(1)}, f32[4,16,128]{2,1,0:T(8,128)S(1)}, u32[]{:S(2)}, u32[]{:S(2)}) collective-permute-start(f32[4,16,128]{2,1,0:T(8,128)S(1)} %bitcast.91), channel_id=1, source_target_pairs={{0,1},{1,2},{2,3},{4,5},{5,6},{6,7},{8,9},{9,10},{10,11},{12,13},{... | collective-permute-start | bytes 98312 | tf_op jit(solution)/shard_map/ppermute | solution.py:15
  47.3 14.5 %copy-start.5 = (f32[2,256]{1,0:T(2,128)}, f32[2,256]{1,0:T(2,128)S(1)}, u32[]{:S(2)}) copy-start(f32[2,256]{1,0:T(2,128)S(1)} %sub.64) | copy-start | bytes 6148
  49.5 32.3 %collective-permute-start.6 = (f32[4,16,128]{2,1,0:T(8,128)S(1)}, f32[4,16,128]{2,1,0:T(8,128)S(1)}, u32[]{:S(2)}, u32[]{:S(2)}) collective-permute-start(f32[4,16,128]{2,1,0:T(8,128)S(1)} %bitcast.94), channel_id=1, source_target_pairs={{1,0},{2,1},{3,2},{5,4},{6,5},{7,6},{9,8},{10,9},{11,10},{13,12},{... | collective-permute-start | bytes 98312 | tf_op jit(solution)/shard_map/ppermute | solution.py:18
  50.8 31.0 %collective-permute-start.7 = (f32[4,16,128]{2,1,0:T(8,128)S(1)}, f32[4,16,128]{2,1,0:T(8,128)S(1)}, u32[]{:S(2)}, u32[]{:S(2)}) collective-permute-start(f32[4,16,128]{2,1,0:T(8,128)S(1)} %bitcast.92), channel_id=1, source_target_pairs={{0,1},{1,2},{2,3},{4,5},{5,6},{6,7},{8,9},{9,10},{10,11},{12,13},{... | collective-permute-start | bytes 98312 | tf_op jit(solution)/shard_map/ppermute | solution.py:15
  84.5 8.7 %copy-start.2 = (f32[1,4,8,64]{3,2,1,0:T(8,128)S(1)}, f32[1,4,8,64]{3,2,1,0:T(8,128)}, u32[]{:S(2)}) copy-start(f32[1,4,8,64]{3,2,1,0:T(8,128)} %param.14) | copy-start | bytes 24580
where the time goes:
time: 128 us; the launch traced here: 127 us
  blocking collectives  42.5 us (33%)
  local copies, waits for them, and re-layouts  41.1 us (32%)
  starting transfers between devices  24.5 us (19%)
  other arithmetic  15 us (12%)
  between operations  3.64 us (3%)
    reshape x8, local copies, waits for them, and re-layouts, inject(): return flat.reshape(field.shape)  33.9 us
    ppermute x4, starting transfers between devices, with_halo(): lax.ppermute(lax.slice_in_dim(block, block.shape[dim] - width, None, axis...  19.4 us
    psum x1, blocking collectives, on_device(): grand = lax.psum(jnp.sum(dist_row), 'particle')  12.4 us
    psum x1, blocking collectives, on_device(): traces = lax.psum(samples, 'slab')  12.4 us
    all_gather x1, blocking collectives, on_device(): gathered = lax.all_gather(stacked, 'particle', axis=0, tiled=True)  9.31 us
    psum x1, blocking collectives, on_device(): dist_row = lax.psum(partial_rows, 'slab')  8.35 us
    scatter-add x4, other arithmetic, inject(): flat = field.reshape(-1).at[placed].add(jnp.where(valid, values, 0.0))  7.28 us
    ppermute x4, starting transfers between devices, with_halo(): lax.ppermute(lax.slice_in_dim(block, 0, width, axis=dim), axis, backward)  5.14 us
  transfers between devices with their start and end apart: 8, of which 0 were waited for; matrix products, arithmetic and copies ran while one was open for 28% of the time, Pallas kernels for 0%

commit v1 on v0

v1 whole, which is shorter than its diff:
```python
import jax
import jax.numpy as jnp
from jax import lax
from jax.experimental import pallas as pl
from jax.experimental.pallas import tpu as pltpu
from jax.sharding import PartitionSpec as P

STENCIL_WEIGHTS = (-205.0 / 72.0, 8.0 / 5.0, -1.0 / 5.0, 8.0 / 315.0, -1.0 / 560.0)
COURANT_FACTOR = 0.1
REACH = 4
PITCH = 32
HIGHEST = lax.Precision.HIGHEST


def swap(block, axis, pairs):
    both = [(a, b) for a, b in pairs] + [(b, a) for a, b in pairs]
    return lax.ppermute(block, axis, both)


def twice(model):
    flat = model.reshape(model.shape[0] * model.shape[1], model.shape[2])
    return jnp.concatenate([flat, flat], axis=1)


def pack_kernel(prev, cur, near, far, vel, to_one, to_two, to_far):
    width = prev.shape[0]
    place = lax.axis_index("slab")
    odd = place % 2
    top = width - REACH
    model = twice(vel[...]).reshape(-1, prev.shape[1], prev.shape[2])
    for ref, low in ((to_one, odd), (to_two, 1 - odd)):
        ref[0:width] = prev[...]
        ref[width : 2 * width] = cur[...]
        ref[2 * width : 3 * width] = near[...]
        ref[3 * width : 3 * width + REACH] = far[pl.ds((1 - low) * top, REACH)]
        ref[3 * width + REACH :] = model
    to_far[0:REACH] = cur[pl.ds((1 - (place % 4) // 2) * top, REACH)]
    to_far[REACH:] = model


def split3(values):
    high = values.astype(jnp.bfloat16)
    rest = values - high.astype(jnp.float32)
    middle = rest.astype(jnp.bfloat16)
    low = (rest - middle.astype(jnp.float32)).astype(jnp.bfloat16)
    return (high, middle, low)


def wave_kernel(
    src_cell, src_step, wavelet, prev, cur, far, near, vel, rec, obs, one, two, *rest, n_far, with_models
):
    fars = rest[:n_far]
    rest = rest[n_far:]
    if with_models:
        ends, rest = rest[0], rest[1:]
    pay, samples = rest[:2]
    cur_s, prev_s, near_s, far_s, first_s, sec_s, two_s, vel_s, c2_s, img_s = rest[2:]
    width, size_y, size_z = prev.shape
    half = width // 2
    coarse_y = size_y // 2
    place = lax.axis_index("slab")
    odd = place % 2
    f32 = jnp.float32
    data = pl.ds(8, size_y)
    for ref in (cur_s, first_s, near_s, two_s):
        ref[:, 0:8, :] = jnp.zeros((ref.shape[0], 8, size_z), f32)
        ref[:, 8 + size_y : PITCH, :] = jnp.zeros((ref.shape[0], PITCH - 8 - size_y, size_z), f32)
    wide = 2 * REACH
    cur_s[wide + REACH : wide + REACH + width, data, :] = cur[...]
    prev_s[wide : wide + width] = prev[...]
    near_s[wide : wide + width, data, :] = near[...]
    far_s[REACH : REACH + width] = far[...]
    own_vel = twice(vel[...])
    rows = half * coarse_y
    vel_s[rows : 2 * rows] = own_vel

    def put(block, high):
        base = high * (width + wide)
        prev_s[pl.ds(base, width)] = block[0:width]
        cur_s[pl.ds(base + REACH, width), data, :] = block[width : 2 * width]
        near_s[pl.ds(base, width), data, :] = block[2 * width : 3 * width]
        far_s[pl.ds(high * (width + REACH), REACH)] = block[3 * width : 3 * width + REACH]
        model = block[3 * width + REACH :].reshape(rows, size_z)
        vel_s[pl.ds(high * 2 * rows, rows)] = model
        return model

    model_one = put(one, 1 - odd)
    put(two, odd)
    far_high = 1 - (place % 4) // 2
    edge = 2 * wide + width + REACH
    models_far = []
    if n_far == 1:
        zero = jnp.zeros((REACH, size_y, size_z), f32)
        cur_s[pl.ds((1 - far_high) * edge, REACH), data, :] = zero
    for index, block in enumerate(fars):
        high = far_high if index == 0 else 1 - far_high
        cur_s[pl.ds(high * edge, REACH), data, :] = block[0:REACH]
        models_far.append(block[REACH:].reshape(rows, size_z))

    lane = lax.broadcasted_iota(jnp.int32, (1, size_z), 1)
    up_w = [None] + [jnp.where(lane >= k, STENCIL_WEIGHTS[k], 0.0).astype(f32) for k in range(1, 5)]
    down_w = [None] + [
        jnp.where(lane < size_z - k, STENCIL_WEIGHTS[k], 0.0).astype(f32) for k in range(1, 5)
    ]

    grid_r = lax.broadcasted_iota(jnp.int32, (size_z, size_z), 0)
    grid_c = lax.broadcasted_iota(jnp.int32, (size_z, size_z), 1)
    spread = jnp.where(grid_r == grid_c // 2, 1.0, 0.0).astype(f32)
    gather = jnp.where(grid_r // 2 == grid_c, 1.0, 0.0).astype(f32)
    scaled = COURANT_FACTOR * vel_s[...]
    fine_z = jnp.dot(scaled * scaled, spread, precision=HIGHEST, preferred_element_type=f32)
    count = fine_z.shape[0]
    c2_s[pl.ds(0, count, stride=2), :] = fine_z
    c2_s[pl.ds(1, count, stride=2), :] = fine_z

    step = 4

    def courant(layer):
        block = c2_s[layer // 2 * size_y : (layer + step) // 2 * size_y, :]
        block = block.reshape(step // 2, 1, size_y, size_z)
        return jnp.broadcast_to(block, (step // 2, 2, size_y, size_z)).reshape(step, size_y, size_z)

    def laplace(ref, at):
        centre = ref[at : at + step, data, :]
        flat = centre.reshape(step * size_y, size_z)
        total = (3.0 * STENCIL_WEIGHTS[0]) * centre
        for k in range(1, 5):
            pairs = (
                ref[at + k : at + k + step, data, :]
                + ref[at - k : at - k + step, data, :]
                + (ref[at : at + step, pl.ds(8 + k, size_y), :] + ref[at : at + step, pl.ds(8 - k, size_y), :])
            )
            along = pltpu.roll(flat, k, 1) * up_w[k] + pltpu.roll(flat, size_z - k, 1) * down_w[k]
            total = total + STENCIL_WEIGHTS[k] * pairs + along.reshape(step, size_y, size_z)
        return centre, total

    plane = size_y * size_z
    cell = src_cell[0]
    now = src_step[0]
    src_y = (cell % plane) // size_z
    src_z = cell % size_z

    def inject(ref, start, layers, offset, pulse):
        layer = cell // plane - (place * width - start)
        inside = (layer >= 0) & (layer < layers)
        layer = jnp.clip(layer, 0, layers - 1)
        value = jnp.where(inside, pulse, 0.0)
        at = pl.ds(offset + src_y, 1)
        ref[layer, at, :] = ref[layer, at, :] + jnp.where(lane == src_z, value, 0.0)

    for ch in range(0, width + 2 * wide, step):
        centre, total = laplace(cur_s, ch + REACH)
        first_s[ch : ch + step, data, :] = 2.0 * centre - prev_s[ch : ch + step] + courant(ch) * total
    inject(first_s, wide, width + 2 * wide, 8, wavelet[now + 1])
    for ch in range(0, width + 2 * REACH, step):
        centre, total = laplace(first_s, ch + REACH)
        older = cur_s[ch + wide : ch + wide + step, data, :]
        sec_s[ch : ch + step] = 2.0 * centre - older + courant(ch + REACH) * total
    inject(sec_s, REACH, width + 2 * REACH, 0, wavelet[now + 2])

    region = (width + 2 * REACH) * size_y
    cells = rec[...]
    row = (cells - (place * width - REACH) * plane) // size_z
    hot = row == lax.broadcasted_iota(jnp.int32, (region, cells.shape[1]), 0)
    hot = jnp.where(hot, 1.0, 0.0).astype(jnp.bfloat16)
    lanes = lax.broadcasted_iota(jnp.int32, (size_z, cells.shape[1]), 0) == cells % size_z
    lo = REACH * size_y
    hi = lo + width * size_y
    own = (row >= lo) & (row < hi)

    def read(field, marks):
        turned = field.T
        total = sum(jnp.dot(part, marks, preferred_element_type=f32) for part in split3(turned))
        return jnp.sum(jnp.where(lanes, total, 0.0), axis=0, keepdims=True)

    def spread_out(values, marks):
        placed = jnp.where(lanes, values, 0.0)
        dims = (((1,), (1,)), ((), ()))
        return sum(lax.dot_general(marks, part, dims, preferred_element_type=f32) for part in split3(placed))

    first_own = first_s[wide : wide + width, data, :].reshape(width * size_y, size_z)
    read_one = read(first_own, hot[lo:hi])
    read_two = read(sec_s[...].reshape(region, size_z), hot)
    samples[0:1, :] = read_one
    samples[1:2, :] = jnp.where(own, read_two, 0.0)
    add_one = spread_out(read_one - obs[0:1, :], hot[lo:hi])
    add_two = spread_out(read_two - obs[1:2, :], hot)

    for ch in range(0, width + 2 * REACH, step):
        centre, total = laplace(near_s, ch + REACH)
        extra = add_two[ch * size_y : (ch + step) * size_y].reshape(step, size_y, size_z)
        two_s[ch : ch + step, data, :] = (
            2.0 * centre - far_s[ch : ch + step] + courant(ch + REACH) * total + extra
        )
    for ch in range(0, width, step):
        centre, total = laplace(two_s, ch + REACH)
        extra = add_one[ch * size_y : (ch + step) * size_y].reshape(step, size_y, size_z)
        older = near_s[ch + wide : ch + wide + step, data, :]
        adj_one = 2.0 * centre - older + courant(ch + wide) * total + extra
        first = first_s[ch + wide : ch + wide + step, data, :]
        now_field = cur_s[ch + wide + REACH : ch + wide + REACH + step, data, :]
        bend_two = sec_s[ch + REACH : ch + REACH + step] - 2.0 * first + now_field
        bend_one = first - 2.0 * now_field + prev_s[ch + wide : ch + wide + step]
        image = centre * bend_two + adj_one * bend_one
        image = image.reshape(step // 2, 2, size_y, size_z)
        image = image[:, 0] + image[:, 1]
        img_s[ch // 2 * size_y : (ch + step) // 2 * size_y, :] = image.reshape(step // 2 * size_y, size_z)
    folded = img_s[pl.ds(0, rows, stride=2), :] + img_s[pl.ds(1, rows, stride=2), :]
    blocks = jnp.dot(folded, gather, precision=HIGHEST, preferred_element_type=f32)
    factor = 2.0 / (own_vel * own_vel * own_vel)
    left = lane < size_z // 2
    pay[0:rows, :] = jnp.where(left, factor * blocks, own_vel)
    if with_models:
        pay[rows : 2 * rows, :] = jnp.where(left, model_one, models_far[0])
        pay[2 * rows : 3 * rows, :] = jnp.where(left, twice(ends[...]), 0.0)


def mix_kernel(*refs, cells):
    count = len(refs) - 5
    pays = refs[:count]
    part, other, obs, update, misfit = refs[count:]
    f32 = jnp.float32
    misfit[...] = part[...] + other[...] - obs[...]
    rows = update.shape[0] * update.shape[1]
    lane = lax.broadcasted_iota(jnp.int32, (1, pays[0].shape[1]), 1)
    half = update.shape[2]
    model_lane = lane >= half
    total = pays[0].shape[0]
    mean = sum(ref[...] for ref in pays[1:]) + pays[0][...]
    mean = mean * (1.0 / count)

    def norm(diff):
        sq = diff * diff
        sq = jnp.concatenate([jnp.where(model_lane, sq[0:rows], 0.0), sq[rows:]], axis=0)
        sq = jnp.sum(sq.reshape(total // 8, 8, sq.shape[1]), axis=0)
        return jnp.sum(jnp.sum(sq, axis=1, keepdims=True), axis=0, keepdims=True)

    spread = jnp.zeros(mean.shape, f32)
    for ref in pays:
        diff = ref[...] - mean
        spread = spread + diff * diff
    spread = jnp.concatenate([jnp.where(model_lane, spread[0:rows], 0.0), spread[rows:]], axis=0)
    spread = jnp.sum(spread.reshape(total // 8, 8, spread.shape[1]), axis=0)
    spread = jnp.sum(jnp.sum(spread, axis=1, keepdims=True), axis=0, keepdims=True)
    band = (2.0 * count / (count * (count - 1))) * spread
    own = pays[0][...]
    mixed = own[0:rows]
    kernel_sum = jnp.ones((1, 1), f32)
    for ref in pays[1:]:
        weight = jnp.exp(-norm(ref[...] - own) / band)
        mixed = mixed + weight * ref[0:rows, :]
        kernel_sum = kernel_sum + weight
    coef = (2.0 * cells) / band
    pull = coef * (own[0:rows, half:] * kernel_sum - mixed[:, half:])
    update[...] = ((mixed[:, 0:half] + pull) * (1.0 / count)).reshape(update.shape)


def on_device(
    vel_coarse,
    fwd_prev,
    fwd_cur,
    adj_far,
    adj_near,
    src_cell,
    src_step,
    wavelet,
    rec_cell,
    observed,
):
    f32 = jnp.float32
    slabs = lax.axis_size("slab")
    count = lax.axis_size("particle")
    fast = slabs == 4 and count == 8
    model = vel_coarse[0]
    prev, cur, far, near = fwd_prev[0], fwd_cur[0], adj_far[0], adj_near[0]
    width, size_y, size_z = prev.shape
    half, coarse_y, coarse_z = model.shape
    rows = half * coarse_y
    model_layers = rows // size_y
    near_layers = 3 * width + REACH + model_layers
    far_layers = REACH + model_layers
    in_vmem = pl.BlockSpec(memory_space=pltpu.VMEM)
    if fast:
        beside = swap(model, "slab", [(0, 1), (2, 3)])
    to_one, to_two, to_far = pl.pallas_call(
        pack_kernel,
        out_shape=(
            jax.ShapeDtypeStruct((near_layers, size_y, size_z), f32),
            jax.ShapeDtypeStruct((near_layers, size_y, size_z), f32),
            jax.ShapeDtypeStruct((far_layers, size_y, size_z), f32),
        ),
        in_specs=[in_vmem] * 5,
        out_specs=(in_vmem,) * 3,
        name="pack_halos",
    )(prev, cur, near, far, model)
    one = swap(to_one, "slab", [(i, i + 1) for i in range(0, slabs - 1, 2)])
    two = swap(to_two, "slab", [(i, i + 1) for i in range(1, slabs - 1, 2)])
    fars = [swap(to_far, "slab", [(i, i + 2) for i in range(slabs - 2) if i % 4 < 2])]
    others = [(i, i + 2) for i in range(slabs - 2) if i % 4 >= 2]
    if others:
        fars.append(swap(other_side(cur, to_far), "slab", others))
    extra = []
    if fast:
        extra = [swap(beside, "slab", [(0, 2), (1, 3)])]
    in_smem = pl.BlockSpec(memory_space=pltpu.SMEM)
    receivers = rec_cell.shape[0]
    wide = 2 * REACH
    pay_rows = 3 * rows if fast else rows
    pay, samples = pl.pallas_call(
        lambda *refs: wave_kernel(*refs, n_far=len(fars), with_models=fast),
        out_shape=(
            jax.ShapeDtypeStruct((pay_rows, size_z), f32),
            jax.ShapeDtypeStruct((2, receivers), f32),
        ),
        in_specs=[in_smem] * 3 + [in_vmem] * (9 + len(fars) + len(extra)),
        out_specs=(in_vmem, in_vmem),
        scratch_shapes=[
            pltpu.VMEM((width + 2 * (wide + REACH), PITCH, size_z), f32),
            pltpu.VMEM((width + 2 * wide, size_y, size_z), f32),
            pltpu.VMEM((width + 2 * wide, PITCH, size_z), f32),
            pltpu.VMEM((width + 2 * REACH, size_y, size_z), f32),
            pltpu.VMEM((width + 2 * wide, PITCH, size_z), f32),
            pltpu.VMEM((width + 2 * REACH, size_y, size_z), f32),
            pltpu.VMEM((width + 2 * REACH, PITCH, size_z), f32),
            pltpu.VMEM((3 * rows, size_z), f32),
            pltpu.VMEM((6 * rows, size_z), f32),
            pltpu.VMEM((2 * rows, size_z), f32),
        ],
        name="wave_steps",
    )(
        src_cell, src_step, wavelet, prev, cur, far, near, model, rec_cell[None], observed,
        one, two, *fars, *extra,
    )
    cells_coarse = rows * slabs * coarse_z
    if not fast:
        residual = lax.psum(samples, "slab") - observed
        gathered = lax.all_gather(pay, "particle", axis=0)
        models = gathered[:, :, coarse_z:]
        deltas = models[:, None] - models[None]
        dist = lax.psum(jnp.sum(deltas * deltas, axis=(2, 3)), "slab")
        band = jnp.sum(dist) / (count * (count - 1))
        row = lax.dynamic_index_in_dim(dist, lax.axis_index("particle"), 0, keepdims=False)
        weights = jnp.exp(-row / band)
        mixed = jnp.einsum("q,qrz->rz", weights, gathered, precision=HIGHEST)
        own = pay[:, coarse_z:]
        pull = (2.0 * cells_coarse / band) * (own * jnp.sum(weights) - mixed[:, coarse_z:])
        update = (mixed[:, :coarse_z] + pull) / count
        return (update.reshape(model.shape)[None], residual[None])

    blocks = {0: pay}
    for flip in (6, 4, 2):
        blocks[flip] = swap(pay, "particle", [(i, i ^ flip) for i in range(count) if i < i ^ flip])
    for flip in (0, 6, 4, 2):
        pairs = [(i, i ^ 1) for i in range(0, count, 2)]
        blocks[flip + 1] = swap(blocks[flip], "particle", pairs)
    part = samples + swap(samples, "slab", [(0, 1), (2, 3)])
    other = swap(part, "slab", [(0, 2), (1, 3)])
    update, residual = pl.pallas_call(
        lambda *refs: mix_kernel(*refs, cells=cells_coarse),
        out_shape=(
            jax.ShapeDtypeStruct(model.shape, f32),
            jax.ShapeDtypeStruct((2, receivers), f32),
        ),
        in_specs=[in_vmem] * 11,
        out_specs=(in_vmem, in_vmem),
        name="mix_particles",
    )(*[blocks[i] for i in range(count)], part, other, observed)
    return (update[None], residual[None])


def other_side(cur, sent):
    top = cur.shape[0] - REACH
    low_first = (lax.axis_index("slab") % 4) // 2 == 0
    outer = jnp.where(low_first, cur[:REACH], cur[top:])
    return jnp.concatenate([outer, sent[REACH:]], axis=0)


def solution(mesh):
    in_specs = (
        P("particle", "slab", None, None),
        P("particle", "slab", None, None),
        P("particle", "slab", None, None),
        P("particle", "slab", None, None),
        P("particle", "slab", None, None),
        P("particle"),
        P("particle"),
        P(),
        P(),
        P(),
    )
    out_specs = (P("particle", "slab", None, None), P("particle", None, None))
    return jax.shard_map(
        on_device, mesh=mesh, in_specs=in_specs, out_specs=out_specs, check_vma=False
    )
```

time: 128 us -> 42.4 us (0.33)
  blocking collectives: 42.5 us -> 0 us
  local copies, waits for them, and re-layouts: 41.1 us -> 1.99 us
  other arithmetic: 15 us -> 0.01 us
  waiting for transfers between devices: 0.02 us -> 13.1 us
  Pallas kernels: 0 us -> 7.87 us
  starting transfers between devices: 24.5 us -> 17.1 us
  between operations: 3.64 us -> 2.06 us
    reshape x8 -> x0, local copies, waits for them, and re-layouts: 33.9 us -> none  [inject(): return flat.reshape(field.shape)]
    psum x3 -> x0, blocking collectives: 33.2 us -> none  [the longest x1 12.4 us: on_device(): grand = lax.psum(jnp.sum(dist_row), 'particle')]
    ppermute x8 -> x14, waiting for transfers between devices: 0.02 us -> 13.1 us  [swap(): return lax.ppermute(block, axis, both)]
    all_gather x1 -> x0, blocking collectives: 9.31 us -> none  [on_device(): gathered = lax.all_gather(stacked, 'particle', axis=0, tiled=True)]
    pallas_call x0 -> x3, Pallas kernels: none -> 7.87 us  [the longest x1 4.19 us: on_device(): pl.pallas_call(lambda *refs: wave_kernel(*refs, n_far=len(fars), with_mod...]
    ppermute x8 -> x14, starting transfers between devices: 24.5 us -> 17.1 us  [swap(): return lax.ppermute(block, axis, both)]
    scatter-add x4 -> x0, other arithmetic: 7.28 us -> none  [inject(): flat = field.reshape(-1).at[placed].add(jnp.where(valid, values, 0.0))]
    gather x2 -> x0, local copies, waits for them, and re-layouts: 3.44 us -> none  [sample(): return jnp.where(valid, field.reshape(-1)[placed], 0.0)]
  transfers between devices with their start and end apart: 8 -> 14, of which waited for: 0 -> 7; matrix products, arithmetic and copies ran while one was open for 28% -> 0% of each run, Pallas kernels for 0% -> 0%
where the time goes in v1:
time: 42.4 us; the launch traced here: 42.1 us
  starting transfers between devices  17.1 us (40%)
  waiting for transfers between devices  13.1 us (31%)
  Pallas kernels  7.87 us (19%)
  between operations  2.06 us (5%)
  local copies, waits for them, and re-layouts  1.99 us (5%)
    ppermute x14, starting transfers between devices, swap(): return lax.ppermute(block, axis, both)  17.1 us
    ppermute x14, waiting for transfers between devices, swap(): return lax.ppermute(block, axis, both)  13.1 us
    pallas_call x1, Pallas kernels, on_device(): pl.pallas_call(lambda *refs: wave_kernel(*refs, n_far=len(fars), with_mod...  4.19 us
    unnamed x30, local copies, waits for them, and re-layouts  1.99 us
    pallas_call x1, Pallas kernels, on_device(): pl.pallas_call(lambda *refs: mix_kernel(*refs, cells=cells_coarse), out_s...  1.86 us
    pallas_call x1, Pallas kernels, on_device(): pl.pallas_call(pack_kernel, out_shape=(jax.ShapeDtypeStruct((near_layers,...  1.82 us
  transfers between devices with their start and end apart: 14, of which 7 were waited for; matrix products, arithmetic and copies ran while one was open for 0% of the time, Pallas kernels for 0%

profile of v1, /device:TPU:0, one launch (start us, length us, event | category | flops | bytes accessed | tf_op | source)
XLA Modules:
  0.0 42.1 jit_solution(17291299819535303817)
XLA Ops:
  0.6 1.8 %pack_halos.1 = (f32[30,16,128]{2,1,0:T(8,128)}, f32[30,16,128]{2,1,0:T(8,128)}, f32[6,16,128]{2,1,0:T(8,128)}) custom-call(f32[8,16,128]{2,1,0:T(8,128)} %bitcast.8, f32[8,16,128]{2,1,0:T(8,128)} %bitcast.10, f32[8,16,128]{2,1,0:T(8,128)} %bitcast.14, f32[8,16,128]{2,1,0:T(8,128)} %bitcast.12, f32[4,8,64]{2,1,0:T(8,128)} %bitcast.16), custom_call_target="tpu_custom_call" | custom-call | tf_op jit(solution)/shard_map/pack_halos/pallas_call | solution.py:285
  2.5 3.1 %collective-permute-start = (f32[30,16,128]{2,1,0:T(8,128)}, f32[30,16,128]{2,1,0:T(8,128)S(1)}, u32[]{:S(2)}, u32[]{:S(2)}) collective-permute-start(f32[30,16,128]{2,1,0:T(8,128)} %get-tuple-element.9), channel_id=1, source_target_pairs={{0,1},{2,3},{1,0},{3,2},{4,5},{6,7},{5,4},{7,6},{8,9},{10,11},{9,8... | collective-permute-start | bytes 737288 | tf_op jit(solution)/shard_map/ppermute | solution.py:17
  5.5 0.7 %collective-permute-start.1 = (f32[30,16,128]{2,1,0:T(8,128)}, f32[30,16,128]{2,1,0:T(8,128)S(1)}, u32[]{:S(2)}, u32[]{:S(2)}) collective-permute-start(f32[30,16,128]{2,1,0:T(8,128)} %get-tuple-element.10), channel_id=1, source_target_pairs={{1,2},{2,1},{5,6},{6,5},{9,10},{10,9},{13,14},{14,13},{17,18},{18,... | collective-permute-start | bytes 737288 | tf_op jit(solution)/shard_map/ppermute | solution.py:17
  6.2 3.9 %collective-permute-start.2 = (f32[6,16,128]{2,1,0:T(8,128)}, f32[6,16,128]{2,1,0:T(8,128)S(1)}, u32[]{:S(2)}, u32[]{:S(2)}) collective-permute-start(f32[6,16,128]{2,1,0:T(8,128)} %get-tuple-element.11), channel_id=1, source_target_pairs={{0,2},{1,3},{2,0},{3,1},{4,6},{5,7},{6,4},{7,5},{8,10},{9,11},{10,... | collective-permute-start | bytes 147464 | tf_op jit(solution)/shard_map/ppermute | solution.py:17
  10.1 0.6 %collective-permute-start.3 = (f32[4,8,64]{2,1,0:T(8,128)S(1)}, f32[4,8,64]{2,1,0:T(8,128)S(1)}, u32[]{:S(2)}, u32[]{:S(2)}) collective-permute-start(f32[4,8,64]{2,1,0:T(8,128)S(1)} %bitcast.18), channel_id=1, source_target_pairs={{0,1},{2,3},{1,0},{3,2},{4,5},{6,7},{5,4},{7,6},{8,9},{10,11},{9,8... | collective-permute-start | bytes 24584 | tf_op jit(solution)/shard_map/ppermute | solution.py:17
  10.7 3.1 %collective-permute-done.3 = f32[4,8,64]{2,1,0:T(8,128)S(1)} collective-permute-done((f32[4,8,64]{2,1,0:T(8,128)S(1)}, f32[4,8,64]{2,1,0:T(8,128)S(1)}, u32[]{:S(2)}, u32[]{:S(2)}) %collective-permute-start.3) | collective-permute-done | bytes 8224 | tf_op jit(solution)/shard_map/ppermute | solution.py:17
  13.8 2.2 %collective-permute-start.4 = (f32[4,8,64]{2,1,0:T(8,128)S(1)}, f32[4,8,64]{2,1,0:T(8,128)S(1)}, u32[]{:S(2)}, u32[]{:S(2)}) collective-permute-start(f32[4,8,64]{2,1,0:T(8,128)S(1)} %collective-permute-done.3), channel_id=1, source_target_pairs={{0,2},{1,3},{2,0},{3,1},{4,6},{5,7},{6,4},{7,5},{8,10},{9,11},{10,... | collective-permute-start | bytes 24584 | tf_op jit(solution)/shard_map/ppermute | solution.py:17
  17.3 1.2 %collective-permute-done.4.refs_13_ = f32[4,8,64]{2,1,0:T(8,128)S(1)} collective-permute-done((f32[4,8,64]{2,1,0:T(8,128)S(1)}, f32[4,8,64]{2,1,0:T(8,128)S(1)}, u32[]{:S(2)}, u32[]{:S(2)}) %collective-permute-start.4) | collective-permute-done | bytes 8224 | tf_op jit(solution)/shard_map/ppermute | solution.py:17
  18.6 0.6 %copy-done.11 = f32[4,8,64]{2,1,0:T(8,128)} copy-done((f32[4,8,64]{2,1,0:T(8,128)}, f32[4,8,64]{2,1,0:T(8,128)S(1)}, u32[]{:S(2)}) %copy-start.11) | copy-done | bytes 8216
  19.1 0.1 copy-done
  19.3 4.2 %wave_steps.1 = (f32[96,128]{1,0:T(8,128)}, f32[2,256]{1,0:T(2,128)}) custom-call(s32[1]{0:T(128)S(6)} %copy.12.refs_0_, s32[1]{0:T(128)S(6)} %copy.13.refs_1_, f32[64]{0:T(128)} %refs_2_.1, f32[8,16,128]{2,1,0:T(8,128)} %bitcast.9, f32[8,16,128]{2,1,0:T(8,128)} %bitcast.11, f32[8,16,128]{2,1,0:T(8,128)} %bitcast.13, f32[8,16,128]{2,1,0:T(8,128)} %bitcast.15, ...), custom_call_target="tpu_custom_call" | custom-call | tf_op jit(solution)/shard_map/wave_steps/pallas_call | solution.py:309
  23.5 2.4 %collective-permute-start.10 = (f32[96,128]{1,0:T(8,128)}, f32[96,128]{1,0:T(8,128)S(1)}, u32[]{:S(2)}, u32[]{:S(2)}) collective-permute-start(f32[96,128]{1,0:T(8,128)} %get-tuple-element.12.refs_0_), channel_id=1, source_target_pairs={{0,24},{4,28},{8,16},{12,20},{24,0},{28,4},{16,8},{20,12},{1,25},{... | collective-permute-start | bytes 147464 | tf_op jit(solution)/shard_map/ppermute | solution.py:17
  26.0 0.5 %collective-permute-start.6 = (f32[96,128]{1,0:T(8,128)}, f32[96,128]{1,0:T(8,128)S(1)}, u32[]{:S(2)}, u32[]{:S(2)}) collective-permute-start(f32[96,128]{1,0:T(8,128)} %get-tuple-element.12.refs_0_), channel_id=1, source_target_pairs={{0,8},{4,12},{16,24},{20,28},{8,0},{12,4},{24,16},{28,20},{1,9},{5... | collective-permute-start | bytes 147464 | tf_op jit(solution)/shard_map/ppermute | solution.py:17
  26.5 0.5 %collective-permute-start.8 = (f32[96,128]{1,0:T(8,128)}, f32[96,128]{1,0:T(8,128)S(1)}, u32[]{:S(2)}, u32[]{:S(2)}) collective-permute-start(f32[96,128]{1,0:T(8,128)} %get-tuple-element.12.refs_0_), channel_id=1, source_target_pairs={{0,16},{4,20},{8,24},{12,28},{16,0},{20,4},{24,8},{28,12},{1,17},{... | collective-permute-start | bytes 147464 | tf_op jit(solution)/shard_map/ppermute | solution.py:17
  27.0 1.7 %collective-permute-done.10.refs_6_ = f32[96,128]{1,0:T(8,128)S(1)} collective-permute-done((f32[96,128]{1,0:T(8,128)}, f32[96,128]{1,0:T(8,128)S(1)}, u32[]{:S(2)}, u32[]{:S(2)}) %collective-permute-start.10) | collective-permute-done | bytes 49184 | tf_op jit(solution)/shard_map/ppermute | solution.py:17
  28.7 1.5 %collective-permute-done.6.refs_2_ = f32[96,128]{1,0:T(8,128)S(1)} collective-permute-done((f32[96,128]{1,0:T(8,128)}, f32[96,128]{1,0:T(8,128)S(1)}, u32[]{:S(2)}, u32[]{:S(2)}) %collective-permute-start.6) | collective-permute-done | bytes 49184 | tf_op jit(solution)/shard_map/ppermute | solution.py:17
  30.3 0.5 %collective-permute-done.8.refs_4_ = f32[96,128]{1,0:T(8,128)S(1)} collective-permute-done((f32[96,128]{1,0:T(8,128)}, f32[96,128]{1,0:T(8,128)S(1)}, u32[]{:S(2)}, u32[]{:S(2)}) %collective-permute-start.8) | collective-permute-done | bytes 49184 | tf_op jit(solution)/shard_map/ppermute | solution.py:17
  30.8 1.0 %collective-permute-start.12 = (f32[2,256]{1,0:T(2,128)S(1)}, f32[2,256]{1,0:T(2,128)S(1)}, u32[]{:S(2)}, u32[]{:S(2)}) collective-permute-start(f32[2,256]{1,0:T(2,128)S(1)} %copy-done.14), channel_id=1, source_target_pairs={{0,1},{2,3},{1,0},{3,2},{4,5},{6,7},{5,4},{7,6},{8,9},{10,11},{9,8... | collective-permute-start | bytes 6152 | tf_op jit(solution)/shard_map/ppermute | solution.py:17
  31.8 2.6 %collective-permute-done.12 = f32[2,256]{1,0:T(2,128)S(1)} collective-permute-done((f32[2,256]{1,0:T(2,128)S(1)}, f32[2,256]{1,0:T(2,128)S(1)}, u32[]{:S(2)}, u32[]{:S(2)}) %collective-permute-start.12) | collective-permute-done | bytes 2080 | tf_op jit(solution)/shard_map/ppermute | solution.py:17
  34.5 2.1 %collective-permute-start.13 = (f32[2,256]{1,0:T(2,128)S(1)}, f32[2,256]{1,0:T(2,128)S(1)}, u32[]{:S(2)}, u32[]{:S(2)}) collective-permute-start(f32[2,256]{1,0:T(2,128)S(1)} %add.3.refs_8_), channel_id=1, source_target_pairs={{0,2},{1,3},{2,0},{3,1},{4,6},{5,7},{6,4},{7,5},{8,10},{9,11},{10,... | collective-permute-start | bytes 6152 | tf_op jit(solution)/shard_map/ppermute | solution.py:17
  36.6 2.3 %collective-permute-done.13.refs_9_ = f32[2,256]{1,0:T(2,128)S(1)} collective-permute-done((f32[2,256]{1,0:T(2,128)S(1)}, f32[2,256]{1,0:T(2,128)S(1)}, u32[]{:S(2)}, u32[]{:S(2)}) %collective-permute-start.13) | collective-permute-done | bytes 2080 | tf_op jit(solution)/shard_map/ppermute | solution.py:17
  39.0 0.5 %copy-done.13 = f32[2,256]{1,0:T(2,128)} copy-done((f32[2,256]{1,0:T(2,128)}, f32[2,256]{1,0:T(2,128)S(1)}, u32[]{:S(2)}) %copy-start.13) | copy-done | bytes 2072
  39.6 0.6 %copy-done.9 = f32[96,128]{1,0:T(8,128)} copy-done((f32[96,128]{1,0:T(8,128)}, f32[96,128]{1,0:T(8,128)S(1)}, u32[]{:S(2)}) %copy-start.9) | copy-done | bytes 49176
  40.2 1.9 %mix_particles.1 = (f32[4,8,64]{2,1,0:T(8,128)}, f32[2,256]{1,0:T(2,128)}) custom-call(f32[96,128]{1,0:T(8,128)} %get-tuple-element.12.refs_0_, f32[96,128]{1,0:T(8,128)} %copy-done.6, f32[96,128]{1,0:T(8,128)} %copy-done.4, f32[96,128]{1,0:T(8,128)} %copy-done.8, f32[96,128]{1,0:T(8,128)} %copy-done.5, f32[96,128]{1,0:T(8,128)} %copy-done.9, ...), custom_call_target="tpu_custom_call" | custom-call | tf_op jit(solution)/shard_map/mix_particles/pallas_call | solution.py:358
  (38 shorter events, 0.3 us)
Async XLA Ops:
  0.6 9.5 %copy-start.2 = (f32[1,4,8,64]{3,2,1,0:T(8,128)S(1)}, f32[1,4,8,64]{3,2,1,0:T(8,128)}, u32[]{:S(2)}) copy-start(f32[1,4,8,64]{3,2,1,0:T(8,128)} %param.10) | copy-start | bytes 24580
  2.5 16.1 %collective-permute-start = (f32[30,16,128]{2,1,0:T(8,128)}, f32[30,16,128]{2,1,0:T(8,128)S(1)}, u32[]{:S(2)}, u32[]{:S(2)}) collective-permute-start(f32[30,16,128]{2,1,0:T(8,128)} %get-tuple-element.9), channel_id=1, source_target_pairs={{0,1},{2,3},{1,0},{3,2},{4,5},{6,7},{5,4},{7,6},{8,9},{10,11},{9,8... | collective-permute-start | bytes 737288 | tf_op jit(solution)/shard_map/ppermute | solution.py:17
  5.5 13.0 %collective-permute-start.1 = (f32[30,16,128]{2,1,0:T(8,128)}, f32[30,16,128]{2,1,0:T(8,128)S(1)}, u32[]{:S(2)}, u32[]{:S(2)}) collective-permute-start(f32[30,16,128]{2,1,0:T(8,128)} %get-tuple-element.10), channel_id=1, source_target_pairs={{1,2},{2,1},{5,6},{6,5},{9,10},{10,9},{13,14},{14,13},{17,18},{18,... | collective-permute-start | bytes 737288 | tf_op jit(solution)/shard_map/ppermute | solution.py:17
  6.2 12.3 %collective-permute-start.2 = (f32[6,16,128]{2,1,0:T(8,128)}, f32[6,16,128]{2,1,0:T(8,128)S(1)}, u32[]{:S(2)}, u32[]{:S(2)}) collective-permute-start(f32[6,16,128]{2,1,0:T(8,128)} %get-tuple-element.11), channel_id=1, source_target_pairs={{0,2},{1,3},{2,0},{3,1},{4,6},{5,7},{6,4},{7,5},{8,10},{9,11},{10,... | collective-permute-start | bytes 147464 | tf_op jit(solution)/shard_map/ppermute | solution.py:17
  10.1 3.7 %collective-permute-start.3 = (f32[4,8,64]{2,1,0:T(8,128)S(1)}, f32[4,8,64]{2,1,0:T(8,128)S(1)}, u32[]{:S(2)}, u32[]{:S(2)}) collective-permute-start(f32[4,8,64]{2,1,0:T(8,128)S(1)} %bitcast.18), channel_id=1, source_target_pairs={{0,1},{2,3},{1,0},{3,2},{4,5},{6,7},{5,4},{7,6},{8,9},{10,11},{9,8... | collective-permute-start | bytes 24584 | tf_op jit(solution)/shard_map/ppermute | solution.py:17
  13.8 4.7 %collective-permute-start.4 = (f32[4,8,64]{2,1,0:T(8,128)S(1)}, f32[4,8,64]{2,1,0:T(8,128)S(1)}, u32[]{:S(2)}, u32[]{:S(2)}) collective-permute-start(f32[4,8,64]{2,1,0:T(8,128)S(1)} %collective-permute-done.3), channel_id=1, source_target_pairs={{0,2},{1,3},{2,0},{3,1},{4,6},{5,7},{6,4},{7,5},{8,10},{9,11},{10,... | collective-permute-start | bytes 24584 | tf_op jit(solution)/shard_map/ppermute | solution.py:17
  18.5 0.7 %copy-start = (f32[30,16,128]{2,1,0:T(8,128)}, f32[30,16,128]{2,1,0:T(8,128)S(1)}, u32[]{:S(2)}) copy-start(f32[30,16,128]{2,1,0:T(8,128)S(1)} %collective-permute-done.refs_10_) | copy-start | bytes 737284
  18.5 0.8 %copy-start.1 = (f32[30,16,128]{2,1,0:T(8,128)}, f32[30,16,128]{2,1,0:T(8,128)S(1)}, u32[]{:S(2)}) copy-start(f32[30,16,128]{2,1,0:T(8,128)S(1)} %collective-permute-done.1.refs_11_) | copy-start | bytes 737284
  23.5 7.3 %copy-start.14 = (f32[2,256]{1,0:T(2,128)S(1)}, f32[2,256]{1,0:T(2,128)}, u32[]{:S(2)}) copy-start(f32[2,256]{1,0:T(2,128)} %get-tuple-element.13) | copy-start | bytes 6148
  23.5 5.2 %collective-permute-start.10 = (f32[96,128]{1,0:T(8,128)}, f32[96,128]{1,0:T(8,128)S(1)}, u32[]{:S(2)}, u32[]{:S(2)}) collective-permute-start(f32[96,128]{1,0:T(8,128)} %get-tuple-element.12.refs_0_), channel_id=1, source_target_pairs={{0,24},{4,28},{8,16},{12,20},{24,0},{28,4},{16,8},{20,12},{1,25},{... | collective-permute-start | bytes 147464 | tf_op jit(solution)/shard_map/ppermute | solution.py:17
  26.0 4.3 %collective-permute-start.6 = (f32[96,128]{1,0:T(8,128)}, f32[96,128]{1,0:T(8,128)S(1)}, u32[]{:S(2)}, u32[]{:S(2)}) collective-permute-start(f32[96,128]{1,0:T(8,128)} %get-tuple-element.12.refs_0_), channel_id=1, source_target_pairs={{0,8},{4,12},{16,24},{20,28},{8,0},{12,4},{24,16},{28,20},{1,9},{5... | collective-permute-start | bytes 147464 | tf_op jit(solution)/shard_map/ppermute | solution.py:17
  26.5 4.3 %collective-permute-start.8 = (f32[96,128]{1,0:T(8,128)}, f32[96,128]{1,0:T(8,128)S(1)}, u32[]{:S(2)}, u32[]{:S(2)}) collective-permute-start(f32[96,128]{1,0:T(8,128)} %get-tuple-element.12.refs_0_), channel_id=1, source_target_pairs={{0,16},{4,20},{8,24},{12,28},{16,0},{20,4},{24,8},{28,12},{1,17},{... | collective-permute-start | bytes 147464 | tf_op jit(solution)/shard_map/ppermute | solution.py:17
  27.0 12.0 %collective-permute-start.5 = (f32[96,128]{1,0:T(8,128)}, f32[96,128]{1,0:T(8,128)S(1)}, u32[]{:S(2)}, u32[]{:S(2)}) collective-permute-start(f32[96,128]{1,0:T(8,128)} %get-tuple-element.12.refs_0_), channel_id=1, source_target_pairs={{0,4},{8,12},{16,20},{24,28},{4,0},{12,8},{20,16},{28,24},{1,5},{9... | collective-permute-start | bytes 147464 | tf_op jit(solution)/shard_map/ppermute | solution.py:17
  28.7 10.3 %copy-start.3 = (f32[96,128]{1,0:T(8,128)}, f32[96,128]{1,0:T(8,128)S(1)}, u32[]{:S(2)}) copy-start(f32[96,128]{1,0:T(8,128)S(1)} %collective-permute-done.10.refs_6_) | copy-start | bytes 147460
  28.7 10.2 %collective-permute-start.11 = (f32[96,128]{1,0:T(8,128)S(1)}, f32[96,128]{1,0:T(8,128)S(1)}, u32[]{:S(2)}, u32[]{:S(2)}) collective-permute-start(f32[96,128]{1,0:T(8,128)S(1)} %collective-permute-done.10.refs_6_), channel_id=1, source_target_pairs={{0,4},{8,12},{16,20},{24,28},{4,0},{12,8},{20,16},{28,24},{1,5},{9... | collective-permute-start | bytes 147464 | tf_op jit(solution)/shard_map/ppermute | solution.py:17
  30.3 8.8 %copy-start.4 = (f32[96,128]{1,0:T(8,128)}, f32[96,128]{1,0:T(8,128)S(1)}, u32[]{:S(2)}) copy-start(f32[96,128]{1,0:T(8,128)S(1)} %collective-permute-done.6.refs_2_) | copy-start | bytes 147460
  30.3 8.7 %collective-permute-start.7 = (f32[96,128]{1,0:T(8,128)S(1)}, f32[96,128]{1,0:T(8,128)S(1)}, u32[]{:S(2)}, u32[]{:S(2)}) collective-permute-start(f32[96,128]{1,0:T(8,128)S(1)} %collective-permute-done.6.refs_2_), channel_id=1, source_target_pairs={{0,4},{8,12},{16,20},{24,28},{4,0},{12,8},{20,16},{28,24},{1,5},{9... | collective-permute-start | bytes 147464 | tf_op jit(solution)/shard_map/ppermute | solution.py:17
  30.8 8.2 %copy-start.5 = (f32[96,128]{1,0:T(8,128)}, f32[96,128]{1,0:T(8,128)S(1)}, u32[]{:S(2)}) copy-start(f32[96,128]{1,0:T(8,128)S(1)} %collective-permute-done.8.refs_4_) | copy-start | bytes 147460
  30.8 8.2 %collective-permute-start.9 = (f32[96,128]{1,0:T(8,128)S(1)}, f32[96,128]{1,0:T(8,128)S(1)}, u32[]{:S(2)}, u32[]{:S(2)}) collective-permute-start(f32[96,128]{1,0:T(8,128)S(1)} %collective-permute-done.8.refs_4_), channel_id=1, source_target_pairs={{0,4},{8,12},{16,20},{24,28},{4,0},{12,8},{20,16},{28,24},{1,5},{9... | collective-permute-start | bytes 147464 | tf_op jit(solution)/shard_map/ppermute | solution.py:17
  30.8 3.7 %collective-permute-start.12 = (f32[2,256]{1,0:T(2,128)S(1)}, f32[2,256]{1,0:T(2,128)S(1)}, u32[]{:S(2)}, u32[]{:S(2)}) collective-permute-start(f32[2,256]{1,0:T(2,128)S(1)} %copy-done.14), channel_id=1, source_target_pairs={{0,1},{2,3},{1,0},{3,2},{4,5},{6,7},{5,4},{7,6},{8,9},{10,11},{9,8... | collective-permute-start | bytes 6152 | tf_op jit(solution)/shard_map/ppermute | solution.py:17
  34.5 4.6 %copy-start.12 = (f32[2,256]{1,0:T(2,128)}, f32[2,256]{1,0:T(2,128)S(1)}, u32[]{:S(2)}) copy-start(f32[2,256]{1,0:T(2,128)S(1)} %add.3.refs_8_) | copy-start | bytes 6148
  34.5 4.5 %collective-permute-start.13 = (f32[2,256]{1,0:T(2,128)S(1)}, f32[2,256]{1,0:T(2,128)S(1)}, u32[]{:S(2)}, u32[]{:S(2)}) collective-permute-start(f32[2,256]{1,0:T(2,128)S(1)} %add.3.refs_8_), channel_id=1, source_target_pairs={{0,2},{1,3},{2,0},{3,1},{4,6},{5,7},{6,4},{7,5},{8,10},{9,11},{10,... | collective-permute-start | bytes 6152 | tf_op jit(solution)/shard_map/ppermute | solution.py:17
  39.0 0.6 %copy-start.7 = (f32[96,128]{1,0:T(8,128)}, f32[96,128]{1,0:T(8,128)S(1)}, u32[]{:S(2)}) copy-start(f32[96,128]{1,0:T(8,128)S(1)} %collective-permute-done.11.refs_7_) | copy-start | bytes 147460
  39.0 0.6 %copy-start.8 = (f32[96,128]{1,0:T(8,128)}, f32[96,128]{1,0:T(8,128)S(1)}, u32[]{:S(2)}) copy-start(f32[96,128]{1,0:T(8,128)S(1)} %collective-permute-done.7.refs_3_) | copy-start | bytes 147460
  (5 other events, 3.1 us)

commit v2 on v1

--- a/solution.py
+++ b/solution.py
@@ -5,11 +5,20 @@
 from jax.experimental.pallas import tpu as pltpu
 from jax.sharding import PartitionSpec as P
 
+
 STENCIL_WEIGHTS = (-205.0 / 72.0, 8.0 / 5.0, -1.0 / 5.0, 8.0 / 315.0, -1.0 / 560.0)
 COURANT_FACTOR = 0.1
 REACH = 4
 PITCH = 32
 HIGHEST = lax.Precision.HIGHEST
+
+
+def resident(block):
+    return pltpu.with_memory_space_constraint(block, pltpu.MemorySpace.VMEM)
+
+
+def is_fast(slabs, count):
+    return slabs == 4 and count == 8
 
 
 def swap(block, axis, pairs):
@@ -255,7 +264,7 @@
     update[...] = ((mixed[:, 0:half] + pull) * (1.0 / count)).reshape(update.shape)
 
 
-def on_device(
+def device_step(
     vel_coarse,
     fwd_prev,
     fwd_cur,
@@ -270,7 +279,7 @@
     f32 = jnp.float32
     slabs = lax.axis_size("slab")
     count = lax.axis_size("particle")
-    fast = slabs == 4 and count == 8
+    fast = is_fast(slabs, count)
     model = vel_coarse[0]
     prev, cur, far, near = fwd_prev[0], fwd_cur[0], adj_far[0], adj_near[0]
     width, size_y, size_z = prev.shape
@@ -282,17 +291,18 @@
     in_vmem = pl.BlockSpec(memory_space=pltpu.VMEM)
     if fast:
         beside = swap(model, "slab", [(0, 1), (2, 3)])
-    to_one, to_two, to_far = pl.pallas_call(
+    pack = pl.pallas_call(
         pack_kernel,
         out_shape=(
-            jax.ShapeDtypeStruct((near_layers, size_y, size_z), f32),
-            jax.ShapeDtypeStruct((near_layers, size_y, size_z), f32),
-            jax.ShapeDtypeStruct((far_layers, size_y, size_z), f32),
+            pltpu.VMEM((near_layers, size_y, size_z), f32),
+            pltpu.VMEM((near_layers, size_y, size_z), f32),
+            pltpu.VMEM((far_layers, size_y, size_z), f32),
         ),
         in_specs=[in_vmem] * 5,
         out_specs=(in_vmem,) * 3,
         name="pack_halos",
-    )(prev, cur, near, far, model)
+    )
+    to_one, to_two, to_far = pack(prev, cur, near, far, model)
     one = swap(to_one, "slab", [(i, i + 1) for i in range(0, slabs - 1, 2)])
     two = swap(to_two, "slab", [(i, i + 1) for i in range(1, slabs - 1, 2)])
     fars = [swap(to_far, "slab", [(i, i + 2) for i in range(slabs - 2) if i % 4 < 2])]
@@ -309,8 +319,8 @@
     pay, samples = pl.pallas_call(
         lambda *refs: wave_kernel(*refs, n_far=len(fars), with_models=fast),
         out_shape=(
-            jax.ShapeDtypeStruct((pay_rows, size_z), f32),
-            jax.ShapeDtypeStruct((2, receivers), f32),
+            pltpu.VMEM((pay_rows, size_z), f32),
+            pltpu.VMEM((2, receivers), f32),
         ),
         in_specs=[in_smem] * 3 + [in_vmem] * (9 + len(fars) + len(extra)),
         out_specs=(in_vmem, in_vmem),
@@ -329,7 +339,7 @@
         name="wave_steps",
     )(
         src_cell, src_step, wavelet, prev, cur, far, near, model, rec_cell[None], observed,
-        one, two, *fars, *extra,
+        *[resident(block) for block in (one, two, *fars, *extra)],
     )
     cells_coarse = rows * slabs * coarse_z
     if not fast:
@@ -364,7 +374,7 @@
         in_specs=[in_vmem] * 11,
         out_specs=(in_vmem, in_vmem),
         name="mix_particles",
-    )(*[blocks[i] for i in range(count)], part, other, observed)
+    )(*[resident(blocks[i]) for i in range(count)], resident(part), resident(other), observed)
     return (update[None], residual[None])
 
 
@@ -390,5 +400,5 @@
     )
     out_specs = (P("particle", "slab", None, None), P("particle", None, None))
     return jax.shard_map(
-        on_device, mesh=mesh, in_specs=in_specs, out_specs=out_specs, check_vma=False
+        device_step, mesh=mesh, in_specs=in_specs, out_specs=out_specs, check_vma=False
     )

time: 42.4 us -> 38.1 us (0.90)
  Pallas kernels: 7.87 us -> 5.88 us
  local copies, waits for them, and re-layouts: 1.99 us -> 0.01 us
  starting transfers between devices: 17.1 us -> 16.6 us
    pallas_call x3, Pallas kernels: 7.87 us -> 5.88 us  [the longest x1 3.28 us: device_step(): pl.pallas_call(lambda *refs: wave_kernel(*refs, n_far=len(fars), with_mod...]
    unnamed x30 -> x2, local copies, waits for them, and re-layouts: 1.99 us -> 0.01 us
    ppermute x14, starting transfers between devices: 17.1 us -> 16.6 us  [swap(): return lax.ppermute(block, axis, both)]
where the time goes in v2:
time: 38.1 us; the launch traced here: 37.8 us
  starting transfers between devices  16.6 us (44%)
  waiting for transfers between devices  13.4 us (35%)
  Pallas kernels  5.88 us (15%)
  between operations  1.98 us (5%)
    ppermute x14, starting transfers between devices, swap(): return lax.ppermute(block, axis, both)  16.6 us
    ppermute x14, waiting for transfers between devices, swap(): return lax.ppermute(block, axis, both)  13.4 us
    pallas_call x1, Pallas kernels, device_step(): pl.pallas_call(lambda *refs: wave_kernel(*refs, n_far=len(fars), with_mod...  3.28 us
    pallas_call x1, Pallas kernels, device_step(): pl.pallas_call(lambda *refs: mix_kernel(*refs, cells=cells_coarse), out_s...  1.58 us
    pallas_call x1, Pallas kernels, device_step(): to_one, to_two, to_far = pack(prev, cur, near, far, model)  1.03 us
  transfers between devices with their start and end apart: 14, of which 7 were waited for; matrix products, arithmetic and copies ran while one was open for 0% of the time, Pallas kernels for 0%

profile of v2, /device:TPU:0, one launch (start us, length us, event | category | flops | bytes accessed | tf_op | source)
XLA Modules:
  0.0 37.8 jit_solution(1693480817342256971)
XLA Ops:
  0.6 0.0 copy-start
  0.6 1.0 %pack_halos.1 = (f32[30,16,128]{2,1,0:T(8,128)S(1)}, f32[30,16,128]{2,1,0:T(8,128)S(1)}, f32[6,16,128]{2,1,0:T(8,128)S(1)}) custom-call(f32[8,16,128]{2,1,0:T(8,128)} %bitcast.8, f32[8,16,128]{2,1,0:T(8,128)} %bitcast.10, f32[8,16,128]{2,1,0:T(8,128)} %bitcast.14, f32[8,16,128]{2,1,0:T(8,128)} %bitcast.12, f32[4,8,64]{2,1,0:T(8,128)} %bitcast.16), custom_call_target="tpu_custom_call" | custom-call | tf_op jit(solution)/shard_map/pack_halos/pallas_call | solution.py:305
  1.7 3.1 %collective-permute-start = (f32[30,16,128]{2,1,0:T(8,128)S(1)}, f32[30,16,128]{2,1,0:T(8,128)S(1)}, u32[]{:S(2)}, u32[]{:S(2)}) collective-permute-start(f32[30,16,128]{2,1,0:T(8,128)S(1)} %get-tuple-element.9), channel_id=1, source_target_pairs={{0,1},{2,3},{1,0},{3,2},{4,5},{6,7},{5,4},{7,6},{8,9},{10,11},{9,8... | collective-permute-start | bytes 737288 | tf_op jit(solution)/shard_map/ppermute | solution.py:26
  4.7 0.7 %collective-permute-start.1 = (f32[30,16,128]{2,1,0:T(8,128)S(1)}, f32[30,16,128]{2,1,0:T(8,128)S(1)}, u32[]{:S(2)}, u32[]{:S(2)}) collective-permute-start(f32[30,16,128]{2,1,0:T(8,128)S(1)} %get-tuple-element.10), channel_id=1, source_target_pairs={{1,2},{2,1},{5,6},{6,5},{9,10},{10,9},{13,14},{14,13},{17,18},{18,... | collective-permute-start | bytes 737288 | tf_op jit(solution)/shard_map/ppermute | solution.py:26
  5.4 3.9 %collective-permute-start.2 = (f32[6,16,128]{2,1,0:T(8,128)S(1)}, f32[6,16,128]{2,1,0:T(8,128)S(1)}, u32[]{:S(2)}, u32[]{:S(2)}) collective-permute-start(f32[6,16,128]{2,1,0:T(8,128)S(1)} %get-tuple-element.11), channel_id=1, source_target_pairs={{0,2},{1,3},{2,0},{3,1},{4,6},{5,7},{6,4},{7,5},{8,10},{9,11},{10,... | collective-permute-start | bytes 147464 | tf_op jit(solution)/shard_map/ppermute | solution.py:26
  9.3 0.6 %collective-permute-start.3 = (f32[4,8,64]{2,1,0:T(8,128)S(1)}, f32[4,8,64]{2,1,0:T(8,128)S(1)}, u32[]{:S(2)}, u32[]{:S(2)}) collective-permute-start(f32[4,8,64]{2,1,0:T(8,128)S(1)} %bitcast.18), channel_id=1, source_target_pairs={{0,1},{2,3},{1,0},{3,2},{4,5},{6,7},{5,4},{7,6},{8,9},{10,11},{9,8... | collective-permute-start | bytes 24584 | tf_op jit(solution)/shard_map/ppermute | solution.py:26
  10.0 3.1 %collective-permute-done.3 = f32[4,8,64]{2,1,0:T(8,128)S(1)} collective-permute-done((f32[4,8,64]{2,1,0:T(8,128)S(1)}, f32[4,8,64]{2,1,0:T(8,128)S(1)}, u32[]{:S(2)}, u32[]{:S(2)}) %collective-permute-start.3) | collective-permute-done | bytes 8224 | tf_op jit(solution)/shard_map/ppermute | solution.py:26
  13.1 2.0 %collective-permute-start.4 = (f32[4,8,64]{2,1,0:T(8,128)S(1)}, f32[4,8,64]{2,1,0:T(8,128)S(1)}, u32[]{:S(2)}, u32[]{:S(2)}) collective-permute-start(f32[4,8,64]{2,1,0:T(8,128)S(1)} %collective-permute-done.3), channel_id=1, source_target_pairs={{0,2},{1,3},{2,0},{3,1},{4,6},{5,7},{6,4},{7,5},{8,10},{9,11},{10,... | collective-permute-start | bytes 24584 | tf_op jit(solution)/shard_map/ppermute | solution.py:26
  16.3 1.4 %collective-permute-done.4.refs_13_ = f32[4,8,64]{2,1,0:T(8,128)S(1)} collective-permute-done((f32[4,8,64]{2,1,0:T(8,128)S(1)}, f32[4,8,64]{2,1,0:T(8,128)S(1)}, u32[]{:S(2)}, u32[]{:S(2)}) %collective-permute-start.4) | collective-permute-done | bytes 8224 | tf_op jit(solution)/shard_map/ppermute | solution.py:26
  17.7 3.3 %wave_steps.1 = (f32[96,128]{1,0:T(8,128)S(1)}, f32[2,256]{1,0:T(2,128)S(1)}) custom-call(s32[1]{0:T(128)S(6)} %copy.12.refs_0_, s32[1]{0:T(128)S(6)} %copy.13.refs_1_, f32[64]{0:T(128)} %refs_2_.1, f32[8,16,128]{2,1,0:T(8,128)} %bitcast.9, f32[8,16,128]{2,1,0:T(8,128)} %bitcast.11, f32[8,16,128]{2,1,0:T(8,128)} %bitcast.13, f32[8,16,128]{2,1,0:T(8,128)} %bitcast.15, ...), custom_call_target="tpu_custom_call" | custom-call | tf_op jit(solution)/shard_map/wave_steps/pallas_call | solution.py:319
  21.0 2.5 %collective-permute-start.10 = (f32[96,128]{1,0:T(8,128)S(1)}, f32[96,128]{1,0:T(8,128)S(1)}, u32[]{:S(2)}, u32[]{:S(2)}) collective-permute-start(f32[96,128]{1,0:T(8,128)S(1)} %get-tuple-element.12.refs_0_), channel_id=1, source_target_pairs={{0,24},{4,28},{8,16},{12,20},{24,0},{28,4},{16,8},{20,12},{1,25},{... | collective-permute-start | bytes 147464 | tf_op jit(solution)/shard_map/ppermute | solution.py:26
  23.5 0.5 %collective-permute-start.6 = (f32[96,128]{1,0:T(8,128)S(1)}, f32[96,128]{1,0:T(8,128)S(1)}, u32[]{:S(2)}, u32[]{:S(2)}) collective-permute-start(f32[96,128]{1,0:T(8,128)S(1)} %get-tuple-element.12.refs_0_), channel_id=1, source_target_pairs={{0,8},{4,12},{16,24},{20,28},{8,0},{12,4},{24,16},{28,20},{1,9},{5... | collective-permute-start | bytes 147464 | tf_op jit(solution)/shard_map/ppermute | solution.py:26
  24.0 0.5 %collective-permute-start.8 = (f32[96,128]{1,0:T(8,128)S(1)}, f32[96,128]{1,0:T(8,128)S(1)}, u32[]{:S(2)}, u32[]{:S(2)}) collective-permute-start(f32[96,128]{1,0:T(8,128)S(1)} %get-tuple-element.12.refs_0_), channel_id=1, source_target_pairs={{0,16},{4,20},{8,24},{12,28},{16,0},{20,4},{24,8},{28,12},{1,17},{... | collective-permute-start | bytes 147464 | tf_op jit(solution)/shard_map/ppermute | solution.py:26
  24.5 1.5 %collective-permute-done.10.refs_6_ = f32[96,128]{1,0:T(8,128)S(1)} collective-permute-done((f32[96,128]{1,0:T(8,128)S(1)}, f32[96,128]{1,0:T(8,128)S(1)}, u32[]{:S(2)}, u32[]{:S(2)}) %collective-permute-start.10) | collective-permute-done | bytes 49184 | tf_op jit(solution)/shard_map/ppermute | solution.py:26
  26.0 0.0 collective-permute-start.11
  26.0 1.5 %collective-permute-done.6.refs_2_ = f32[96,128]{1,0:T(8,128)S(1)} collective-permute-done((f32[96,128]{1,0:T(8,128)S(1)}, f32[96,128]{1,0:T(8,128)S(1)}, u32[]{:S(2)}, u32[]{:S(2)}) %collective-permute-start.6) | collective-permute-done | bytes 49184 | tf_op jit(solution)/shard_map/ppermute | solution.py:26
  27.6 0.0 collective-permute-start.7
  27.6 0.5 %collective-permute-done.8.refs_4_ = f32[96,128]{1,0:T(8,128)S(1)} collective-permute-done((f32[96,128]{1,0:T(8,128)S(1)}, f32[96,128]{1,0:T(8,128)S(1)}, u32[]{:S(2)}, u32[]{:S(2)}) %collective-permute-start.8) | collective-permute-done | bytes 49184 | tf_op jit(solution)/shard_map/ppermute | solution.py:26
  28.1 0.0 collective-permute-start.9
  28.1 0.8 %collective-permute-start.12 = (f32[2,256]{1,0:T(2,128)S(1)}, f32[2,256]{1,0:T(2,128)S(1)}, u32[]{:S(2)}, u32[]{:S(2)}) collective-permute-start(f32[2,256]{1,0:T(2,128)S(1)} %get-tuple-element.13), channel_id=1, source_target_pairs={{0,1},{2,3},{1,0},{3,2},{4,5},{6,7},{5,4},{7,6},{8,9},{10,11},{9,8... | collective-permute-start | bytes 6152 | tf_op jit(solution)/shard_map/ppermute | solution.py:26
  28.9 2.8 %collective-permute-done.12 = f32[2,256]{1,0:T(2,128)S(1)} collective-permute-done((f32[2,256]{1,0:T(2,128)S(1)}, f32[2,256]{1,0:T(2,128)S(1)}, u32[]{:S(2)}, u32[]{:S(2)}) %collective-permute-start.12) | collective-permute-done | bytes 2080 | tf_op jit(solution)/shard_map/ppermute | solution.py:26
  31.7 2.0 %collective-permute-start.13 = (f32[2,256]{1,0:T(2,128)S(1)}, f32[2,256]{1,0:T(2,128)S(1)}, u32[]{:S(2)}, u32[]{:S(2)}) collective-permute-start(f32[2,256]{1,0:T(2,128)S(1)} %add.3.refs_8_), channel_id=1, source_target_pairs={{0,2},{1,3},{2,0},{3,1},{4,6},{5,7},{6,4},{7,5},{8,10},{9,11},{10,... | collective-permute-start | bytes 6152 | tf_op jit(solution)/shard_map/ppermute | solution.py:26
  33.7 2.5 %collective-permute-done.13.refs_9_ = f32[2,256]{1,0:T(2,128)S(1)} collective-permute-done((f32[2,256]{1,0:T(2,128)S(1)}, f32[2,256]{1,0:T(2,128)S(1)}, u32[]{:S(2)}, u32[]{:S(2)}) %collective-permute-start.13) | collective-permute-done | bytes 2080 | tf_op jit(solution)/shard_map/ppermute | solution.py:26
  36.2 1.6 %mix_particles.1 = (f32[4,8,64]{2,1,0:T(8,128)}, f32[2,256]{1,0:T(2,128)}) custom-call(f32[96,128]{1,0:T(8,128)S(1)} %get-tuple-element.12.refs_0_, f32[96,128]{1,0:T(8,128)S(1)} %collective-permute-done.5.refs_1_, f32[96,128]{1,0:T(8,128)S(1)} %collective-permute-done.6.refs_2_, f32[96,128]{1,0:T(8,128)S(1)} %collective-permute-done.7.refs_3_, ...), custom_call_target="tpu_custom_call" | custom-call | tf_op jit(solution)/shard_map/mix_particles/pallas_call | solution.py:368
  (10 shorter events, 0.0 us)
Async XLA Ops:
  0.6 8.7 %copy-start = (f32[1,4,8,64]{3,2,1,0:T(8,128)S(1)}, f32[1,4,8,64]{3,2,1,0:T(8,128)}, u32[]{:S(2)}) copy-start(f32[1,4,8,64]{3,2,1,0:T(8,128)} %param.10) | copy-start | bytes 24580
  1.7 16.0 %collective-permute-start = (f32[30,16,128]{2,1,0:T(8,128)S(1)}, f32[30,16,128]{2,1,0:T(8,128)S(1)}, u32[]{:S(2)}, u32[]{:S(2)}) collective-permute-start(f32[30,16,128]{2,1,0:T(8,128)S(1)} %get-tuple-element.9), channel_id=1, source_target_pairs={{0,1},{2,3},{1,0},{3,2},{4,5},{6,7},{5,4},{7,6},{8,9},{10,11},{9,8... | collective-permute-start | bytes 737288 | tf_op jit(solution)/shard_map/ppermute | solution.py:26
  4.7 13.0 %collective-permute-start.1 = (f32[30,16,128]{2,1,0:T(8,128)S(1)}, f32[30,16,128]{2,1,0:T(8,128)S(1)}, u32[]{:S(2)}, u32[]{:S(2)}) collective-permute-start(f32[30,16,128]{2,1,0:T(8,128)S(1)} %get-tuple-element.10), channel_id=1, source_target_pairs={{1,2},{2,1},{5,6},{6,5},{9,10},{10,9},{13,14},{14,13},{17,18},{18,... | collective-permute-start | bytes 737288 | tf_op jit(solution)/shard_map/ppermute | solution.py:26
  5.4 12.3 %collective-permute-start.2 = (f32[6,16,128]{2,1,0:T(8,128)S(1)}, f32[6,16,128]{2,1,0:T(8,128)S(1)}, u32[]{:S(2)}, u32[]{:S(2)}) collective-permute-start(f32[6,16,128]{2,1,0:T(8,128)S(1)} %get-tuple-element.11), channel_id=1, source_target_pairs={{0,2},{1,3},{2,0},{3,1},{4,6},{5,7},{6,4},{7,5},{8,10},{9,11},{10,... | collective-permute-start | bytes 147464 | tf_op jit(solution)/shard_map/ppermute | solution.py:26
  9.3 3.7 %collective-permute-start.3 = (f32[4,8,64]{2,1,0:T(8,128)S(1)}, f32[4,8,64]{2,1,0:T(8,128)S(1)}, u32[]{:S(2)}, u32[]{:S(2)}) collective-permute-start(f32[4,8,64]{2,1,0:T(8,128)S(1)} %bitcast.18), channel_id=1, source_target_pairs={{0,1},{2,3},{1,0},{3,2},{4,5},{6,7},{5,4},{7,6},{8,9},{10,11},{9,8... | collective-permute-start | bytes 24584 | tf_op jit(solution)/shard_map/ppermute | solution.py:26
  13.1 4.6 %collective-permute-start.4 = (f32[4,8,64]{2,1,0:T(8,128)S(1)}, f32[4,8,64]{2,1,0:T(8,128)S(1)}, u32[]{:S(2)}, u32[]{:S(2)}) collective-permute-start(f32[4,8,64]{2,1,0:T(8,128)S(1)} %collective-permute-done.3), channel_id=1, source_target_pairs={{0,2},{1,3},{2,0},{3,1},{4,6},{5,7},{6,4},{7,5},{8,10},{9,11},{10,... | collective-permute-start | bytes 24584 | tf_op jit(solution)/shard_map/ppermute | solution.py:26
  21.0 5.1 %collective-permute-start.10 = (f32[96,128]{1,0:T(8,128)S(1)}, f32[96,128]{1,0:T(8,128)S(1)}, u32[]{:S(2)}, u32[]{:S(2)}) collective-permute-start(f32[96,128]{1,0:T(8,128)S(1)} %get-tuple-element.12.refs_0_), channel_id=1, source_target_pairs={{0,24},{4,28},{8,16},{12,20},{24,0},{28,4},{16,8},{20,12},{1,25},{... | collective-permute-start | bytes 147464 | tf_op jit(solution)/shard_map/ppermute | solution.py:26
  23.5 4.1 %collective-permute-start.6 = (f32[96,128]{1,0:T(8,128)S(1)}, f32[96,128]{1,0:T(8,128)S(1)}, u32[]{:S(2)}, u32[]{:S(2)}) collective-permute-start(f32[96,128]{1,0:T(8,128)S(1)} %get-tuple-element.12.refs_0_), channel_id=1, source_target_pairs={{0,8},{4,12},{16,24},{20,28},{8,0},{12,4},{24,16},{28,20},{1,9},{5... | collective-permute-start | bytes 147464 | tf_op jit(solution)/shard_map/ppermute | solution.py:26
  24.0 4.1 %collective-permute-start.8 = (f32[96,128]{1,0:T(8,128)S(1)}, f32[96,128]{1,0:T(8,128)S(1)}, u32[]{:S(2)}, u32[]{:S(2)}) collective-permute-start(f32[96,128]{1,0:T(8,128)S(1)} %get-tuple-element.12.refs_0_), channel_id=1, source_target_pairs={{0,16},{4,20},{8,24},{12,28},{16,0},{20,4},{24,8},{28,12},{1,17},{... | collective-permute-start | bytes 147464 | tf_op jit(solution)/shard_map/ppermute | solution.py:26
  24.5 11.7 %collective-permute-start.5 = (f32[96,128]{1,0:T(8,128)S(1)}, f32[96,128]{1,0:T(8,128)S(1)}, u32[]{:S(2)}, u32[]{:S(2)}) collective-permute-start(f32[96,128]{1,0:T(8,128)S(1)} %get-tuple-element.12.refs_0_), channel_id=1, source_target_pairs={{0,4},{8,12},{16,20},{24,28},{4,0},{12,8},{20,16},{28,24},{1,5},{9... | collective-permute-start | bytes 147464 | tf_op jit(solution)/shard_map/ppermute | solution.py:26
  26.0 10.2 %collective-permute-start.11 = (f32[96,128]{1,0:T(8,128)S(1)}, f32[96,128]{1,0:T(8,128)S(1)}, u32[]{:S(2)}, u32[]{:S(2)}) collective-permute-start(f32[96,128]{1,0:T(8,128)S(1)} %collective-permute-done.10.refs_6_), channel_id=1, source_target_pairs={{0,4},{8,12},{16,20},{24,28},{4,0},{12,8},{20,16},{28,24},{1,5},{9... | collective-permute-start | bytes 147464 | tf_op jit(solution)/shard_map/ppermute | solution.py:26
  27.6 8.6 %collective-permute-start.7 = (f32[96,128]{1,0:T(8,128)S(1)}, f32[96,128]{1,0:T(8,128)S(1)}, u32[]{:S(2)}, u32[]{:S(2)}) collective-permute-start(f32[96,128]{1,0:T(8,128)S(1)} %collective-permute-done.6.refs_2_), channel_id=1, source_target_pairs={{0,4},{8,12},{16,20},{24,28},{4,0},{12,8},{20,16},{28,24},{1,5},{9... | collective-permute-start | bytes 147464 | tf_op jit(solution)/shard_map/ppermute | solution.py:26
  28.1 8.1 %collective-permute-start.9 = (f32[96,128]{1,0:T(8,128)S(1)}, f32[96,128]{1,0:T(8,128)S(1)}, u32[]{:S(2)}, u32[]{:S(2)}) collective-permute-start(f32[96,128]{1,0:T(8,128)S(1)} %collective-permute-done.8.refs_4_), channel_id=1, source_target_pairs={{0,4},{8,12},{16,20},{24,28},{4,0},{12,8},{20,16},{28,24},{1,5},{9... | collective-permute-start | bytes 147464 | tf_op jit(solution)/shard_map/ppermute | solution.py:26
  28.1 3.6 %collective-permute-start.12 = (f32[2,256]{1,0:T(2,128)S(1)}, f32[2,256]{1,0:T(2,128)S(1)}, u32[]{:S(2)}, u32[]{:S(2)}) collective-permute-start(f32[2,256]{1,0:T(2,128)S(1)} %get-tuple-element.13), channel_id=1, source_target_pairs={{0,1},{2,3},{1,0},{3,2},{4,5},{6,7},{5,4},{7,6},{8,9},{10,11},{9,8... | collective-permute-start | bytes 6152 | tf_op jit(solution)/shard_map/ppermute | solution.py:26
  31.7 4.5 %collective-permute-start.13 = (f32[2,256]{1,0:T(2,128)S(1)}, f32[2,256]{1,0:T(2,128)S(1)}, u32[]{:S(2)}, u32[]{:S(2)}) collective-permute-start(f32[2,256]{1,0:T(2,128)S(1)} %add.3.refs_8_), channel_id=1, source_target_pairs={{0,2},{1,3},{2,0},{3,1},{4,6},{5,7},{6,4},{7,5},{8,10},{9,11},{10,... | collective-permute-start | bytes 6152 | tf_op jit(solution)/shard_map/ppermute | solution.py:26

commit v3 on v2

v3 whole, which is shorter than its diff:
```python
import jax
import jax.numpy as jnp
from jax import lax
from jax.experimental import pallas as pl
from jax.experimental.pallas import tpu as pltpu
from jax.sharding import PartitionSpec as P


STENCIL_WEIGHTS = (-205.0 / 72.0, 8.0 / 5.0, -1.0 / 5.0, 8.0 / 315.0, -1.0 / 560.0)
COURANT_FACTOR = 0.1
REACH = 4
STEP = 4
PITCH = 32
HIGHEST = lax.Precision.HIGHEST


def resident(block):
    return pltpu.with_memory_space_constraint(block, pltpu.MemorySpace.VMEM)


def is_fast(slabs, count):
    return slabs == 4 and count == 8


def swap(block, axis, pairs):
    both = [(a, b) for a, b in pairs] + [(b, a) for a, b in pairs]
    return lax.ppermute(block, axis, both)


def twice(model):
    flat = model.reshape(model.shape[0] * model.shape[1], model.shape[2])
    return jnp.concatenate([flat, flat], axis=1)


def lane_weights(size_z):
    lane = lax.broadcasted_iota(jnp.int32, (1, size_z), 1)
    below = [jnp.where(lane >= k, w, 0.0).astype(jnp.float32) for k, w in enumerate(STENCIL_WEIGHTS)]
    above = [
        jnp.where(lane < size_z - k, w, 0.0).astype(jnp.float32) for k, w in enumerate(STENCIL_WEIGHTS)
    ]
    return below, above


def clear_margins(ref, size_y):
    ref[:, 0:8, :] = jnp.zeros((ref.shape[0], 8, ref.shape[2]), jnp.float32)
    rest = PITCH - 8 - size_y
    ref[:, 8 + size_y : PITCH, :] = jnp.zeros((ref.shape[0], rest, ref.shape[2]), jnp.float32)


def laplace(ref, at, size_y, weights):
    below, above = weights
    data = pl.ds(8, size_y)
    size_z = ref.shape[2]
    centre = ref[at : at + STEP, data, :]
    flat = centre.reshape(STEP * size_y, size_z)
    total = (3.0 * STENCIL_WEIGHTS[0]) * centre
    for k in range(1, 5):
        pairs = (
            ref[at + k : at + k + STEP, data, :]
            + ref[at - k : at - k + STEP, data, :]
            + (ref[at : at + STEP, pl.ds(8 + k, size_y), :] + ref[at : at + STEP, pl.ds(8 - k, size_y), :])
        )
        along = pltpu.roll(flat, k, 1) * below[k] + pltpu.roll(flat, size_z - k, 1) * above[k]
        total = total + STENCIL_WEIGHTS[k] * pairs + along.reshape(STEP, size_y, size_z)
    return centre, total


def fill_courant(c2_ref, packed, size_z):
    grid_r = lax.broadcasted_iota(jnp.int32, (size_z, 2 * size_z), 0)
    grid_c = lax.broadcasted_iota(jnp.int32, (size_z, 2 * size_z), 1)
    spread = jnp.where(grid_r == grid_c // 2, 1.0, 0.0).astype(jnp.float32)
    scaled = COURANT_FACTOR * packed
    fine = jnp.dot(scaled * scaled, spread, precision=HIGHEST, preferred_element_type=jnp.float32)
    count = packed.shape[0]
    part = count if count < 16 else 16
    for start in range(0, count, part):
        for side in range(2):
            rows = fine[start : start + part, side * size_z : (side + 1) * size_z]
            base = 4 * start + 2 * part * side
            c2_ref[pl.ds(base, part, stride=2), :] = rows
            c2_ref[pl.ds(base + 1, part, stride=2), :] = rows


def courant(c2_ref, layer, count, size_y):
    size_z = c2_ref.shape[1]
    block = c2_ref[layer // 2 * size_y : (layer + count) // 2 * size_y, :]
    block = block.reshape(count // 2, 1, size_y, size_z)
    return jnp.broadcast_to(block, (count // 2, 2, size_y, size_z)).reshape(count, size_y, size_z)


def start_kernel(
    prev, cur, far, near, vel, to_one, to_two, to_far, packed, near_part, cur_s, near_s, c2_s
):
    width, size_y, size_z = prev.shape
    place = lax.axis_index("slab")
    odd = place % 2
    top = width - REACH
    data = pl.ds(8, size_y)
    weights = lane_weights(size_z)
    for ref, field in ((cur_s, cur), (near_s, near)):
        clear_margins(ref, size_y)
        for start in (0, REACH + width):
            ref[start : start + REACH, data, :] = jnp.zeros((REACH, size_y, size_z), jnp.float32)
        ref[REACH : REACH + width, data, :] = field[...]
    rows = vel.shape[0] * vel.shape[1]
    flat = vel[...].reshape(rows, vel.shape[2])
    packed[...] = jnp.concatenate([flat[: rows // 2], flat[rows // 2 :]], axis=1)
    fill_courant(c2_s, packed[...], size_z)
    for ch in range(0, width, STEP):
        factor = courant(c2_s, ch, STEP, size_y)
        centre, total = laplace(cur_s, ch + REACH, size_y, weights)
        part = 2.0 * centre - prev[ch : ch + STEP] + factor * total
        to_one[ch : ch + STEP] = part
        to_two[ch : ch + STEP] = part
        centre, total = laplace(near_s, ch + REACH, size_y, weights)
        near_part[ch : ch + STEP] = 2.0 * centre - far[ch : ch + STEP] + factor * total
    for ref, low in ((to_one, odd), (to_two, 1 - odd)):
        outer = pl.ds((1 - low) * top, REACH)
        ref[width : width + REACH] = cur[outer]
        ref[width + REACH : width + 2 * REACH] = near_part[outer]
        ref[width + 2 * REACH : width + 3 * REACH] = near[outer]
    to_far[0:REACH] = cur[pl.ds((1 - (place % 4) // 2) * top, REACH)]
    to_far[REACH:] = packed[...].reshape(to_far.shape[0] - REACH, size_y, size_z)


def split3(values):
    high = values.astype(jnp.bfloat16)
    rest = values - high.astype(jnp.float32)
    middle = rest.astype(jnp.bfloat16)
    low = (rest - middle.astype(jnp.float32)).astype(jnp.bfloat16)
    return (high, middle, low)


def wave_kernel(
    src_cell, src_step, wavelet, prev, cur, near, vel, rec, obs, own_part, near_part, packed,
    one, two, model_one, model_two, *rest, n_far, with_models
):
    fars = rest[:n_far]
    pay, samples = rest[n_far : n_far + 2]
    cur_s, near_s, hop_s, first_s, sec_s, two_s, vel_s, c2_s, img_s = rest[n_far + 2 :]
    width, size_y, size_z = prev.shape
    rows = vel.shape[0] * vel.shape[1]
    place = lax.axis_index("slab")
    odd = place % 2
    f32 = jnp.float32
    data = pl.ds(8, size_y)
    lane = lax.broadcasted_iota(jnp.int32, (1, size_z), 1)
    weights = lane_weights(size_z)
    wide = 2 * REACH
    clear_margins(first_s, size_y)
    clear_margins(two_s, size_y)
    cur_s[REACH : REACH + width] = cur[...]
    near_s[REACH : REACH + width] = near[...]
    first_s[wide : wide + width, data, :] = own_part[0:width]
    two_s[REACH : REACH + width, data, :] = near_part[...]
    short = packed.shape[0]
    vel_s[short : 2 * short] = packed[...]

    def put(block, model, high):
        outer = pl.ds(high * (width + REACH), REACH)
        first_s[pl.ds(high * (width + wide), width), data, :] = block[0:width]
        cur_s[outer] = block[width : width + REACH]
        two_s[outer, data, :] = block[width + REACH : width + 2 * REACH]
        near_s[outer] = block[width + 2 * REACH : width + 3 * REACH]
        vel_s[pl.ds(high * 2 * short, short)] = model

    put(one, model_one[...], 1 - odd)
    inner = (place > 0) & (place < lax.axis_size("slab") - 1)
    put(two, jnp.where(inner, model_two[...], 0.0), odd)
    far_high = 1 - (place % 4) // 2
    if n_far == 1:
        hop_s[pl.ds((1 - far_high) * REACH, REACH)] = jnp.zeros((REACH, size_y, size_z), f32)
    for index, block in enumerate(fars):
        high = far_high if index == 0 else 1 - far_high
        hop_s[pl.ds(high * REACH, REACH)] = block[0:REACH]
    fill_courant(c2_s, vel_s[...], size_z)

    def crossing(sources, depth):
        terms = [STENCIL_WEIGHTS[depth + 1 + j] * sources[j] for j in range(REACH - depth)]
        return sum(terms[1:], terms[0])

    def cross(ref, at, shift, upward, read):
        for depth in range(REACH):
            layer = at + depth if upward else at - 1 - depth
            sources = [read(j) for j in range(REACH - depth)]
            fine = (layer + shift) // 2 * size_y
            factor = c2_s[fine : fine + size_y, :]
            ref[layer, data, :] = ref[layer, data, :] + factor * crossing(sources, depth)

    cross(first_s, 0, 0, True, lambda j: hop_s[REACH - 1 - j])
    cross(first_s, wide, 0, False, lambda j: cur_s[REACH + j])
    cross(first_s, wide, 0, True, lambda j: cur_s[REACH - 1 - j])
    cross(first_s, wide + width, 0, False, lambda j: cur_s[REACH + width + j])
    cross(first_s, wide + width, 0, True, lambda j: cur_s[REACH + width - 1 - j])
    cross(first_s, 2 * wide + width, 0, False, lambda j: hop_s[REACH + j])
    cross(two_s, REACH, REACH, False, lambda j: near_s[REACH + j])
    cross(two_s, REACH, REACH, True, lambda j: near_s[REACH - 1 - j])
    cross(two_s, REACH + width, REACH, False, lambda j: near_s[REACH + width + j])
    cross(two_s, REACH + width, REACH, True, lambda j: near_s[REACH + width - 1 - j])

    plane = size_y * size_z
    cell = src_cell[0]
    now = src_step[0]
    src_y = (cell % plane) // size_z
    src_z = cell % size_z

    def inject(ref, start, layers, offset, pulse):
        layer = cell // plane - (place * width - start)
        inside = (layer >= 0) & (layer < layers)
        layer = jnp.clip(layer, 0, layers - 1)
        value = jnp.where(inside, pulse, 0.0)
        at = pl.ds(offset + src_y, 1)
        ref[layer, at, :] = ref[layer, at, :] + jnp.where(lane == src_z, value, 0.0)

    inject(first_s, wide, width + 2 * wide, 8, wavelet[now + 1])
    for ch in range(0, width + 2 * REACH, STEP):
        centre, total = laplace(first_s, ch + REACH, size_y, weights)
        factor = courant(c2_s, ch + REACH, STEP, size_y)
        sec_s[ch : ch + STEP] = 2.0 * centre - cur_s[ch : ch + STEP] + factor * total
    inject(sec_s, REACH, width + 2 * REACH, 0, wavelet[now + 2])

    region = (width + 2 * REACH) * size_y
    cells = rec[...]
    row = (cells - (place * width - REACH) * plane) // size_z
    hot = row == lax.broadcasted_iota(jnp.int32, (region, cells.shape[1]), 0)
    hot = jnp.where(hot, 1.0, 0.0).astype(jnp.bfloat16)
    lanes = lax.broadcasted_iota(jnp.int32, (size_z, cells.shape[1]), 0) == cells % size_z
    lo = REACH * size_y
    hi = lo + width * size_y
    own = (row >= lo) & (row < hi)

    def read(field, marks):
        turned = field.T
        total = sum(jnp.dot(part, marks, preferred_element_type=f32) for part in split3(turned))
        return jnp.sum(jnp.where(lanes, total, 0.0), axis=0, keepdims=True)

    def spread_out(values, marks):
        placed = jnp.where(lanes, values, 0.0)
        dims = (((1,), (1,)), ((), ()))
        return sum(lax.dot_general(marks, part, dims, preferred_element_type=f32) for part in split3(placed))

    first_own = first_s[wide : wide + width, data, :].reshape(width * size_y, size_z)
    read_one = read(first_own, hot[lo:hi])
    read_two = read(sec_s[...].reshape(region, size_z), hot)
    samples[0:1, :] = read_one
    samples[1:2, :] = jnp.where(own, read_two, 0.0)
    add_one = spread_out(read_one - obs[0:1, :], hot[lo:hi])
    add_two = spread_out(read_two - obs[1:2, :], hot)

    for ch in range(0, width + 2 * REACH, STEP):
        extra = add_two[ch * size_y : (ch + STEP) * size_y].reshape(STEP, size_y, size_z)
        two_s[ch : ch + STEP, data, :] = two_s[ch : ch + STEP, data, :] + extra
    for ch in range(0, width, STEP):
        centre, total = laplace(two_s, ch + REACH, size_y, weights)
        extra = add_one[ch * size_y : (ch + STEP) * size_y].reshape(STEP, size_y, size_z)
        factor = courant(c2_s, ch + wide, STEP, size_y)
        adj_one = 2.0 * centre - near[ch : ch + STEP] + factor * total + extra
        first = first_s[ch + wide : ch + wide + STEP, data, :]
        now_field = cur[ch : ch + STEP]
        bend_two = sec_s[ch + REACH : ch + REACH + STEP] - 2.0 * first + now_field
        bend_one = first - 2.0 * now_field + prev[ch : ch + STEP]
        image = centre * bend_two + adj_one * bend_one
        image = image.reshape(STEP // 2, 2, size_y, size_z)
        image = image[:, 0] + image[:, 1]
        img_s[ch // 2 * size_y : (ch + STEP) // 2 * size_y, :] = image.reshape(STEP // 2 * size_y, size_z)
    grid_r = lax.broadcasted_iota(jnp.int32, (size_z, size_z), 0)
    grid_c = lax.broadcasted_iota(jnp.int32, (size_z, size_z), 1)
    gather = jnp.where(grid_r // 2 == grid_c, 1.0, 0.0).astype(f32)
    folded = img_s[pl.ds(0, rows, stride=2), :] + img_s[pl.ds(1, rows, stride=2), :]
    blocks = jnp.dot(folded, gather, precision=HIGHEST, preferred_element_type=f32)
    own_vel = twice(vel[...])
    factor = 2.0 / (own_vel * own_vel * own_vel)
    pay[0:rows, :] = jnp.where(lane < size_z // 2, factor * blocks, own_vel)
    if with_models:
        pay[rows : rows + short, :] = model_one[...]
        pay[rows + short : rows + 2 * short, :] = model_two[...]
        pay[rows + 2 * short :, :] = fars[0][REACH:].reshape(short, size_z)


def mix_kernel(*refs, cells):
    count = len(refs) - 5
    pays = refs[:count]
    part, other, obs, update, misfit = refs[count:]
    f32 = jnp.float32
    misfit[...] = part[...] + other[...] - obs[...]
    rows = update.shape[0] * update.shape[1]
    lane = lax.broadcasted_iota(jnp.int32, (1, pays[0].shape[1]), 1)
    half = update.shape[2]
    model_lane = lane >= half
    total = pays[0].shape[0]
    mean = sum(ref[...] for ref in pays[1:]) + pays[0][...]
    mean = mean * (1.0 / count)

    def norm(diff):
        sq = diff * diff
        sq = jnp.concatenate([jnp.where(model_lane, sq[0:rows], 0.0), sq[rows:]], axis=0)
        sq = jnp.sum(sq.reshape(total // 8, 8, sq.shape[1]), axis=0)
        return jnp.sum(jnp.sum(sq, axis=1, keepdims=True), axis=0, keepdims=True)

    spread = jnp.zeros(mean.shape, f32)
    for ref in pays:
        diff = ref[...] - mean
        spread = spread + diff * diff
    spread = jnp.concatenate([jnp.where(model_lane, spread[0:rows], 0.0), spread[rows:]], axis=0)
    spread = jnp.sum(spread.reshape(total // 8, 8, spread.shape[1]), axis=0)
    spread = jnp.sum(jnp.sum(spread, axis=1, keepdims=True), axis=0, keepdims=True)
    band = (2.0 * count / (count * (count - 1))) * spread
    own = pays[0][...]
    mixed = own[0:rows]
    kernel_sum = jnp.ones((1, 1), f32)
    for ref in pays[1:]:
        weight = jnp.exp(-norm(ref[...] - own) / band)
        mixed = mixed + weight * ref[0:rows, :]
        kernel_sum = kernel_sum + weight
    coef = (2.0 * cells) / band
    pull = coef * (own[0:rows, half:] * kernel_sum - mixed[:, half:])
    update[...] = ((mixed[:, 0:half] + pull) * (1.0 / count)).reshape(update.shape)


def device_step(
    vel_coarse,
    fwd_prev,
    fwd_cur,
    adj_far,
    adj_near,
    src_cell,
    src_step,
    wavelet,
    rec_cell,
    observed,
):
    f32 = jnp.float32
    slabs = lax.axis_size("slab")
    count = lax.axis_size("particle")
    fast = is_fast(slabs, count)
    model = vel_coarse[0]
    prev, cur, far, near = fwd_prev[0], fwd_cur[0], adj_far[0], adj_near[0]
    width, size_y, size_z = prev.shape
    half, coarse_y, coarse_z = model.shape
    rows = half * coarse_y
    short = rows // 2
    near_layers = width + 3 * REACH
    far_layers = REACH + short // size_y
    in_vmem = pl.BlockSpec(memory_space=pltpu.VMEM)
    in_smem = pl.BlockSpec(memory_space=pltpu.SMEM)
    padded = pltpu.VMEM((width + 2 * REACH, PITCH, size_z), f32)
    start = pl.pallas_call(
        start_kernel,
        out_shape=(
            pltpu.VMEM((near_layers, size_y, size_z), f32),
            pltpu.VMEM((near_layers, size_y, size_z), f32),
            pltpu.VMEM((far_layers, size_y, size_z), f32),
            pltpu.VMEM((short, size_z), f32),
            pltpu.VMEM((width, size_y, size_z), f32),
        ),
        in_specs=[in_vmem] * 5,
        out_specs=(in_vmem,) * 5,
        scratch_shapes=[padded, padded, pltpu.VMEM((2 * rows, size_z), f32)],
        name="start_steps",
    )
    to_one, to_two, to_far, packed, near_part = start(prev, cur, far, near, model)
    even = [(i, i + 1) for i in range(0, slabs - 1, 2)]
    model_one = swap(packed, "slab", even)
    one = swap(to_one, "slab", even)
    uneven = [(i, i + 1) for i in range(1, slabs - 1, 2)]
    two = swap(to_two, "slab", uneven)
    fars = [swap(to_far, "slab", [(i, i + 2) for i in range(slabs - 2) if i % 4 < 2])]
    if fast:
        model_two = swap(model_one, "slab", [(0, 2), (1, 3)])
    else:
        model_two = swap(packed, "slab", uneven)
        others = [(i, i + 2) for i in range(slabs - 2) if i % 4 >= 2]
        if others:
            fars.append(swap(other_side(cur, to_far), "slab", others))
    receivers = rec_cell.shape[0]
    wide = 2 * REACH
    pay_rows = rows + 3 * short if fast else rows
    operands = (
        prev, cur, near, model, rec_cell[None], observed, to_one, near_part, packed,
        one, two, model_one, model_two, *fars,
    )
    plain = pltpu.VMEM((width + 2 * REACH, size_y, size_z), f32)
    pay, samples = pl.pallas_call(
        lambda *refs: wave_kernel(*refs, n_far=len(fars), with_models=fast),
        out_shape=(
            pltpu.VMEM((pay_rows, size_z), f32),
            pltpu.VMEM((2, receivers), f32),
        ),
        in_specs=[in_smem] * 3 + [in_vmem] * len(operands),
        out_specs=(in_vmem, in_vmem),
        scratch_shapes=[
            plain,
            plain,
            pltpu.VMEM((2 * REACH, size_y, size_z), f32),
            pltpu.VMEM((width + 2 * wide, PITCH, size_z), f32),
            plain,
            padded,
            pltpu.VMEM((3 * short, size_z), f32),
            pltpu.VMEM((6 * rows, size_z), f32),
            pltpu.VMEM((2 * rows, size_z), f32),
        ],
        name="wave_steps",
    )(src_cell, src_step, wavelet, *[resident(block) for block in operands])
    cells_coarse = rows * slabs * coarse_z
    if not fast:
        residual = lax.psum(samples, "slab") - observed
        gathered = lax.all_gather(pay, "particle", axis=0)
        models = gathered[:, :, coarse_z:]
        deltas = models[:, None] - models[None]
        dist = lax.psum(jnp.sum(deltas * deltas, axis=(2, 3)), "slab")
        band = jnp.sum(dist) / (count * (count - 1))
        row = lax.dynamic_index_in_dim(dist, lax.axis_index("particle"), 0, keepdims=False)
        weights = jnp.exp(-row / band)
        mixed = jnp.einsum("q,qrz->rz", weights, gathered, precision=HIGHEST)
        own = pay[:, coarse_z:]
        pull = (2.0 * cells_coarse / band) * (own * jnp.sum(weights) - mixed[:, coarse_z:])
        update = (mixed[:, :coarse_z] + pull) / count
        return (update.reshape(model.shape)[None], residual[None])

    blocks = {0: pay}
    for flip in (6, 4, 2):
        blocks[flip] = swap(pay, "particle", [(i, i ^ flip) for i in range(count) if i < i ^ flip])
    for flip in (0, 6, 4, 2):
        pairs = [(i, i ^ 1) for i in range(0, count, 2)]
        blocks[flip + 1] = swap(blocks[flip], "particle", pairs)
    part = samples + swap(samples, "slab", [(0, 1), (2, 3)])
    other = swap(part, "slab", [(0, 2), (1, 3)])
    update, residual = pl.pallas_call(
        lambda *refs: mix_kernel(*refs, cells=cells_coarse),
        out_shape=(
            jax.ShapeDtypeStruct(model.shape, f32),
            jax.ShapeDtypeStruct((2, receivers), f32),
        ),
        in_specs=[in_vmem] * 11,
        out_specs=(in_vmem, in_vmem),
        name="mix_particles",
    )(*[resident(blocks[i]) for i in range(count)], resident(part), resident(other), resident(observed))
    return (update[None], residual[None])


def other_side(cur, sent):
    top = cur.shape[0] - REACH
    low_first = (lax.axis_index("slab") % 4) // 2 == 0
    outer = jnp.where(low_first, cur[:REACH], cur[top:])
    return jnp.concatenate([outer, sent[REACH:]], axis=0)


def solution(mesh):
    in_specs = (
        P("particle", "slab", None, None),
        P("particle", "slab", None, None),
        P("particle", "slab", None, None),
        P("particle", "slab", None, None),
        P("particle", "slab", None, None),
        P("particle"),
        P("particle"),
        P(),
        P(),
        P(),
    )
    out_specs = (P("particle", "slab", None, None), P("particle", None, None))
    return jax.shard_map(
        device_step, mesh=mesh, in_specs=in_specs, out_specs=out_specs, check_vma=False
    )
```

time: 38.1 us -> 37.2 us (0.976)
  waiting for transfers between devices: 13.4 us -> 11.4 us
  starting transfers between devices: 16.6 us -> 18.2 us
  Pallas kernels: 5.88 us -> 4.69 us
  local copies, waits for them, and re-layouts: 0.01 us -> 0.65 us
    ppermute x14, waiting for transfers between devices: 13.4 us -> 11.4 us  [swap(): return lax.ppermute(block, axis, both)]
    ppermute x14, starting transfers between devices: 16.6 us -> 18.2 us  [swap(): return lax.ppermute(block, axis, both)]
    pallas_call x1, Pallas kernels: 3.28 us -> 2.41 us  [device_step(): pl.pallas_call(lambda *refs: wave_kernel(*refs, n_far=len(fars), with_mod...]
    pallas_call x1, Pallas kernels: 1.58 us -> 0.88 us  [device_step(): pl.pallas_call(lambda *refs: mix_kernel(*refs, cells=cells_coarse), out_s...]
    unnamed x2 -> x12, local copies, waits for them, and re-layouts: 0.01 us -> 0.65 us
where the time goes in v3:
time: 37.2 us; the launch traced here: 37 us
  starting transfers between devices  18.2 us (49%)
  waiting for transfers between devices  11.4 us (31%)
  Pallas kernels  4.69 us (13%)
  between operations  2.06 us (6%)
  local copies, waits for them, and re-layouts  0.65 us (2%)
    ppermute x14, starting transfers between devices, swap(): return lax.ppermute(block, axis, both)  18.2 us
    ppermute x14, waiting for transfers between devices, swap(): return lax.ppermute(block, axis, both)  11.4 us
    pallas_call x1, Pallas kernels, device_step(): pl.pallas_call(lambda *refs: wave_kernel(*refs, n_far=len(fars), with_mod...  2.41 us
    pallas_call x1, Pallas kernels, device_step(): start(prev, cur, far, near, model)  1.4 us
    pallas_call x1, Pallas kernels, device_step(): pl.pallas_call(lambda *refs: mix_kernel(*refs, cells=cells_coarse), out_s...  0.88 us
  transfers between devices with their start and end apart: 14, of which 7 were waited for; matrix products, arithmetic and copies ran while one was open for 0% of the time, Pallas kernels for 0%

profile of v3, /device:TPU:0, one launch (start us, length us, event | category | flops | bytes accessed | tf_op | source)
XLA Modules:
  0.0 37.0 jit_solution(8661102208411584099)
XLA Ops:
  0.7 1.4 %start_steps.1 = (f32[20,16,128]{2,1,0:T(8,128)S(1)}, f32[20,16,128]{2,1,0:T(8,128)S(1)}, f32[5,16,128]{2,1,0:T(8,128)S(1)}, f32[16,128]{1,0:T(8,128)S(1)}, f32[8,16,128]{2,1,0:T(8,128)S(1)}) custom-call(f32[8,16,128]{2,1,0:T(8,128)} %bitcast.8, f32[8,16,128]{2,1,0:T(8,128)} %bitcast.10, f32[8,16,128]{2,1,0:T(8,128)} %bitcast.17, f32[8,16,128]{2,1,0:T(8,128)} %bitcast.12, ...), custom_call_target="tpu_custom_call" | custom-call | tf_op jit(solution)/shard_map/start_steps/pallas_call | solution.py:361
  2.1 0.7 %collective-permute-start.1 = (f32[20,16,128]{2,1,0:T(8,128)S(1)}, f32[20,16,128]{2,1,0:T(8,128)S(1)}, u32[]{:S(2)}, u32[]{:S(2)}) collective-permute-start(f32[20,16,128]{2,1,0:T(8,128)S(1)} %get-tuple-element.14), channel_id=1, source_target_pairs={{1,2},{2,1},{5,6},{6,5},{9,10},{10,9},{13,14},{14,13},{17,18},{18,... | collective-permute-start | bytes 491528 | tf_op jit(solution)/shard_map/ppermute | solution.py:27
  2.8 5.9 %collective-permute-start = (f32[20,16,128]{2,1,0:T(8,128)S(1)}, f32[20,16,128]{2,1,0:T(8,128)S(1)}, u32[]{:S(2)}, u32[]{:S(2)}) collective-permute-start(f32[20,16,128]{2,1,0:T(8,128)S(1)} %get-tuple-element.11.refs_9_), channel_id=1, source_target_pairs={{0,1},{2,3},{1,0},{3,2},{4,5},{6,7},{5,4},{7,6},{8,9},{10,11},{9,8... | collective-permute-start | bytes 491528 | tf_op jit(solution)/shard_map/ppermute | solution.py:27
  8.7 1.9 %collective-permute-start.2 = (f32[16,128]{1,0:T(8,128)S(1)}, f32[16,128]{1,0:T(8,128)S(1)}, u32[]{:S(2)}, u32[]{:S(2)}) collective-permute-start(f32[16,128]{1,0:T(8,128)S(1)} %get-tuple-element.13.refs_11_), channel_id=1, source_target_pairs={{0,1},{2,3},{1,0},{3,2},{4,5},{6,7},{5,4},{7,6},{8,9},{10,11},{9,8... | collective-permute-start | bytes 24584 | tf_op jit(solution)/shard_map/ppermute | solution.py:27
  10.6 2.6 %collective-permute-done.2.refs_14_ = f32[16,128]{1,0:T(8,128)S(1)} collective-permute-done((f32[16,128]{1,0:T(8,128)S(1)}, f32[16,128]{1,0:T(8,128)S(1)}, u32[]{:S(2)}, u32[]{:S(2)}) %collective-permute-start.2) | collective-permute-done | bytes 8224 | tf_op jit(solution)/shard_map/ppermute | solution.py:27
  13.2 2.1 %collective-permute-start.3 = (f32[16,128]{1,0:T(8,128)S(1)}, f32[16,128]{1,0:T(8,128)S(1)}, u32[]{:S(2)}, u32[]{:S(2)}) collective-permute-start(f32[16,128]{1,0:T(8,128)S(1)} %collective-permute-done.2.refs_14_), channel_id=1, source_target_pairs={{0,2},{1,3},{2,0},{3,1},{4,6},{5,7},{6,4},{7,5},{8,10},{9,11},{10,... | collective-permute-start | bytes 24584 | tf_op jit(solution)/shard_map/ppermute | solution.py:27
  16.6 0.0 copy-start.4
  16.6 1.2 %collective-permute-done.3.refs_15_ = f32[16,128]{1,0:T(8,128)S(1)} collective-permute-done((f32[16,128]{1,0:T(8,128)S(1)}, f32[16,128]{1,0:T(8,128)S(1)}, u32[]{:S(2)}, u32[]{:S(2)}) %collective-permute-start.3) | collective-permute-done | bytes 8224 | tf_op jit(solution)/shard_map/ppermute | solution.py:27
  17.8 0.0 collective-permute-done.4.refs_16_
  17.8 0.0 copy-start.5
  17.8 0.6 %copy-done.5 = s32[256]{0:T(256)S(1)} copy-done((s32[256]{0:T(256)S(1)}, s32[256]{0:T(256)}, u32[]{:S(2)}) %copy-start.5) | copy-done | bytes 1048
  18.5 2.4 %wave_steps.1 = (f32[80,128]{1,0:T(8,128)S(1)}, f32[2,256]{1,0:T(2,128)S(1)}) custom-call(s32[1]{0:T(128)S(6)} %copy.12.refs_0_, s32[1]{0:T(128)S(6)} %copy.13.refs_1_, f32[64]{0:T(128)} %refs_2_.1, f32[8,16,128]{2,1,0:T(8,128)S(1)} %bitcast.9, f32[8,16,128]{2,1,0:T(8,128)S(1)} %bitcast.11, f32[8,16,128]{2,1,0:T(8,128)S(1)} %bitcast.13, ...), custom_call_target="tpu_custom_call" | custom-call | tf_op jit(solution)/shard_map/wave_steps/pallas_call | solution.py:383
  20.9 2.5 %collective-permute-start.10 = (f32[80,128]{1,0:T(8,128)S(1)}, f32[80,128]{1,0:T(8,128)S(1)}, u32[]{:S(2)}, u32[]{:S(2)}) collective-permute-start(f32[80,128]{1,0:T(8,128)S(1)} %get-tuple-element.16.refs_0_), channel_id=1, source_target_pairs={{0,24},{4,28},{8,16},{12,20},{24,0},{28,4},{16,8},{20,12},{1,25},{... | collective-permute-start | bytes 122888 | tf_op jit(solution)/shard_map/ppermute | solution.py:27
  23.4 0.5 %collective-permute-start.8 = (f32[80,128]{1,0:T(8,128)S(1)}, f32[80,128]{1,0:T(8,128)S(1)}, u32[]{:S(2)}, u32[]{:S(2)}) collective-permute-start(f32[80,128]{1,0:T(8,128)S(1)} %get-tuple-element.16.refs_0_), channel_id=1, source_target_pairs={{0,16},{4,20},{8,24},{12,28},{16,0},{20,4},{24,8},{28,12},{1,17},{... | collective-permute-start | bytes 122888 | tf_op jit(solution)/shard_map/ppermute | solution.py:27
  23.9 0.5 %collective-permute-start.6 = (f32[80,128]{1,0:T(8,128)S(1)}, f32[80,128]{1,0:T(8,128)S(1)}, u32[]{:S(2)}, u32[]{:S(2)}) collective-permute-start(f32[80,128]{1,0:T(8,128)S(1)} %get-tuple-element.16.refs_0_), channel_id=1, source_target_pairs={{0,8},{4,12},{16,24},{20,28},{8,0},{12,4},{24,16},{28,20},{1,9},{5... | collective-permute-start | bytes 122888 | tf_op jit(solution)/shard_map/ppermute | solution.py:27
  24.4 1.4 %collective-permute-done.10.refs_6_ = f32[80,128]{1,0:T(8,128)S(1)} collective-permute-done((f32[80,128]{1,0:T(8,128)S(1)}, f32[80,128]{1,0:T(8,128)S(1)}, u32[]{:S(2)}, u32[]{:S(2)}) %collective-permute-start.10) | collective-permute-done | bytes 40992 | tf_op jit(solution)/shard_map/ppermute | solution.py:27
  25.8 1.5 %collective-permute-done.8.refs_4_ = f32[80,128]{1,0:T(8,128)S(1)} collective-permute-done((f32[80,128]{1,0:T(8,128)S(1)}, f32[80,128]{1,0:T(8,128)S(1)}, u32[]{:S(2)}, u32[]{:S(2)}) %collective-permute-start.8) | collective-permute-done | bytes 40992 | tf_op jit(solution)/shard_map/ppermute | solution.py:27
  27.4 0.5 %collective-permute-done.6.refs_2_ = f32[80,128]{1,0:T(8,128)S(1)} collective-permute-done((f32[80,128]{1,0:T(8,128)S(1)}, f32[80,128]{1,0:T(8,128)S(1)}, u32[]{:S(2)}, u32[]{:S(2)}) %collective-permute-start.6) | collective-permute-done | bytes 40992 | tf_op jit(solution)/shard_map/ppermute | solution.py:27
  27.9 0.0 collective-permute-start.7
  27.9 2.2 %collective-permute-start.12 = (f32[2,256]{1,0:T(2,128)S(1)}, f32[2,256]{1,0:T(2,128)S(1)}, u32[]{:S(2)}, u32[]{:S(2)}) collective-permute-start(f32[2,256]{1,0:T(2,128)S(1)} %get-tuple-element.17), channel_id=1, source_target_pairs={{0,1},{2,3},{1,0},{3,2},{4,5},{6,7},{5,4},{7,6},{8,9},{10,11},{9,8... | collective-permute-start | bytes 6152 | tf_op jit(solution)/shard_map/ppermute | solution.py:27
  30.1 1.6 %collective-permute-done.12 = f32[2,256]{1,0:T(2,128)S(1)} collective-permute-done((f32[2,256]{1,0:T(2,128)S(1)}, f32[2,256]{1,0:T(2,128)S(1)}, u32[]{:S(2)}, u32[]{:S(2)}) %collective-permute-start.12) | collective-permute-done | bytes 2080 | tf_op jit(solution)/shard_map/ppermute | solution.py:27
  31.6 1.9 %collective-permute-start.13 = (f32[2,256]{1,0:T(2,128)S(1)}, f32[2,256]{1,0:T(2,128)S(1)}, u32[]{:S(2)}, u32[]{:S(2)}) collective-permute-start(f32[2,256]{1,0:T(2,128)S(1)} %add.3.refs_8_), channel_id=1, source_target_pairs={{0,2},{1,3},{2,0},{3,1},{4,6},{5,7},{6,4},{7,5},{8,10},{9,11},{10,... | collective-permute-start | bytes 6152 | tf_op jit(solution)/shard_map/ppermute | solution.py:27
  33.5 2.6 %collective-permute-done.13.refs_9_ = f32[2,256]{1,0:T(2,128)S(1)} collective-permute-done((f32[2,256]{1,0:T(2,128)S(1)}, f32[2,256]{1,0:T(2,128)S(1)}, u32[]{:S(2)}, u32[]{:S(2)}) %collective-permute-start.13) | collective-permute-done | bytes 2080 | tf_op jit(solution)/shard_map/ppermute | solution.py:27
  36.1 0.9 %mix_particles.1 = (f32[4,8,64]{2,1,0:T(8,128)}, f32[2,256]{1,0:T(2,128)}) custom-call(f32[80,128]{1,0:T(8,128)S(1)} %get-tuple-element.16.refs_0_, f32[80,128]{1,0:T(8,128)S(1)} %collective-permute-done.5.refs_1_, f32[80,128]{1,0:T(8,128)S(1)} %collective-permute-done.6.refs_2_, f32[80,128]{1,0:T(8,128)S(1)} %collective-permute-done.7.refs_3_, ...), custom_call_target="tpu_custom_call" | custom-call | tf_op jit(solution)/shard_map/mix_particles/pallas_call | solution.py:428
  (20 shorter events, 0.0 us)
Async XLA Ops:
  0.6 17.2 %copy-start = (f32[1,8,16,128]{3,2,1,0:T(8,128)S(1)}, f32[1,8,16,128]{3,2,1,0:T(8,128)}, u32[]{:S(2)}) copy-start(f32[1,8,16,128]{3,2,1,0:T(8,128)} %param.11) | copy-start | bytes 196612
  0.6 17.2 %copy-start.1 = (f32[1,8,16,128]{3,2,1,0:T(8,128)S(1)}, f32[1,8,16,128]{3,2,1,0:T(8,128)}, u32[]{:S(2)}) copy-start(f32[1,8,16,128]{3,2,1,0:T(8,128)} %param.12) | copy-start | bytes 196612
  0.7 17.2 %copy-start.2 = (f32[1,8,16,128]{3,2,1,0:T(8,128)S(1)}, f32[1,8,16,128]{3,2,1,0:T(8,128)}, u32[]{:S(2)}) copy-start(f32[1,8,16,128]{3,2,1,0:T(8,128)} %param.14) | copy-start | bytes 196612
  0.7 17.2 %copy-start.3 = (f32[1,4,8,64]{3,2,1,0:T(8,128)S(1)}, f32[1,4,8,64]{3,2,1,0:T(8,128)}, u32[]{:S(2)}) copy-start(f32[1,4,8,64]{3,2,1,0:T(8,128)} %param.10) | copy-start | bytes 24580
  2.1 15.7 %collective-permute-start.1 = (f32[20,16,128]{2,1,0:T(8,128)S(1)}, f32[20,16,128]{2,1,0:T(8,128)S(1)}, u32[]{:S(2)}, u32[]{:S(2)}) collective-permute-start(f32[20,16,128]{2,1,0:T(8,128)S(1)} %get-tuple-element.14), channel_id=1, source_target_pairs={{1,2},{2,1},{5,6},{6,5},{9,10},{10,9},{13,14},{14,13},{17,18},{18,... | collective-permute-start | bytes 491528 | tf_op jit(solution)/shard_map/ppermute | solution.py:27
  2.8 15.0 %collective-permute-start = (f32[20,16,128]{2,1,0:T(8,128)S(1)}, f32[20,16,128]{2,1,0:T(8,128)S(1)}, u32[]{:S(2)}, u32[]{:S(2)}) collective-permute-start(f32[20,16,128]{2,1,0:T(8,128)S(1)} %get-tuple-element.11.refs_9_), channel_id=1, source_target_pairs={{0,1},{2,3},{1,0},{3,2},{4,5},{6,7},{5,4},{7,6},{8,9},{10,11},{9,8... | collective-permute-start | bytes 491528 | tf_op jit(solution)/shard_map/ppermute | solution.py:27
  8.7 9.1 %collective-permute-start.4 = (f32[5,16,128]{2,1,0:T(8,128)S(1)}, f32[5,16,128]{2,1,0:T(8,128)S(1)}, u32[]{:S(2)}, u32[]{:S(2)}) collective-permute-start(f32[5,16,128]{2,1,0:T(8,128)S(1)} %get-tuple-element.15), channel_id=1, source_target_pairs={{0,2},{1,3},{2,0},{3,1},{4,6},{5,7},{6,4},{7,5},{8,10},{9,11},{10,... | collective-permute-start | bytes 122888 | tf_op jit(solution)/shard_map/ppermute | solution.py:27
  8.7 4.5 %collective-permute-start.2 = (f32[16,128]{1,0:T(8,128)S(1)}, f32[16,128]{1,0:T(8,128)S(1)}, u32[]{:S(2)}, u32[]{:S(2)}) collective-permute-start(f32[16,128]{1,0:T(8,128)S(1)} %get-tuple-element.13.refs_11_), channel_id=1, source_target_pairs={{0,1},{2,3},{1,0},{3,2},{4,5},{6,7},{5,4},{7,6},{8,9},{10,11},{9,8... | collective-permute-start | bytes 24584 | tf_op jit(solution)/shard_map/ppermute | solution.py:27
  13.2 4.5 %collective-permute-start.3 = (f32[16,128]{1,0:T(8,128)S(1)}, f32[16,128]{1,0:T(8,128)S(1)}, u32[]{:S(2)}, u32[]{:S(2)}) collective-permute-start(f32[16,128]{1,0:T(8,128)S(1)} %collective-permute-done.2.refs_14_), channel_id=1, source_target_pairs={{0,2},{1,3},{2,0},{3,1},{4,6},{5,7},{6,4},{7,5},{8,10},{9,11},{10,... | collective-permute-start | bytes 24584 | tf_op jit(solution)/shard_map/ppermute | solution.py:27
  16.6 1.3 %copy-start.4 = (f32[2,256]{1,0:T(2,128)S(1)}, f32[2,256]{1,0:T(2,128)}, u32[]{:S(2)}) copy-start(f32[2,256]{1,0:T(2,128)} %refs_10_.1) | copy-start | bytes 6148
  17.8 0.7 %copy-start.5 = (s32[256]{0:T(256)S(1)}, s32[256]{0:T(256)}, u32[]{:S(2)}) copy-start(s32[256]{0:T(256)} %param.18) | copy-start | bytes 3076
  20.9 4.9 %collective-permute-start.10 = (f32[80,128]{1,0:T(8,128)S(1)}, f32[80,128]{1,0:T(8,128)S(1)}, u32[]{:S(2)}, u32[]{:S(2)}) collective-permute-start(f32[80,128]{1,0:T(8,128)S(1)} %get-tuple-element.16.refs_0_), channel_id=1, source_target_pairs={{0,24},{4,28},{8,16},{12,20},{24,0},{28,4},{16,8},{20,12},{1,25},{... | collective-permute-start | bytes 122888 | tf_op jit(solution)/shard_map/ppermute | solution.py:27
  23.4 4.0 %collective-permute-start.8 = (f32[80,128]{1,0:T(8,128)S(1)}, f32[80,128]{1,0:T(8,128)S(1)}, u32[]{:S(2)}, u32[]{:S(2)}) collective-permute-start(f32[80,128]{1,0:T(8,128)S(1)} %get-tuple-element.16.refs_0_), channel_id=1, source_target_pairs={{0,16},{4,20},{8,24},{12,28},{16,0},{20,4},{24,8},{28,12},{1,17},{... | collective-permute-start | bytes 122888 | tf_op jit(solution)/shard_map/ppermute | solution.py:27
  23.9 4.0 %collective-permute-start.6 = (f32[80,128]{1,0:T(8,128)S(1)}, f32[80,128]{1,0:T(8,128)S(1)}, u32[]{:S(2)}, u32[]{:S(2)}) collective-permute-start(f32[80,128]{1,0:T(8,128)S(1)} %get-tuple-element.16.refs_0_), channel_id=1, source_target_pairs={{0,8},{4,12},{16,24},{20,28},{8,0},{12,4},{24,16},{28,20},{1,9},{5... | collective-permute-start | bytes 122888 | tf_op jit(solution)/shard_map/ppermute | solution.py:27
  24.4 11.7 %collective-permute-start.5 = (f32[80,128]{1,0:T(8,128)S(1)}, f32[80,128]{1,0:T(8,128)S(1)}, u32[]{:S(2)}, u32[]{:S(2)}) collective-permute-start(f32[80,128]{1,0:T(8,128)S(1)} %get-tuple-element.16.refs_0_), channel_id=1, source_target_pairs={{0,4},{8,12},{16,20},{24,28},{4,0},{12,8},{20,16},{28,24},{1,5},{9... | collective-permute-start | bytes 122888 | tf_op jit(solution)/shard_map/ppermute | solution.py:27
  25.8 10.3 %collective-permute-start.11 = (f32[80,128]{1,0:T(8,128)S(1)}, f32[80,128]{1,0:T(8,128)S(1)}, u32[]{:S(2)}, u32[]{:S(2)}) collective-permute-start(f32[80,128]{1,0:T(8,128)S(1)} %collective-permute-done.10.refs_6_), channel_id=1, source_target_pairs={{0,4},{8,12},{16,20},{24,28},{4,0},{12,8},{20,16},{28,24},{1,5},{9... | collective-permute-start | bytes 122888 | tf_op jit(solution)/shard_map/ppermute | solution.py:27
  27.4 8.8 %collective-permute-start.9 = (f32[80,128]{1,0:T(8,128)S(1)}, f32[80,128]{1,0:T(8,128)S(1)}, u32[]{:S(2)}, u32[]{:S(2)}) collective-permute-start(f32[80,128]{1,0:T(8,128)S(1)} %collective-permute-done.8.refs_4_), channel_id=1, source_target_pairs={{0,4},{8,12},{16,20},{24,28},{4,0},{12,8},{20,16},{28,24},{1,5},{9... | collective-permute-start | bytes 122888 | tf_op jit(solution)/shard_map/ppermute | solution.py:27
  27.9 8.3 %collective-permute-start.7 = (f32[80,128]{1,0:T(8,128)S(1)}, f32[80,128]{1,0:T(8,128)S(1)}, u32[]{:S(2)}, u32[]{:S(2)}) collective-permute-start(f32[80,128]{1,0:T(8,128)S(1)} %collective-permute-done.6.refs_2_), channel_id=1, source_target_pairs={{0,4},{8,12},{16,20},{24,28},{4,0},{12,8},{20,16},{28,24},{1,5},{9... | collective-permute-start | bytes 122888 | tf_op jit(solution)/shard_map/ppermute | solution.py:27
  27.9 3.7 %collective-permute-start.12 = (f32[2,256]{1,0:T(2,128)S(1)}, f32[2,256]{1,0:T(2,128)S(1)}, u32[]{:S(2)}, u32[]{:S(2)}) collective-permute-start(f32[2,256]{1,0:T(2,128)S(1)} %get-tuple-element.17), channel_id=1, source_target_pairs={{0,1},{2,3},{1,0},{3,2},{4,5},{6,7},{5,4},{7,6},{8,9},{10,11},{9,8... | collective-permute-start | bytes 6152 | tf_op jit(solution)/shard_map/ppermute | solution.py:27
  31.6 4.5 %collective-permute-start.13 = (f32[2,256]{1,0:T(2,128)S(1)}, f32[2,256]{1,0:T(2,128)S(1)}, u32[]{:S(2)}, u32[]{:S(2)}) collective-permute-start(f32[2,256]{1,0:T(2,128)S(1)} %add.3.refs_8_), channel_id=1, source_target_pairs={{0,2},{1,3},{2,0},{3,1},{4,6},{5,7},{6,4},{7,5},{8,10},{9,11},{10,... | collective-permute-start | bytes 6152 | tf_op jit(solution)/shard_map/ppermute | solution.py:27

commit v4 on v3

--- a/solution.py
+++ b/solution.py
@@ -88,41 +88,6 @@
     return jnp.broadcast_to(block, (count // 2, 2, size_y, size_z)).reshape(count, size_y, size_z)
 
 
-def start_kernel(
-    prev, cur, far, near, vel, to_one, to_two, to_far, packed, near_part, cur_s, near_s, c2_s
-):
-    width, size_y, size_z = prev.shape
-    place = lax.axis_index("slab")
-    odd = place % 2
-    top = width - REACH
-    data = pl.ds(8, size_y)
-    weights = lane_weights(size_z)
-    for ref, field in ((cur_s, cur), (near_s, near)):
-        clear_margins(ref, size_y)
-        for start in (0, REACH + width):
-            ref[start : start + REACH, data, :] = jnp.zeros((REACH, size_y, size_z), jnp.float32)
-        ref[REACH : REACH + width, data, :] = field[...]
-    rows = vel.shape[0] * vel.shape[1]
-    flat = vel[...].reshape(rows, vel.shape[2])
-    packed[...] = jnp.concatenate([flat[: rows // 2], flat[rows // 2 :]], axis=1)
-    fill_courant(c2_s, packed[...], size_z)
-    for ch in range(0, width, STEP):
-        factor = courant(c2_s, ch, STEP, size_y)
-        centre, total = laplace(cur_s, ch + REACH, size_y, weights)
-        part = 2.0 * centre - prev[ch : ch + STEP] + factor * total
-        to_one[ch : ch + STEP] = part
-        to_two[ch : ch + STEP] = part
-        centre, total = laplace(near_s, ch + REACH, size_y, weights)
-        near_part[ch : ch + STEP] = 2.0 * centre - far[ch : ch + STEP] + factor * total
-    for ref, low in ((to_one, odd), (to_two, 1 - odd)):
-        outer = pl.ds((1 - low) * top, REACH)
-        ref[width : width + REACH] = cur[outer]
-        ref[width + REACH : width + 2 * REACH] = near_part[outer]
-        ref[width + 2 * REACH : width + 3 * REACH] = near[outer]
-    to_far[0:REACH] = cur[pl.ds((1 - (place % 4) // 2) * top, REACH)]
-    to_far[REACH:] = packed[...].reshape(to_far.shape[0] - REACH, size_y, size_z)
-
-
 def split3(values):
     high = values.astype(jnp.bfloat16)
     rest = values - high.astype(jnp.float32)
@@ -131,15 +96,88 @@
     return (high, middle, low)
 
 
+def start_kernel(
+    prev, cur, far, near, vel, rec, obs, wavelet, to_one, to_two, to_far, packed,
+    own_part, near_part, lanes_out, rec_out, wavelet_out, obs_out, cur_s, near_s, c2_s
+):
+    width, size_y, size_z = prev.shape
+    f32 = jnp.float32
+    place = lax.axis_index("slab")
+    odd = place % 2
+    top = width - REACH
+    plane = size_y * size_z
+    data = pl.ds(8, size_y)
+    weights = lane_weights(size_z)
+    for ref, field in ((cur_s, cur), (near_s, near)):
+        clear_margins(ref, size_y)
+        for start in (0, REACH + width):
+            ref[start : start + REACH, data, :] = jnp.zeros((REACH, size_y, size_z), f32)
+        ref[REACH : REACH + width, data, :] = field[...]
+    rows = vel.shape[0] * vel.shape[1]
+    flat = vel[...].reshape(rows, vel.shape[2])
+    packed[...] = jnp.concatenate([flat[: rows // 2], flat[rows // 2 :]], axis=1)
+    fill_courant(c2_s, packed[...], size_z)
+    rec_out[...] = rec[...]
+    obs_out[...] = obs[...]
+    wavelet_out[...] = wavelet[...]
+    for ch in range(0, width, STEP):
+        factor = courant(c2_s, ch, STEP, size_y)
+        centre, total = laplace(cur_s, ch + REACH, size_y, weights)
+        part = 2.0 * centre - prev[ch : ch + STEP] + factor * total
+        own_part[ch : ch + STEP] = part
+        centre, total = laplace(near_s, ch + REACH, size_y, weights)
+        near_part[ch : ch + STEP] = 2.0 * centre - far[ch : ch + STEP] + factor * total
+
+    cells = rec[...]
+    count = cells.shape[1]
+    lanes = lax.broadcasted_iota(jnp.int32, (size_z, count), 0) == cells % size_z
+    lanes = jnp.where(lanes, 1.0, 0.0).astype(jnp.bfloat16)
+    lanes_out[...] = lanes
+    in_row = lax.broadcasted_iota(jnp.int32, (size_y, count), 0) == cells % plane // size_z
+    fields = jnp.concatenate(
+        [own_part[...].reshape(width * size_y, size_z), c2_s[...], cur[...].reshape(width * size_y, size_z)],
+        axis=0,
+    )
+    picked = sum(jnp.dot(part, lanes, preferred_element_type=f32) for part in split3(fields))
+    picked = picked.reshape(-1, size_y, count)
+    picked = jnp.sum(jnp.where(in_row[None], picked, 0.0), axis=1)
+    half = width // 2
+    columns = picked[width + half :]
+    for ref, low in ((to_one, odd), (to_two, 1 - odd)):
+        outer = pl.ds((1 - low) * top, REACH)
+        ref[0:REACH] = own_part[outer]
+        ref[REACH : 2 * REACH] = cur[outer]
+        ref[2 * REACH : 3 * REACH] = near_part[outer]
+        ref[3 * REACH : 4 * REACH] = near[outer]
+        deep = jnp.where(low == 0, picked[0:REACH], picked[top:width])
+        block = jnp.concatenate([deep, picked[width : width + half]], axis=0)
+        ref[4 * REACH :] = fold(block, size_y, size_z)
+    to_far[0:1] = fold(columns, size_y, size_z)
+    to_far[1:] = packed[...].reshape(to_far.shape[0] - 1, size_y, size_z)
+
+
+def fold(block, size_y, size_z):
+    pieces = [block[:, at : at + size_z] for at in range(0, block.shape[1], size_z)]
+    return jnp.concatenate(pieces, axis=0).reshape(-1, size_y, size_z)
+
+
+def unfold(layer, count):
+    flat = layer.reshape(-1, layer.shape[-1])
+    rows = flat.shape[0] * flat.shape[1] // count
+    return jnp.concatenate([flat[at : at + rows] for at in range(0, flat.shape[0], rows)], axis=1)
+
+
 def wave_kernel(
-    src_cell, src_step, wavelet, prev, cur, near, vel, rec, obs, own_part, near_part, packed,
+    src_cell, src_step, prev, cur, near, vel, own_part, near_part, packed, lanes_in, rec, wavelet, obs,
     one, two, model_one, model_two, *rest, n_far, with_models
 ):
     fars = rest[:n_far]
     pay, samples = rest[n_far : n_far + 2]
-    cur_s, near_s, hop_s, first_s, sec_s, two_s, vel_s, c2_s, img_s = rest[n_far + 2 :]
+    cur_s, near_s, first_s, sec_s, two_s, vel_s, c2_s, img_s = rest[n_far + 2 :]
     width, size_y, size_z = prev.shape
     rows = vel.shape[0] * vel.shape[1]
+    receivers = rec.shape[1]
+    plane = size_y * size_z
     place = lax.axis_index("slab")
     odd = place % 2
     f32 = jnp.float32
@@ -149,30 +187,74 @@
     wide = 2 * REACH
     clear_margins(first_s, size_y)
     clear_margins(two_s, size_y)
+    for start in (0, width + wide + REACH):
+        first_s[start : start + REACH, data, :] = jnp.zeros((REACH, size_y, size_z), f32)
     cur_s[REACH : REACH + width] = cur[...]
     near_s[REACH : REACH + width] = near[...]
-    first_s[wide : wide + width, data, :] = own_part[0:width]
+    first_s[wide : wide + width, data, :] = own_part[...]
     two_s[REACH : REACH + width, data, :] = near_part[...]
     short = packed.shape[0]
     vel_s[short : 2 * short] = packed[...]
 
+    cell = src_cell[0]
+    now = src_step[0]
+    src_layer = cell // plane - place * width
+    same_column = rec[...] % plane == cell % plane
+
+    ticks = lax.broadcasted_iota(jnp.int32, wavelet.shape, 1)
+
+    def pulse(ahead):
+        return jnp.sum(jnp.where(ticks == now + ahead, wavelet[...], 0.0), axis=1, keepdims=True)
+
+    pulse_one = pulse(1)
+
+    def inject(ref, start, layers, offset, pulse):
+        layer = src_layer + start
+        inside = (layer >= 0) & (layer < layers)
+        layer = jnp.clip(layer, 0, layers - 1)
+        value = jnp.where(inside, pulse, 0.0)
+        at = pl.ds(offset + cell % plane // size_z, 1)
+        ref[layer, at, :] = ref[layer, at, :] + jnp.where(lane == cell % size_z, value, 0.0)
+
+    far_high = 1 - (place % 4) // 2
+    hops = [unfold(block[0:1], receivers) for block in fars]
+
     def put(block, model, high):
         outer = pl.ds(high * (width + REACH), REACH)
-        first_s[pl.ds(high * (width + wide), width), data, :] = block[0:width]
-        cur_s[outer] = block[width : width + REACH]
-        two_s[outer, data, :] = block[width + REACH : width + 2 * REACH]
-        near_s[outer] = block[width + 2 * REACH : width + 3 * REACH]
+        first_s[pl.ds(high * (width + REACH) + REACH, REACH), data, :] = block[0:REACH]
+        cur_s[outer] = block[REACH : 2 * REACH]
+        two_s[outer, data, :] = block[2 * REACH : 3 * REACH]
+        near_s[outer] = block[3 * REACH : 4 * REACH]
         vel_s[pl.ds(high * 2 * short, short)] = model
-
-    put(one, model_one[...], 1 - odd)
+        up = high == 1
+        columns = unfold(block[4 * REACH :], receivers)
+        half = columns.shape[0] - REACH
+        deep = [jnp.where(up, columns[j : j + 1], columns[3 - j : 4 - j]) for j in range(REACH)]
+        factor = [
+            jnp.where(up, columns[REACH + m : REACH + m + 1], columns[REACH + half - 1 - m : REACH + half - m])
+            for m in range(half)
+        ]
+        beyond = [jnp.zeros((1, receivers), f32)] * REACH
+        for index, hop in enumerate(hops):
+            side = far_high if index == 0 else 1 - far_high
+            last = hop.shape[0] - 1
+            for u in range(REACH):
+                seen = jnp.where(up, hop[u : u + 1], hop[last - u : last - u + 1])
+                beyond[u] = jnp.where(side == high, seen, beyond[u])
+        src_depth = high * (src_layer - width) + (1 - high) * (-1 - src_layer)
+        for j in range(REACH):
+            source = jnp.where(src_depth == REACH + j, pulse_one, 0.0)
+            deep[j] = deep[j] + jnp.where(same_column, source, 0.0)
+            more = sum(STENCIL_WEIGHTS[4 + u - j] * beyond[u] for u in range(j + 1))
+            deep[j] = deep[j] + factor[(REACH + j) // 2] * more
+        return [
+            factor[depth // 2] * sum(STENCIL_WEIGHTS[4 + j - depth] * deep[j] for j in range(depth + 1))
+            for depth in range(REACH)
+        ]
+
+    gains_one = put(one, model_one[...], 1 - odd)
     inner = (place > 0) & (place < lax.axis_size("slab") - 1)
-    put(two, jnp.where(inner, model_two[...], 0.0), odd)
-    far_high = 1 - (place % 4) // 2
-    if n_far == 1:
-        hop_s[pl.ds((1 - far_high) * REACH, REACH)] = jnp.zeros((REACH, size_y, size_z), f32)
-    for index, block in enumerate(fars):
-        high = far_high if index == 0 else 1 - far_high
-        hop_s[pl.ds(high * REACH, REACH)] = block[0:REACH]
+    gains_two = put(two, jnp.where(inner, model_two[...], 0.0), odd)
     fill_courant(c2_s, vel_s[...], size_z)
 
     def crossing(sources, depth):
@@ -187,47 +269,38 @@
             factor = c2_s[fine : fine + size_y, :]
             ref[layer, data, :] = ref[layer, data, :] + factor * crossing(sources, depth)
 
-    cross(first_s, 0, 0, True, lambda j: hop_s[REACH - 1 - j])
     cross(first_s, wide, 0, False, lambda j: cur_s[REACH + j])
     cross(first_s, wide, 0, True, lambda j: cur_s[REACH - 1 - j])
     cross(first_s, wide + width, 0, False, lambda j: cur_s[REACH + width + j])
     cross(first_s, wide + width, 0, True, lambda j: cur_s[REACH + width - 1 - j])
-    cross(first_s, 2 * wide + width, 0, False, lambda j: hop_s[REACH + j])
     cross(two_s, REACH, REACH, False, lambda j: near_s[REACH + j])
     cross(two_s, REACH, REACH, True, lambda j: near_s[REACH - 1 - j])
     cross(two_s, REACH + width, REACH, False, lambda j: near_s[REACH + width + j])
     cross(two_s, REACH + width, REACH, True, lambda j: near_s[REACH + width - 1 - j])
 
-    plane = size_y * size_z
-    cell = src_cell[0]
-    now = src_step[0]
-    src_y = (cell % plane) // size_z
-    src_z = cell % size_z
-
-    def inject(ref, start, layers, offset, pulse):
-        layer = cell // plane - (place * width - start)
-        inside = (layer >= 0) & (layer < layers)
-        layer = jnp.clip(layer, 0, layers - 1)
-        value = jnp.where(inside, pulse, 0.0)
-        at = pl.ds(offset + src_y, 1)
-        ref[layer, at, :] = ref[layer, at, :] + jnp.where(lane == src_z, value, 0.0)
-
-    inject(first_s, wide, width + 2 * wide, 8, wavelet[now + 1])
+    inject(first_s.at[pl.ds(REACH, width + wide)], REACH, width + wide, 8, pulse_one)
     for ch in range(0, width + 2 * REACH, STEP):
         centre, total = laplace(first_s, ch + REACH, size_y, weights)
         factor = courant(c2_s, ch + REACH, STEP, size_y)
         sec_s[ch : ch + STEP] = 2.0 * centre - cur_s[ch : ch + STEP] + factor * total
-    inject(sec_s, REACH, width + 2 * REACH, 0, wavelet[now + 2])
+    inject(sec_s, REACH, width + wide, 0, pulse(2))
 
     region = (width + 2 * REACH) * size_y
-    cells = rec[...]
-    row = (cells - (place * width - REACH) * plane) // size_z
-    hot = row == lax.broadcasted_iota(jnp.int32, (region, cells.shape[1]), 0)
+    row = (rec[...] - (place * width - REACH) * plane) // size_z
+    hot = row == lax.broadcasted_iota(jnp.int32, (region, receivers), 0)
     hot = jnp.where(hot, 1.0, 0.0).astype(jnp.bfloat16)
-    lanes = lax.broadcasted_iota(jnp.int32, (size_z, cells.shape[1]), 0) == cells % size_z
+    lanes = lanes_in[...].astype(f32) > 0.5
     lo = REACH * size_y
     hi = lo + width * size_y
     own = (row >= lo) & (row < hi)
+    layer = row // size_y
+    gain = jnp.zeros((1, receivers), f32)
+    for depth in range(REACH):
+        low_layer = REACH - 1 - depth
+        high_layer = REACH + width + depth
+        one_side = layer == low_layer + (1 - odd) * (high_layer - low_layer)
+        two_side = layer == low_layer + odd * (high_layer - low_layer)
+        gain = jnp.where(one_side, gains_one[depth], jnp.where(two_side, gains_two[depth], gain))
 
     def read(field, marks):
         turned = field.T
@@ -241,7 +314,7 @@
 
     first_own = first_s[wide : wide + width, data, :].reshape(width * size_y, size_z)
     read_one = read(first_own, hot[lo:hi])
-    read_two = read(sec_s[...].reshape(region, size_z), hot)
+    read_two = read(sec_s[...].reshape(region, size_z), hot) + gain
     samples[0:1, :] = read_one
     samples[1:2, :] = jnp.where(own, read_two, 0.0)
     add_one = spread_out(read_one - obs[0:1, :], hot[lo:hi])
@@ -274,7 +347,7 @@
     if with_models:
         pay[rows : rows + short, :] = model_one[...]
         pay[rows + short : rows + 2 * short, :] = model_two[...]
-        pay[rows + 2 * short :, :] = fars[0][REACH:].reshape(short, size_z)
+        pay[rows + 2 * short :, :] = fars[0][1:].reshape(short, size_z)
 
 
 def mix_kernel(*refs, cells):
@@ -339,10 +412,10 @@
     half, coarse_y, coarse_z = model.shape
     rows = half * coarse_y
     short = rows // 2
-    near_layers = width + 3 * REACH
-    far_layers = REACH + short // size_y
+    near_layers = 4 * REACH + 1
+    far_layers = 1 + short // size_y
+    receivers = rec_cell.shape[0]
     in_vmem = pl.BlockSpec(memory_space=pltpu.VMEM)
-    in_smem = pl.BlockSpec(memory_space=pltpu.SMEM)
     padded = pltpu.VMEM((width + 2 * REACH, PITCH, size_z), f32)
     start = pl.pallas_call(
         start_kernel,
@@ -352,13 +425,20 @@
             pltpu.VMEM((far_layers, size_y, size_z), f32),
             pltpu.VMEM((short, size_z), f32),
             pltpu.VMEM((width, size_y, size_z), f32),
+            pltpu.VMEM((width, size_y, size_z), f32),
+            pltpu.VMEM((size_z, receivers), jnp.bfloat16),
+            pltpu.VMEM((1, receivers), jnp.int32),
+            pltpu.VMEM((1, wavelet.shape[0]), f32),
+            pltpu.VMEM((2, receivers), f32),
         ),
-        in_specs=[in_vmem] * 5,
-        out_specs=(in_vmem,) * 5,
+        in_specs=[in_vmem] * 8,
+        out_specs=(in_vmem,) * 10,
         scratch_shapes=[padded, padded, pltpu.VMEM((2 * rows, size_z), f32)],
         name="start_steps",
     )
-    to_one, to_two, to_far, packed, near_part = start(prev, cur, far, near, model)
+    to_one, to_two, to_far, packed, *kept, obs = start(
+        prev, cur, far, near, model, rec_cell[None], observed, wavelet[None]
+    )
     even = [(i, i + 1) for i in range(0, slabs - 1, 2)]
     model_one = swap(packed, "slab", even)
     one = swap(to_one, "slab", even)
@@ -371,12 +451,12 @@
         model_two = swap(packed, "slab", uneven)
         others = [(i, i + 2) for i in range(slabs - 2) if i % 4 >= 2]
         if others:
-            fars.append(swap(other_side(cur, to_far), "slab", others))
-    receivers = rec_cell.shape[0]
+            fars.append(swap(to_far, "slab", others))
     wide = 2 * REACH
     pay_rows = rows + 3 * short if fast else rows
+    own_part, near_part, *small = kept
     operands = (
-        prev, cur, near, model, rec_cell[None], observed, to_one, near_part, packed,
+        prev, cur, near, model, own_part, near_part, packed, *small, obs,
         one, two, model_one, model_two, *fars,
     )
     plain = pltpu.VMEM((width + 2 * REACH, size_y, size_z), f32)
@@ -386,12 +466,11 @@
             pltpu.VMEM((pay_rows, size_z), f32),
             pltpu.VMEM((2, receivers), f32),
         ),
-        in_specs=[in_smem] * 3 + [in_vmem] * len(operands),
+        in_specs=[pl.BlockSpec(memory_space=pltpu.SMEM)] * 2 + [in_vmem] * len(operands),
         out_specs=(in_vmem, in_vmem),
         scratch_shapes=[
             plain,
             plain,
-            pltpu.VMEM((2 * REACH, size_y, size_z), f32),
             pltpu.VMEM((width + 2 * wide, PITCH, size_z), f32),
             plain,
             padded,
@@ -400,7 +479,7 @@
             pltpu.VMEM((2 * rows, size_z), f32),
         ],
         name="wave_steps",
-    )(src_cell, src_step, wavelet, *[resident(block) for block in operands])
+    )(src_cell, src_step, *[resident(block) for block in operands])
     cells_coarse = rows * slabs * coarse_z
     if not fast:
         residual = lax.psum(samples, "slab") - observed
@@ -434,15 +513,8 @@
         in_specs=[in_vmem] * 11,
         out_specs=(in_vmem, in_vmem),
         name="mix_particles",
-    )(*[resident(blocks[i]) for i in range(count)], resident(part), resident(other), resident(observed))
+    )(*[resident(blocks[i]) for i in range(count)], resident(part), resident(other), resident(obs))
     return (update[None], residual[None])
-
-
-def other_side(cur, sent):
-    top = cur.shape[0] - REACH
-    low_first = (lax.axis_index("slab") % 4) // 2 == 0
-    outer = jnp.where(low_first, cur[:REACH], cur[top:])
-    return jnp.concatenate([outer, sent[REACH:]], axis=0)
 
 
 def solution(mesh):
@@ -459,6 +531,4 @@
         P(),
     )
     out_specs = (P("particle", "slab", None, None), P("particle", None, None))
-    return jax.shard_map(
-        device_step, mesh=mesh, in_specs=in_specs, out_specs=out_specs, check_vma=False
-    )
+    return jax.shard_map(device_step, mesh=mesh, in_specs=in_specs, out_specs=out_specs, check_vma=False)

time: 37.2 us -> 35.8 us (0.962)
  starting transfers between devices: 18.2 us -> 16.7 us
  waiting for transfers between devices: 11.4 us -> 12.4 us
  local copies, waits for them, and re-layouts: 0.65 us -> 0.02 us
    ppermute x14, starting transfers between devices: 18.2 us -> 16.7 us  [swap(): return lax.ppermute(block, axis, both)]
    ppermute x14, waiting for transfers between devices: 11.4 us -> 12.4 us  [swap(): return lax.ppermute(block, axis, both)]
    unnamed x12 -> x8, local copies, waits for them, and re-layouts: 0.65 us -> 0.02 us
    pallas_call x1, Pallas kernels: 2.41 us -> 1.79 us  [device_step(): pl.pallas_call(lambda *refs: wave_kernel(*refs, n_far=len(fars), with_mod...]
where the time goes in v4:
time: 35.8 us; the launch traced here: 35.6 us
  starting transfers between devices  16.7 us (47%)
  waiting for transfers between devices  12.4 us (35%)
  Pallas kernels  4.36 us (12%)
  between operations  2.04 us (6%)
    ppermute x14, starting transfers between devices, swap(): return lax.ppermute(block, axis, both)  16.7 us
    ppermute x14, waiting for transfers between devices, swap(): return lax.ppermute(block, axis, both)  12.4 us
    pallas_call x1, Pallas kernels, device_step(): pl.pallas_call(lambda *refs: wave_kernel(*refs, n_far=len(fars), with_mod...  1.79 us
    pallas_call x1, Pallas kernels, device_step(): start(prev, cur, far, near, model, rec_cell[None], observed, wavelet[None])  1.69 us
    pallas_call x1, Pallas kernels, device_step(): pl.pallas_call(lambda *refs: mix_kernel(*refs, cells=cells_coarse), out_s...  0.88 us
  transfers between devices with their start and end apart: 14, of which 7 were waited for; matrix products, arithmetic and copies ran while one was open for 0% of the time, Pallas kernels for 0%

profile of v4, /device:TPU:0, one launch (start us, length us, event | category | flops | bytes accessed | tf_op | source)
XLA Modules:
  0.0 35.6 jit_solution(4154152143386735370)
XLA Ops:
  0.7 1.7 %start_steps.1 = (f32[17,16,128]{2,1,0:T(8,128)S(1)}, f32[17,16,128]{2,1,0:T(8,128)S(1)}, f32[2,16,128]{2,1,0:T(8,128)S(1)}, f32[16,128]{1,0:T(8,128)S(1)}, f32[...) custom-call(f32[8,16,128]{2,1,0:T(8,128)} %bitcast.9, ...), custom_call_target="tpu_custom_call" | custom-call | tf_op jit(solution)/shard_map/start_steps/pallas_call | solution.py:439
  2.4 0.0 copy-start.3
  2.4 3.1 %collective-permute-start = (f32[17,16,128]{2,1,0:T(8,128)S(1)}, f32[17,16,128]{2,1,0:T(8,128)S(1)}, u32[]{:S(2)}, u32[]{:S(2)}) collective-permute-start(f32[17,16,128]{2,1,0:T(8,128)S(1)} %get-tuple-element.23), channel_id=1, source_target_pairs={{0,1},{2,3},{1,0},{3,2},{4,5},{6,7},{5,4},{7,6},{8,9},{10,11},{9,8... | collective-permute-start | bytes 417800 | tf_op jit(solution)/shard_map/ppermute | solution.py:27
  5.5 0.7 %collective-permute-start.1 = (f32[17,16,128]{2,1,0:T(8,128)S(1)}, f32[17,16,128]{2,1,0:T(8,128)S(1)}, u32[]{:S(2)}, u32[]{:S(2)}) collective-permute-start(f32[17,16,128]{2,1,0:T(8,128)S(1)} %get-tuple-element.24), channel_id=1, source_target_pairs={{1,2},{2,1},{5,6},{6,5},{9,10},{10,9},{13,14},{14,13},{17,18},{18,... | collective-permute-start | bytes 417800 | tf_op jit(solution)/shard_map/ppermute | solution.py:27
  6.2 4.5 %collective-permute-start.2 = (f32[16,128]{1,0:T(8,128)S(1)}, f32[16,128]{1,0:T(8,128)S(1)}, u32[]{:S(2)}, u32[]{:S(2)}) collective-permute-start(f32[16,128]{1,0:T(8,128)S(1)} %get-tuple-element.18.refs_8_), channel_id=1, source_target_pairs={{0,1},{2,3},{1,0},{3,2},{4,5},{6,7},{5,4},{7,6},{8,9},{10,11},{9,8... | collective-permute-start | bytes 24584 | tf_op jit(solution)/shard_map/ppermute | solution.py:27
  10.6 0.0 collective-permute-start.4
  10.6 1.6 %collective-permute-done.2.refs_15_ = f32[16,128]{1,0:T(8,128)S(1)} collective-permute-done((f32[16,128]{1,0:T(8,128)S(1)}, f32[16,128]{1,0:T(8,128)S(1)}, u32[]{:S(2)}, u32[]{:S(2)}) %collective-permute-start.2) | collective-permute-done | bytes 8224 | tf_op jit(solution)/shard_map/ppermute | solution.py:27
  12.2 1.5 %collective-permute-start.3 = (f32[16,128]{1,0:T(8,128)S(1)}, f32[16,128]{1,0:T(8,128)S(1)}, u32[]{:S(2)}, u32[]{:S(2)}) collective-permute-start(f32[16,128]{1,0:T(8,128)S(1)} %collective-permute-done.2.refs_15_), channel_id=1, source_target_pairs={{0,2},{1,3},{2,0},{3,1},{4,6},{5,7},{6,4},{7,5},{8,10},{9,11},{10,... | collective-permute-start | bytes 24584 | tf_op jit(solution)/shard_map/ppermute | solution.py:27
  15.0 1.8 %collective-permute-done.3.refs_16_ = f32[16,128]{1,0:T(8,128)S(1)} collective-permute-done((f32[16,128]{1,0:T(8,128)S(1)}, f32[16,128]{1,0:T(8,128)S(1)}, u32[]{:S(2)}, u32[]{:S(2)}) %collective-permute-start.3) | collective-permute-done | bytes 8224 | tf_op jit(solution)/shard_map/ppermute | solution.py:27
  16.8 0.0 collective-permute-done.4.refs_17_
  16.8 0.0 collective-permute-done.refs_13_
  16.8 0.0 collective-permute-done.1.refs_14_
  16.8 1.8 %wave_steps.1 = (f32[80,128]{1,0:T(8,128)S(1)}, f32[2,256]{1,0:T(2,128)S(1)}) custom-call(s32[1]{0:T(128)S(6)} %copy.12.refs_0_, s32[1]{0:T(128)S(6)} %copy.13.refs_1_, f32[8,16,128]{2,1,0:T(8,128)S(1)} %bitcast.10, f32[8,16,128]{2,1,0:T(8,128)S(1)} %bitcast.12, f32[8,16,128]{2,1,0:T(8,128)S(1)} %bitcast.14, f32[4,8,64]{2,1,0:T(8,128)S(1)} %bitcast.16, ...), custom_call_target="tpu_custom_call" | custom-call | tf_op jit(solution)/shard_map/wave_steps/pallas_call | solution.py:463
  18.6 1.5 %collective-permute-start.6 = (f32[80,128]{1,0:T(8,128)S(1)}, f32[80,128]{1,0:T(8,128)S(1)}, u32[]{:S(2)}, u32[]{:S(2)}) collective-permute-start(f32[80,128]{1,0:T(8,128)S(1)} %get-tuple-element.26.refs_0_), channel_id=1, source_target_pairs={{0,8},{4,12},{16,24},{20,28},{8,0},{12,4},{24,16},{28,20},{1,9},{5... | collective-permute-start | bytes 122888 | tf_op jit(solution)/shard_map/ppermute | solution.py:27
  20.2 1.5 %collective-permute-start.8 = (f32[80,128]{1,0:T(8,128)S(1)}, f32[80,128]{1,0:T(8,128)S(1)}, u32[]{:S(2)}, u32[]{:S(2)}) collective-permute-start(f32[80,128]{1,0:T(8,128)S(1)} %get-tuple-element.26.refs_0_), channel_id=1, source_target_pairs={{0,16},{4,20},{8,24},{12,28},{16,0},{20,4},{24,8},{28,12},{1,17},{... | collective-permute-start | bytes 122888 | tf_op jit(solution)/shard_map/ppermute | solution.py:27
  21.7 0.5 %collective-permute-start.10 = (f32[80,128]{1,0:T(8,128)S(1)}, f32[80,128]{1,0:T(8,128)S(1)}, u32[]{:S(2)}, u32[]{:S(2)}) collective-permute-start(f32[80,128]{1,0:T(8,128)S(1)} %get-tuple-element.26.refs_0_), channel_id=1, source_target_pairs={{0,24},{4,28},{8,16},{12,20},{24,0},{28,4},{16,8},{20,12},{1,25},{... | collective-permute-start | bytes 122888 | tf_op jit(solution)/shard_map/ppermute | solution.py:27
  22.2 0.5 %collective-permute-done.6.refs_2_ = f32[80,128]{1,0:T(8,128)S(1)} collective-permute-done((f32[80,128]{1,0:T(8,128)S(1)}, f32[80,128]{1,0:T(8,128)S(1)}, u32[]{:S(2)}, u32[]{:S(2)}) %collective-permute-start.6) | collective-permute-done | bytes 40992 | tf_op jit(solution)/shard_map/ppermute | solution.py:27
  22.7 1.5 %collective-permute-done.8.refs_4_ = f32[80,128]{1,0:T(8,128)S(1)} collective-permute-done((f32[80,128]{1,0:T(8,128)S(1)}, f32[80,128]{1,0:T(8,128)S(1)}, u32[]{:S(2)}, u32[]{:S(2)}) %collective-permute-start.8) | collective-permute-done | bytes 40992 | tf_op jit(solution)/shard_map/ppermute | solution.py:27
  24.2 2.4 %collective-permute-done.10.refs_6_ = f32[80,128]{1,0:T(8,128)S(1)} collective-permute-done((f32[80,128]{1,0:T(8,128)S(1)}, f32[80,128]{1,0:T(8,128)S(1)}, u32[]{:S(2)}, u32[]{:S(2)}) %collective-permute-start.10) | collective-permute-done | bytes 40992 | tf_op jit(solution)/shard_map/ppermute | solution.py:27
  26.6 2.0 %collective-permute-start.12 = (f32[2,256]{1,0:T(2,128)S(1)}, f32[2,256]{1,0:T(2,128)S(1)}, u32[]{:S(2)}, u32[]{:S(2)}) collective-permute-start(f32[2,256]{1,0:T(2,128)S(1)} %get-tuple-element.27), channel_id=1, source_target_pairs={{0,1},{2,3},{1,0},{3,2},{4,5},{6,7},{5,4},{7,6},{8,9},{10,11},{9,8... | collective-permute-start | bytes 6152 | tf_op jit(solution)/shard_map/ppermute | solution.py:27
  28.6 1.6 %collective-permute-done.12 = f32[2,256]{1,0:T(2,128)S(1)} collective-permute-done((f32[2,256]{1,0:T(2,128)S(1)}, f32[2,256]{1,0:T(2,128)S(1)}, u32[]{:S(2)}, u32[]{:S(2)}) %collective-permute-start.12) | collective-permute-done | bytes 2080 | tf_op jit(solution)/shard_map/ppermute | solution.py:27
  30.2 1.5 %collective-permute-start.13 = (f32[2,256]{1,0:T(2,128)S(1)}, f32[2,256]{1,0:T(2,128)S(1)}, u32[]{:S(2)}, u32[]{:S(2)}) collective-permute-start(f32[2,256]{1,0:T(2,128)S(1)} %add.3.refs_8_), channel_id=1, source_target_pairs={{0,2},{1,3},{2,0},{3,1},{4,6},{5,7},{6,4},{7,5},{8,10},{9,11},{10,... | collective-permute-start | bytes 6152 | tf_op jit(solution)/shard_map/ppermute | solution.py:27
  31.7 3.0 %collective-permute-done.13.refs_9_ = f32[2,256]{1,0:T(2,128)S(1)} collective-permute-done((f32[2,256]{1,0:T(2,128)S(1)}, f32[2,256]{1,0:T(2,128)S(1)}, u32[]{:S(2)}, u32[]{:S(2)}) %collective-permute-start.13) | collective-permute-done | bytes 2080 | tf_op jit(solution)/shard_map/ppermute | solution.py:27
  34.7 0.9 %mix_particles.1 = (f32[4,8,64]{2,1,0:T(8,128)}, f32[2,256]{1,0:T(2,128)}) custom-call(f32[80,128]{1,0:T(8,128)S(1)} %get-tuple-element.26.refs_0_, f32[80,128]{1,0:T(8,128)S(1)} %collective-permute-done.5.refs_1_, f32[80,128]{1,0:T(8,128)S(1)} %collective-permute-done.6.refs_2_, f32[80,128]{1,0:T(8,128)S(1)} %collective-permute-done.7.refs_3_, ...), custom_call_target="tpu_custom_call" | custom-call | tf_op jit(solution)/shard_map/mix_particles/pallas_call | solution.py:507
  (16 shorter events, 0.0 us)
Async XLA Ops:
  0.6 16.2 %copy-start = (f32[1,8,16,128]{3,2,1,0:T(8,128)S(1)}, f32[1,8,16,128]{3,2,1,0:T(8,128)}, u32[]{:S(2)}) copy-start(f32[1,8,16,128]{3,2,1,0:T(8,128)} %param.11) | copy-start | bytes 196612
  0.6 16.2 %copy-start.1 = (f32[1,8,16,128]{3,2,1,0:T(8,128)S(1)}, f32[1,8,16,128]{3,2,1,0:T(8,128)}, u32[]{:S(2)}) copy-start(f32[1,8,16,128]{3,2,1,0:T(8,128)} %param.12) | copy-start | bytes 196612
  0.7 16.2 %copy-start.2 = (f32[1,8,16,128]{3,2,1,0:T(8,128)S(1)}, f32[1,8,16,128]{3,2,1,0:T(8,128)}, u32[]{:S(2)}) copy-start(f32[1,8,16,128]{3,2,1,0:T(8,128)} %param.14) | copy-start | bytes 196612
  2.4 14.5 %copy-start.3 = (f32[1,4,8,64]{3,2,1,0:T(8,128)S(1)}, f32[1,4,8,64]{3,2,1,0:T(8,128)}, u32[]{:S(2)}) copy-start(f32[1,4,8,64]{3,2,1,0:T(8,128)} %param.10) | copy-start | bytes 24580
  2.4 14.4 %collective-permute-start = (f32[17,16,128]{2,1,0:T(8,128)S(1)}, f32[17,16,128]{2,1,0:T(8,128)S(1)}, u32[]{:S(2)}, u32[]{:S(2)}) collective-permute-start(f32[17,16,128]{2,1,0:T(8,128)S(1)} %get-tuple-element.23), channel_id=1, source_target_pairs={{0,1},{2,3},{1,0},{3,2},{4,5},{6,7},{5,4},{7,6},{8,9},{10,11},{9,8... | collective-permute-start | bytes 417800 | tf_op jit(solution)/shard_map/ppermute | solution.py:27
  5.5 11.3 %collective-permute-start.1 = (f32[17,16,128]{2,1,0:T(8,128)S(1)}, f32[17,16,128]{2,1,0:T(8,128)S(1)}, u32[]{:S(2)}, u32[]{:S(2)}) collective-permute-start(f32[17,16,128]{2,1,0:T(8,128)S(1)} %get-tuple-element.24), channel_id=1, source_target_pairs={{1,2},{2,1},{5,6},{6,5},{9,10},{10,9},{13,14},{14,13},{17,18},{18,... | collective-permute-start | bytes 417800 | tf_op jit(solution)/shard_map/ppermute | solution.py:27
  6.2 6.1 %collective-permute-start.2 = (f32[16,128]{1,0:T(8,128)S(1)}, f32[16,128]{1,0:T(8,128)S(1)}, u32[]{:S(2)}, u32[]{:S(2)}) collective-permute-start(f32[16,128]{1,0:T(8,128)S(1)} %get-tuple-element.18.refs_8_), channel_id=1, source_target_pairs={{0,1},{2,3},{1,0},{3,2},{4,5},{6,7},{5,4},{7,6},{8,9},{10,11},{9,8... | collective-permute-start | bytes 24584 | tf_op jit(solution)/shard_map/ppermute | solution.py:27
  10.6 6.2 %collective-permute-start.4 = (f32[2,16,128]{2,1,0:T(8,128)S(1)}, f32[2,16,128]{2,1,0:T(8,128)S(1)}, u32[]{:S(2)}, u32[]{:S(2)}) collective-permute-start(f32[2,16,128]{2,1,0:T(8,128)S(1)} %get-tuple-element.25), channel_id=1, source_target_pairs={{0,2},{1,3},{2,0},{3,1},{4,6},{5,7},{6,4},{7,5},{8,10},{9,11},{10,... | collective-permute-start | bytes 49160 | tf_op jit(solution)/shard_map/ppermute | solution.py:27
  12.2 4.5 %collective-permute-start.3 = (f32[16,128]{1,0:T(8,128)S(1)}, f32[16,128]{1,0:T(8,128)S(1)}, u32[]{:S(2)}, u32[]{:S(2)}) collective-permute-start(f32[16,128]{1,0:T(8,128)S(1)} %collective-permute-done.2.refs_15_), channel_id=1, source_target_pairs={{0,2},{1,3},{2,0},{3,1},{4,6},{5,7},{6,4},{7,5},{8,10},{9,11},{10,... | collective-permute-start | bytes 24584 | tf_op jit(solution)/shard_map/ppermute | solution.py:27
  18.6 4.0 %collective-permute-start.6 = (f32[80,128]{1,0:T(8,128)S(1)}, f32[80,128]{1,0:T(8,128)S(1)}, u32[]{:S(2)}, u32[]{:S(2)}) collective-permute-start(f32[80,128]{1,0:T(8,128)S(1)} %get-tuple-element.26.refs_0_), channel_id=1, source_target_pairs={{0,8},{4,12},{16,24},{20,28},{8,0},{12,4},{24,16},{28,20},{1,9},{5... | collective-permute-start | bytes 122888 | tf_op jit(solution)/shard_map/ppermute | solution.py:27
  20.2 4.0 %collective-permute-start.8 = (f32[80,128]{1,0:T(8,128)S(1)}, f32[80,128]{1,0:T(8,128)S(1)}, u32[]{:S(2)}, u32[]{:S(2)}) collective-permute-start(f32[80,128]{1,0:T(8,128)S(1)} %get-tuple-element.26.refs_0_), channel_id=1, source_target_pairs={{0,16},{4,20},{8,24},{12,28},{16,0},{20,4},{24,8},{28,12},{1,17},{... | collective-permute-start | bytes 122888 | tf_op jit(solution)/shard_map/ppermute | solution.py:27
  21.7 4.9 %collective-permute-start.10 = (f32[80,128]{1,0:T(8,128)S(1)}, f32[80,128]{1,0:T(8,128)S(1)}, u32[]{:S(2)}, u32[]{:S(2)}) collective-permute-start(f32[80,128]{1,0:T(8,128)S(1)} %get-tuple-element.26.refs_0_), channel_id=1, source_target_pairs={{0,24},{4,28},{8,16},{12,20},{24,0},{28,4},{16,8},{20,12},{1,25},{... | collective-permute-start | bytes 122888 | tf_op jit(solution)/shard_map/ppermute | solution.py:27
  22.2 12.5 %collective-permute-start.5 = (f32[80,128]{1,0:T(8,128)S(1)}, f32[80,128]{1,0:T(8,128)S(1)}, u32[]{:S(2)}, u32[]{:S(2)}) collective-permute-start(f32[80,128]{1,0:T(8,128)S(1)} %get-tuple-element.26.refs_0_), channel_id=1, source_target_pairs={{0,4},{8,12},{16,20},{24,28},{4,0},{12,8},{20,16},{28,24},{1,5},{9... | collective-permute-start | bytes 122888 | tf_op jit(solution)/shard_map/ppermute | solution.py:27
  22.7 12.0 %collective-permute-start.7 = (f32[80,128]{1,0:T(8,128)S(1)}, f32[80,128]{1,0:T(8,128)S(1)}, u32[]{:S(2)}, u32[]{:S(2)}) collective-permute-start(f32[80,128]{1,0:T(8,128)S(1)} %collective-permute-done.6.refs_2_), channel_id=1, source_target_pairs={{0,4},{8,12},{16,20},{24,28},{4,0},{12,8},{20,16},{28,24},{1,5},{9... | collective-permute-start | bytes 122888 | tf_op jit(solution)/shard_map/ppermute | solution.py:27
  24.2 10.5 %collective-permute-start.9 = (f32[80,128]{1,0:T(8,128)S(1)}, f32[80,128]{1,0:T(8,128)S(1)}, u32[]{:S(2)}, u32[]{:S(2)}) collective-permute-start(f32[80,128]{1,0:T(8,128)S(1)} %collective-permute-done.8.refs_4_), channel_id=1, source_target_pairs={{0,4},{8,12},{16,20},{24,28},{4,0},{12,8},{20,16},{28,24},{1,5},{9... | collective-permute-start | bytes 122888 | tf_op jit(solution)/shard_map/ppermute | solution.py:27
  26.6 8.1 %collective-permute-start.11 = (f32[80,128]{1,0:T(8,128)S(1)}, f32[80,128]{1,0:T(8,128)S(1)}, u32[]{:S(2)}, u32[]{:S(2)}) collective-permute-start(f32[80,128]{1,0:T(8,128)S(1)} %collective-permute-done.10.refs_6_), channel_id=1, source_target_pairs={{0,4},{8,12},{16,20},{24,28},{4,0},{12,8},{20,16},{28,24},{1,5},{9... | collective-permute-start | bytes 122888 | tf_op jit(solution)/shard_map/ppermute | solution.py:27
  26.6 3.6 %collective-permute-start.12 = (f32[2,256]{1,0:T(2,128)S(1)}, f32[2,256]{1,0:T(2,128)S(1)}, u32[]{:S(2)}, u32[]{:S(2)}) collective-permute-start(f32[2,256]{1,0:T(2,128)S(1)} %get-tuple-element.27), channel_id=1, source_target_pairs={{0,1},{2,3},{1,0},{3,2},{4,5},{6,7},{5,4},{7,6},{8,9},{10,11},{9,8... | collective-permute-start | bytes 6152 | tf_op jit(solution)/shard_map/ppermute | solution.py:27
  30.2 4.5 %collective-permute-start.13 = (f32[2,256]{1,0:T(2,128)S(1)}, f32[2,256]{1,0:T(2,128)S(1)}, u32[]{:S(2)}, u32[]{:S(2)}) collective-permute-start(f32[2,256]{1,0:T(2,128)S(1)} %add.3.refs_8_), channel_id=1, source_target_pairs={{0,2},{1,3},{2,0},{3,1},{4,6},{5,7},{6,4},{7,5},{8,10},{9,11},{10,... | collective-permute-start | bytes 6152 | tf_op jit(solution)/shard_map/ppermute | solution.py:27

commit v5 on v4

--- a/solution.py
+++ b/solution.py
@@ -12,6 +12,16 @@
 STEP = 4
 PITCH = 32
 HIGHEST = lax.Precision.HIGHEST
+
+
+def swap_uneven(block, slabs, count):
+    pairs = []
+    for particle in range(count):
+        base = particle * slabs
+        pairs += [(base + i, base + i + 1) for i in range(1, slabs - 1, 2)]
+        if particle % 2 == 0:
+            pairs += [(base, base + slabs), (base + slabs - 1, base + 2 * slabs - 1)]
+    return swap(block, ("particle", "slab"), pairs)
 
 
 def resident(block):
@@ -156,6 +166,11 @@
     to_far[1:] = packed[...].reshape(to_far.shape[0] - 1, size_y, size_z)
 
 
+def join_kernel(first, second, out):
+    out[0 : first.shape[0]] = first[...]
+    out[first.shape[0] :] = second[...].reshape(-1, out.shape[1], out.shape[2])
+
+
 def fold(block, size_y, size_z):
     pieces = [block[:, at : at + size_z] for at in range(0, block.shape[1], size_z)]
     return jnp.concatenate(pieces, axis=0).reshape(-1, size_y, size_z)
@@ -169,8 +184,10 @@
 
 def wave_kernel(
     src_cell, src_step, prev, cur, near, vel, own_part, near_part, packed, lanes_in, rec, wavelet, obs,
-    one, two, model_one, model_two, *rest, n_far, with_models
+    one, two, model_one, *rest, n_far, with_models
 ):
+    if not with_models:
+        model_two, rest = rest[0], rest[1:]
     fars = rest[:n_far]
     pay, samples = rest[n_far : n_far + 2]
     cur_s, near_s, first_s, sec_s, two_s, vel_s, c2_s, img_s = rest[n_far + 2 :]
@@ -254,7 +271,9 @@
 
     gains_one = put(one, model_one[...], 1 - odd)
     inner = (place > 0) & (place < lax.axis_size("slab") - 1)
-    gains_two = put(two, jnp.where(inner, model_two[...], 0.0), odd)
+    if with_models:
+        model_two = fars[0][2:].reshape(short, size_z)
+    gains_two = put(jnp.where(inner, two[...], 0.0), jnp.where(inner, model_two[...], 0.0), odd)
     fill_courant(c2_s, vel_s[...], size_z)
 
     def crossing(sources, depth):
@@ -346,8 +365,7 @@
     pay[0:rows, :] = jnp.where(lane < size_z // 2, factor * blocks, own_vel)
     if with_models:
         pay[rows : rows + short, :] = model_one[...]
-        pay[rows + short : rows + 2 * short, :] = model_two[...]
-        pay[rows + 2 * short :, :] = fars[0][1:].reshape(short, size_z)
+        pay[rows + short :, :] = fars[0][1:].reshape(2 * short, size_z)
 
 
 def mix_kernel(*refs, cells):
@@ -442,13 +460,19 @@
     even = [(i, i + 1) for i in range(0, slabs - 1, 2)]
     model_one = swap(packed, "slab", even)
     one = swap(to_one, "slab", even)
-    uneven = [(i, i + 1) for i in range(1, slabs - 1, 2)]
-    two = swap(to_two, "slab", uneven)
+    two = swap_uneven(to_two, slabs, count)
+    if fast:
+        to_far = pl.pallas_call(
+            join_kernel,
+            out_shape=pltpu.VMEM((far_layers + short // size_y, size_y, size_z), f32),
+            in_specs=[in_vmem] * 2,
+            out_specs=in_vmem,
+            name="join_messages",
+        )(resident(to_far), resident(model_one))
     fars = [swap(to_far, "slab", [(i, i + 2) for i in range(slabs - 2) if i % 4 < 2])]
-    if fast:
-        model_two = swap(model_one, "slab", [(0, 2), (1, 3)])
-    else:
-        model_two = swap(packed, "slab", uneven)
+    models = [model_one]
+    if not fast:
+        models.append(swap_uneven(packed, slabs, count))
         others = [(i, i + 2) for i in range(slabs - 2) if i % 4 >= 2]
         if others:
             fars.append(swap(to_far, "slab", others))
@@ -457,7 +481,7 @@
     own_part, near_part, *small = kept
     operands = (
         prev, cur, near, model, own_part, near_part, packed, *small, obs,
-        one, two, model_one, model_two, *fars,
+        one, two, *models, *fars,
     )
     plain = pltpu.VMEM((width + 2 * REACH, size_y, size_z), f32)
     pay, samples = pl.pallas_call(
@@ -531,4 +555,6 @@
         P(),
     )
     out_specs = (P("particle", "slab", None, None), P("particle", None, None))
-    return jax.shard_map(device_step, mesh=mesh, in_specs=in_specs, out_specs=out_specs, check_vma=False)
+    return jax.shard_map(
+        device_step, mesh=mesh, in_specs=in_specs, out_specs=out_specs, check_vma=False
+    )

time: 35.8 us -> 33.9 us (0.947)
  starting transfers between devices: 16.7 us -> 15.5 us
  waiting for transfers between devices: 12.4 us -> 11.9 us
    ppermute x14 -> x13, starting transfers between devices: 16.7 us -> 15.5 us  [swap(): return lax.ppermute(block, axis, both)]
    ppermute x14 -> x13, waiting for transfers between devices: 12.4 us -> 11.9 us  [swap(): return lax.ppermute(block, axis, both)]
  transfers between devices with their start and end apart: 14 -> 13, of which waited for: 7 -> 7; matrix products, arithmetic and copies ran while one was open for 0% -> 0% of each run, Pallas kernels for 0% -> 0%
where the time goes in v5:
time: 33.9 us; the launch traced here: 33.7 us
  starting transfers between devices  15.5 us (46%)
  waiting for transfers between devices  11.9 us (35%)
  Pallas kernels  4.34 us (13%)
  between operations  2.02 us (6%)
    ppermute x13, starting transfers between devices, swap(): return lax.ppermute(block, axis, both)  15.5 us
    ppermute x13, waiting for transfers between devices, swap(): return lax.ppermute(block, axis, both)  11.9 us
    pallas_call x1, Pallas kernels, device_step(): pl.pallas_call(lambda *refs: wave_kernel(*refs, n_far=len(fars), with_mod...  1.78 us
    pallas_call x1, Pallas kernels, device_step(): start(prev, cur, far, near, model, rec_cell[None], observed, wavelet[None])  1.67 us
    pallas_call x1, Pallas kernels, device_step(): pl.pallas_call(lambda *refs: mix_kernel(*refs, cells=cells_coarse), out_s...  0.88 us
  transfers between devices with their start and end apart: 13, of which 7 were waited for; matrix products, arithmetic and copies ran while one was open for 0% of the time, Pallas kernels for 0%

profile of v5, /device:TPU:0, one launch (start us, length us, event | category | flops | bytes accessed | tf_op | source)
XLA Modules:
  0.0 33.7 jit_solution(11792061650683298470)
XLA Ops:
  0.7 1.7 %start_steps.1 = (f32[17,16,128]{2,1,0:T(8,128)S(1)}, f32[17,16,128]{2,1,0:T(8,128)S(1)}, f32[2,16,128]{2,1,0:T(8,128)S(1)}, f32[16,128]{1,0:T(8,128)S(1)}, f32[...) custom-call(f32[8,16,128]{2,1,0:T(8,128)} %bitcast.9, ...), custom_call_target="tpu_custom_call" | custom-call | tf_op jit(solution)/shard_map/start_steps/pallas_call | solution.py:457
  2.3 0.0 copy-start
  2.4 3.1 %collective-permute-start = (f32[17,16,128]{2,1,0:T(8,128)S(1)}, f32[17,16,128]{2,1,0:T(8,128)S(1)}, u32[]{:S(2)}, u32[]{:S(2)}) collective-permute-start(f32[17,16,128]{2,1,0:T(8,128)S(1)} %get-tuple-element.23), channel_id=1, source_target_pairs={{0,1},{2,3},{1,0},{3,2},{4,5},{6,7},{5,4},{7,6},{8,9},{10,11},{9,8... | collective-permute-start | bytes 417800 | tf_op jit(solution)/shard_map/ppermute | solution.py:37
  5.5 0.0 collective-permute-start.1
  5.5 3.1 %collective-permute-start.2 = (f32[16,128]{1,0:T(8,128)S(1)}, f32[16,128]{1,0:T(8,128)S(1)}, u32[]{:S(2)}, u32[]{:S(2)}) collective-permute-start(f32[16,128]{1,0:T(8,128)S(1)} %get-tuple-element.18.refs_8_), channel_id=1, source_target_pairs={{0,1},{2,3},{1,0},{3,2},{4,5},{6,7},{5,4},{7,6},{8,9},{10,11},{9,8... | collective-permute-start | bytes 24584 | tf_op jit(solution)/shard_map/ppermute | solution.py:37
  8.6 1.6 %collective-permute-done.2.second.refs_15_ = f32[16,128]{1,0:T(8,128)S(1)} collective-permute-done((f32[16,128]{1,0:T(8,128)S(1)}, f32[16,128]{1,0:T(8,128)S(1)}, u32[]{:S(2)}, u32[]{:S(2)}) %collective-permute-start.2) | collective-permute-done | bytes 8224 | tf_op jit(solution)/shard_map/ppermute | solution.py:37
  10.3 1.8 %collective-permute-start.3 = (f32[3,16,128]{2,1,0:T(8,128)S(1)}, f32[3,16,128]{2,1,0:T(8,128)S(1)}, u32[]{:S(2)}, u32[]{:S(2)}) collective-permute-start(f32[3,16,128]{2,1,0:T(8,128)S(1)} %join_messages.1), channel_id=1, source_target_pairs={{0,2},{1,3},{2,0},{3,1},{4,6},{5,7},{6,4},{7,5},{8,10},{9,11},{10,... | collective-permute-start | bytes 73736 | tf_op jit(solution)/shard_map/ppermute | solution.py:37
  13.4 1.6 %collective-permute-done.3.refs_16_ = f32[3,16,128]{2,1,0:T(8,128)S(1)} collective-permute-done((f32[3,16,128]{2,1,0:T(8,128)S(1)}, f32[3,16,128]{2,1,0:T(8,128)S(1)}, u32[]{:S(2)}, u32[]{:S(2)}) %collective-permute-start.3) | collective-permute-done | bytes 24608 | tf_op jit(solution)/shard_map/ppermute | solution.py:37
  15.0 0.0 collective-permute-done.refs_13_
  15.0 0.0 collective-permute-done.1.refs_14_
  15.0 1.8 %wave_steps.1 = (f32[80,128]{1,0:T(8,128)S(1)}, f32[2,256]{1,0:T(2,128)S(1)}) custom-call(s32[1]{0:T(128)S(6)} %copy.12.refs_0_, s32[1]{0:T(128)S(6)} %copy.13.refs_1_, f32[8,16,128]{2,1,0:T(8,128)S(1)} %bitcast.10, f32[8,16,128]{2,1,0:T(8,128)S(1)} %bitcast.12, f32[8,16,128]{2,1,0:T(8,128)S(1)} %bitcast.14, f32[4,8,64]{2,1,0:T(8,128)S(1)} %bitcast.16, ...), custom_call_target="tpu_custom_call" | custom-call | tf_op jit(solution)/shard_map/wave_steps/pallas_call | solution.py:487
  16.8 1.5 %collective-permute-start.5 = (f32[80,128]{1,0:T(8,128)S(1)}, f32[80,128]{1,0:T(8,128)S(1)}, u32[]{:S(2)}, u32[]{:S(2)}) collective-permute-start(f32[80,128]{1,0:T(8,128)S(1)} %get-tuple-element.26.refs_0_), channel_id=1, source_target_pairs={{0,8},{4,12},{16,24},{20,28},{8,0},{12,4},{24,16},{28,20},{1,9},{5... | collective-permute-start | bytes 122888 | tf_op jit(solution)/shard_map/ppermute | solution.py:37
  18.3 1.5 %collective-permute-start.7 = (f32[80,128]{1,0:T(8,128)S(1)}, f32[80,128]{1,0:T(8,128)S(1)}, u32[]{:S(2)}, u32[]{:S(2)}) collective-permute-start(f32[80,128]{1,0:T(8,128)S(1)} %get-tuple-element.26.refs_0_), channel_id=1, source_target_pairs={{0,16},{4,20},{8,24},{12,28},{16,0},{20,4},{24,8},{28,12},{1,17},{... | collective-permute-start | bytes 122888 | tf_op jit(solution)/shard_map/ppermute | solution.py:37
  19.9 0.5 %collective-permute-start.9 = (f32[80,128]{1,0:T(8,128)S(1)}, f32[80,128]{1,0:T(8,128)S(1)}, u32[]{:S(2)}, u32[]{:S(2)}) collective-permute-start(f32[80,128]{1,0:T(8,128)S(1)} %get-tuple-element.26.refs_0_), channel_id=1, source_target_pairs={{0,24},{4,28},{8,16},{12,20},{24,0},{28,4},{16,8},{20,12},{1,25},{... | collective-permute-start | bytes 122888 | tf_op jit(solution)/shard_map/ppermute | solution.py:37
  20.3 0.0 collective-permute-start.4
  20.3 0.5 %collective-permute-done.5.refs_2_ = f32[80,128]{1,0:T(8,128)S(1)} collective-permute-done((f32[80,128]{1,0:T(8,128)S(1)}, f32[80,128]{1,0:T(8,128)S(1)}, u32[]{:S(2)}, u32[]{:S(2)}) %collective-permute-start.5) | collective-permute-done | bytes 40992 | tf_op jit(solution)/shard_map/ppermute | solution.py:37
  20.8 0.0 collective-permute-start.6
  20.9 1.5 %collective-permute-done.7.refs_4_ = f32[80,128]{1,0:T(8,128)S(1)} collective-permute-done((f32[80,128]{1,0:T(8,128)S(1)}, f32[80,128]{1,0:T(8,128)S(1)}, u32[]{:S(2)}, u32[]{:S(2)}) %collective-permute-start.7) | collective-permute-done | bytes 40992 | tf_op jit(solution)/shard_map/ppermute | solution.py:37
  22.3 2.4 %collective-permute-done.9.refs_6_ = f32[80,128]{1,0:T(8,128)S(1)} collective-permute-done((f32[80,128]{1,0:T(8,128)S(1)}, f32[80,128]{1,0:T(8,128)S(1)}, u32[]{:S(2)}, u32[]{:S(2)}) %collective-permute-start.9) | collective-permute-done | bytes 40992 | tf_op jit(solution)/shard_map/ppermute | solution.py:37
  24.8 2.0 %collective-permute-start.11 = (f32[2,256]{1,0:T(2,128)S(1)}, f32[2,256]{1,0:T(2,128)S(1)}, u32[]{:S(2)}, u32[]{:S(2)}) collective-permute-start(f32[2,256]{1,0:T(2,128)S(1)} %get-tuple-element.27), channel_id=1, source_target_pairs={{0,1},{2,3},{1,0},{3,2},{4,5},{6,7},{5,4},{7,6},{8,9},{10,11},{9,8... | collective-permute-start | bytes 6152 | tf_op jit(solution)/shard_map/ppermute | solution.py:37
  26.8 1.6 %collective-permute-done.11 = f32[2,256]{1,0:T(2,128)S(1)} collective-permute-done((f32[2,256]{1,0:T(2,128)S(1)}, f32[2,256]{1,0:T(2,128)S(1)}, u32[]{:S(2)}, u32[]{:S(2)}) %collective-permute-start.11) | collective-permute-done | bytes 2080 | tf_op jit(solution)/shard_map/ppermute | solution.py:37
  28.4 1.8 %collective-permute-start.12 = (f32[2,256]{1,0:T(2,128)S(1)}, f32[2,256]{1,0:T(2,128)S(1)}, u32[]{:S(2)}, u32[]{:S(2)}) collective-permute-start(f32[2,256]{1,0:T(2,128)S(1)} %add.3.refs_8_), channel_id=1, source_target_pairs={{0,2},{1,3},{2,0},{3,1},{4,6},{5,7},{6,4},{7,5},{8,10},{9,11},{10,... | collective-permute-start | bytes 6152 | tf_op jit(solution)/shard_map/ppermute | solution.py:37
  30.2 2.7 %collective-permute-done.12.refs_9_ = f32[2,256]{1,0:T(2,128)S(1)} collective-permute-done((f32[2,256]{1,0:T(2,128)S(1)}, f32[2,256]{1,0:T(2,128)S(1)}, u32[]{:S(2)}, u32[]{:S(2)}) %collective-permute-start.12) | collective-permute-done | bytes 2080 | tf_op jit(solution)/shard_map/ppermute | solution.py:37
  32.9 0.9 %mix_particles.1 = (f32[4,8,64]{2,1,0:T(8,128)}, f32[2,256]{1,0:T(2,128)}) custom-call(f32[80,128]{1,0:T(8,128)S(1)} %get-tuple-element.26.refs_0_, f32[80,128]{1,0:T(8,128)S(1)} %collective-permute-done.4.refs_1_, f32[80,128]{1,0:T(8,128)S(1)} %collective-permute-done.5.refs_2_, f32[80,128]{1,0:T(8,128)S(1)} %collective-permute-done.6.refs_3_, ...), custom_call_target="tpu_custom_call" | custom-call | tf_op jit(solution)/shard_map/mix_particles/pallas_call | solution.py:531
  (15 shorter events, 0.0 us)
Async XLA Ops:
  0.6 14.4 %copy-start.1 = (f32[1,8,16,128]{3,2,1,0:T(8,128)S(1)}, f32[1,8,16,128]{3,2,1,0:T(8,128)}, u32[]{:S(2)}) copy-start(f32[1,8,16,128]{3,2,1,0:T(8,128)} %param.12) | copy-start | bytes 196612
  0.6 14.4 %copy-start.2 = (f32[1,8,16,128]{3,2,1,0:T(8,128)S(1)}, f32[1,8,16,128]{3,2,1,0:T(8,128)}, u32[]{:S(2)}) copy-start(f32[1,8,16,128]{3,2,1,0:T(8,128)} %param.14) | copy-start | bytes 196612
  0.7 14.4 %copy-start.3 = (f32[1,4,8,64]{3,2,1,0:T(8,128)S(1)}, f32[1,4,8,64]{3,2,1,0:T(8,128)}, u32[]{:S(2)}) copy-start(f32[1,4,8,64]{3,2,1,0:T(8,128)} %param.10) | copy-start | bytes 24580
  2.3 12.7 %copy-start = (f32[1,8,16,128]{3,2,1,0:T(8,128)S(1)}, f32[1,8,16,128]{3,2,1,0:T(8,128)}, u32[]{:S(2)}) copy-start(f32[1,8,16,128]{3,2,1,0:T(8,128)} %param.11) | copy-start | bytes 196612
  2.4 12.6 %collective-permute-start = (f32[17,16,128]{2,1,0:T(8,128)S(1)}, f32[17,16,128]{2,1,0:T(8,128)S(1)}, u32[]{:S(2)}, u32[]{:S(2)}) collective-permute-start(f32[17,16,128]{2,1,0:T(8,128)S(1)} %get-tuple-element.23), channel_id=1, source_target_pairs={{0,1},{2,3},{1,0},{3,2},{4,5},{6,7},{5,4},{7,6},{8,9},{10,11},{9,8... | collective-permute-start | bytes 417800 | tf_op jit(solution)/shard_map/ppermute | solution.py:37
  5.5 9.5 %collective-permute-start.1 = (f32[17,16,128]{2,1,0:T(8,128)S(1)}, f32[17,16,128]{2,1,0:T(8,128)S(1)}, u32[]{:S(2)}, u32[]{:S(2)}) collective-permute-start(f32[17,16,128]{2,1,0:T(8,128)S(1)} %get-tuple-element.24), channel_id=1, source_target_pairs={{1,2},{0,4},{3,7},{5,6},{9,10},{8,12},{11,15},{13,14},{17,18},{16,... | collective-permute-start | bytes 417800 | tf_op jit(solution)/shard_map/ppermute | solution.py:37
  5.5 4.8 %collective-permute-start.2 = (f32[16,128]{1,0:T(8,128)S(1)}, f32[16,128]{1,0:T(8,128)S(1)}, u32[]{:S(2)}, u32[]{:S(2)}) collective-permute-start(f32[16,128]{1,0:T(8,128)S(1)} %get-tuple-element.18.refs_8_), channel_id=1, source_target_pairs={{0,1},{2,3},{1,0},{3,2},{4,5},{6,7},{5,4},{7,6},{8,9},{10,11},{9,8... | collective-permute-start | bytes 24584 | tf_op jit(solution)/shard_map/ppermute | solution.py:37
  10.3 4.7 %collective-permute-start.3 = (f32[3,16,128]{2,1,0:T(8,128)S(1)}, f32[3,16,128]{2,1,0:T(8,128)S(1)}, u32[]{:S(2)}, u32[]{:S(2)}) collective-permute-start(f32[3,16,128]{2,1,0:T(8,128)S(1)} %join_messages.1), channel_id=1, source_target_pairs={{0,2},{1,3},{2,0},{3,1},{4,6},{5,7},{6,4},{7,5},{8,10},{9,11},{10,... | collective-permute-start | bytes 73736 | tf_op jit(solution)/shard_map/ppermute | solution.py:37
  16.8 4.0 %collective-permute-start.5 = (f32[80,128]{1,0:T(8,128)S(1)}, f32[80,128]{1,0:T(8,128)S(1)}, u32[]{:S(2)}, u32[]{:S(2)}) collective-permute-start(f32[80,128]{1,0:T(8,128)S(1)} %get-tuple-element.26.refs_0_), channel_id=1, source_target_pairs={{0,8},{4,12},{16,24},{20,28},{8,0},{12,4},{24,16},{28,20},{1,9},{5... | collective-permute-start | bytes 122888 | tf_op jit(solution)/shard_map/ppermute | solution.py:37
  18.3 4.0 %collective-permute-start.7 = (f32[80,128]{1,0:T(8,128)S(1)}, f32[80,128]{1,0:T(8,128)S(1)}, u32[]{:S(2)}, u32[]{:S(2)}) collective-permute-start(f32[80,128]{1,0:T(8,128)S(1)} %get-tuple-element.26.refs_0_), channel_id=1, source_target_pairs={{0,16},{4,20},{8,24},{12,28},{16,0},{20,4},{24,8},{28,12},{1,17},{... | collective-permute-start | bytes 122888 | tf_op jit(solution)/shard_map/ppermute | solution.py:37
  19.9 4.9 %collective-permute-start.9 = (f32[80,128]{1,0:T(8,128)S(1)}, f32[80,128]{1,0:T(8,128)S(1)}, u32[]{:S(2)}, u32[]{:S(2)}) collective-permute-start(f32[80,128]{1,0:T(8,128)S(1)} %get-tuple-element.26.refs_0_), channel_id=1, source_target_pairs={{0,24},{4,28},{8,16},{12,20},{24,0},{28,4},{16,8},{20,12},{1,25},{... | collective-permute-start | bytes 122888 | tf_op jit(solution)/shard_map/ppermute | solution.py:37
  20.3 12.5 %collective-permute-start.4 = (f32[80,128]{1,0:T(8,128)S(1)}, f32[80,128]{1,0:T(8,128)S(1)}, u32[]{:S(2)}, u32[]{:S(2)}) collective-permute-start(f32[80,128]{1,0:T(8,128)S(1)} %get-tuple-element.26.refs_0_), channel_id=1, source_target_pairs={{0,4},{8,12},{16,20},{24,28},{4,0},{12,8},{20,16},{28,24},{1,5},{9... | collective-permute-start | bytes 122888 | tf_op jit(solution)/shard_map/ppermute | solution.py:37
  20.8 12.0 %collective-permute-start.6 = (f32[80,128]{1,0:T(8,128)S(1)}, f32[80,128]{1,0:T(8,128)S(1)}, u32[]{:S(2)}, u32[]{:S(2)}) collective-permute-start(f32[80,128]{1,0:T(8,128)S(1)} %collective-permute-done.5.refs_2_), channel_id=1, source_target_pairs={{0,4},{8,12},{16,20},{24,28},{4,0},{12,8},{20,16},{28,24},{1,5},{9... | collective-permute-start | bytes 122888 | tf_op jit(solution)/shard_map/ppermute | solution.py:37
  22.3 10.5 %collective-permute-start.8 = (f32[80,128]{1,0:T(8,128)S(1)}, f32[80,128]{1,0:T(8,128)S(1)}, u32[]{:S(2)}, u32[]{:S(2)}) collective-permute-start(f32[80,128]{1,0:T(8,128)S(1)} %collective-permute-done.7.refs_4_), channel_id=1, source_target_pairs={{0,4},{8,12},{16,20},{24,28},{4,0},{12,8},{20,16},{28,24},{1,5},{9... | collective-permute-start | bytes 122888 | tf_op jit(solution)/shard_map/ppermute | solution.py:37
  24.8 8.1 %collective-permute-start.10 = (f32[80,128]{1,0:T(8,128)S(1)}, f32[80,128]{1,0:T(8,128)S(1)}, u32[]{:S(2)}, u32[]{:S(2)}) collective-permute-start(f32[80,128]{1,0:T(8,128)S(1)} %collective-permute-done.9.refs_6_), channel_id=1, source_target_pairs={{0,4},{8,12},{16,20},{24,28},{4,0},{12,8},{20,16},{28,24},{1,5},{9... | collective-permute-start | bytes 122888 | tf_op jit(solution)/shard_map/ppermute | solution.py:37
  24.8 3.6 %collective-permute-start.11 = (f32[2,256]{1,0:T(2,128)S(1)}, f32[2,256]{1,0:T(2,128)S(1)}, u32[]{:S(2)}, u32[]{:S(2)}) collective-permute-start(f32[2,256]{1,0:T(2,128)S(1)} %get-tuple-element.27), channel_id=1, source_target_pairs={{0,1},{2,3},{1,0},{3,2},{4,5},{6,7},{5,4},{7,6},{8,9},{10,11},{9,8... | collective-permute-start | bytes 6152 | tf_op jit(solution)/shard_map/ppermute | solution.py:37
  28.4 4.5 %collective-permute-start.12 = (f32[2,256]{1,0:T(2,128)S(1)}, f32[2,256]{1,0:T(2,128)S(1)}, u32[]{:S(2)}, u32[]{:S(2)}) collective-permute-start(f32[2,256]{1,0:T(2,128)S(1)} %add.3.refs_8_), channel_id=1, source_target_pairs={{0,2},{1,3},{2,0},{3,1},{4,6},{5,7},{6,4},{7,5},{8,10},{9,11},{10,... | collective-permute-start | bytes 6152 | tf_op jit(solution)/shard_map/ppermute | solution.py:37

commit v6 on v5

--- a/solution.py
+++ b/solution.py
@@ -35,11 +35,6 @@
 def swap(block, axis, pairs):
     both = [(a, b) for a, b in pairs] + [(b, a) for a, b in pairs]
     return lax.ppermute(block, axis, both)
-
-
-def twice(model):
-    flat = model.reshape(model.shape[0] * model.shape[1], model.shape[2])
-    return jnp.concatenate([flat, flat], axis=1)
 
 
 def lane_weights(size_z):
@@ -123,9 +118,7 @@
         for start in (0, REACH + width):
             ref[start : start + REACH, data, :] = jnp.zeros((REACH, size_y, size_z), f32)
         ref[REACH : REACH + width, data, :] = field[...]
-    rows = vel.shape[0] * vel.shape[1]
-    flat = vel[...].reshape(rows, vel.shape[2])
-    packed[...] = jnp.concatenate([flat[: rows // 2], flat[rows // 2 :]], axis=1)
+    packed[...] = pack(vel[...])
     fill_courant(c2_s, packed[...], size_z)
     rec_out[...] = rec[...]
     obs_out[...] = obs[...]
@@ -161,14 +154,22 @@
         ref[3 * REACH : 4 * REACH] = near[outer]
         deep = jnp.where(low == 0, picked[0:REACH], picked[top:width])
         block = jnp.concatenate([deep, picked[width : width + half]], axis=0)
-        ref[4 * REACH :] = fold(block, size_y, size_z)
+        ref[4 * REACH : 4 * REACH + 1] = fold(block, size_y, size_z)
+        ref[4 * REACH + 1 :] = packed[...].reshape(-1, size_y, size_z)
     to_far[0:1] = fold(columns, size_y, size_z)
     to_far[1:] = packed[...].reshape(to_far.shape[0] - 1, size_y, size_z)
 
 
-def join_kernel(first, second, out):
-    out[0 : first.shape[0]] = first[...]
-    out[first.shape[0] :] = second[...].reshape(-1, out.shape[1], out.shape[2])
+def pack(model):
+    flat = model.reshape(model.shape[0] * model.shape[1], model.shape[2])
+    half = flat.shape[0] // 2
+    return jnp.concatenate([flat[:half], flat[half:]], axis=1)
+
+
+def far_kernel(message, model, out, packed):
+    packed[...] = pack(model[...])
+    out[0 : message.shape[0]] = message[...]
+    out[message.shape[0] :] = packed[...].reshape(-1, *out.shape[1:])
 
 
 def fold(block, size_y, size_z):
@@ -182,48 +183,74 @@
     return jnp.concatenate([flat[at : at + rows] for at in range(0, flat.shape[0], rows)], axis=1)
 
 
-def wave_kernel(
-    src_cell, src_step, prev, cur, near, vel, own_part, near_part, packed, lanes_in, rec, wavelet, obs,
-    one, two, model_one, *rest, n_far, with_models
+def crossing(sources, depth):
+    terms = [STENCIL_WEIGHTS[depth + 1 + j] * sources[j] for j in range(REACH - depth)]
+    return sum(terms[1:], terms[0])
+
+
+def cross(ref, c2_s, size_y, at, shift, upward, read):
+    data = pl.ds(8, size_y)
+    for depth in range(REACH):
+        layer = at + depth if upward else at - 1 - depth
+        sources = [read(j) for j in range(REACH - depth)]
+        fine = (layer + shift) // 2 * size_y
+        factor = c2_s[fine : fine + size_y, :]
+        ref[layer, data, :] = ref[layer, data, :] + factor * crossing(sources, depth)
+
+
+def pulse_of(wavelet, at):
+    ticks = lax.broadcasted_iota(jnp.int32, wavelet.shape, 1)
+    return jnp.sum(jnp.where(ticks == at, wavelet[...], 0.0), axis=1, keepdims=True)
+
+
+def masked(block, inner):
+    return jnp.where(inner, block[...], 0.0)
+
+
+def place_of_slab():
+    place = lax.axis_index("slab")
+    inner = (place > 0) & (place < lax.axis_size("slab") - 1)
+    return place, place % 2, inner
+
+
+def forward_kernel(
+    src_cell, src_step, cur, own_part, packed, lanes_in, rec, wavelet, one, two,
+    samples, values, first_s, sec_s, c2_s, hot_out, cur_s, vel_s
 ):
-    if not with_models:
-        model_two, rest = rest[0], rest[1:]
-    fars = rest[:n_far]
-    pay, samples = rest[n_far : n_far + 2]
-    cur_s, near_s, first_s, sec_s, two_s, vel_s, c2_s, img_s = rest[n_far + 2 :]
-    width, size_y, size_z = prev.shape
-    rows = vel.shape[0] * vel.shape[1]
+    width, size_y, size_z = cur.shape
     receivers = rec.shape[1]
     plane = size_y * size_z
-    place = lax.axis_index("slab")
-    odd = place % 2
+    place, odd, inner = place_of_slab()
     f32 = jnp.float32
     data = pl.ds(8, size_y)
     lane = lax.broadcasted_iota(jnp.int32, (1, size_z), 1)
     weights = lane_weights(size_z)
     wide = 2 * REACH
     clear_margins(first_s, size_y)
-    clear_margins(two_s, size_y)
     for start in (0, width + wide + REACH):
         first_s[start : start + REACH, data, :] = jnp.zeros((REACH, size_y, size_z), f32)
     cur_s[REACH : REACH + width] = cur[...]
-    near_s[REACH : REACH + width] = near[...]
     first_s[wide : wide + width, data, :] = own_part[...]
-    two_s[REACH : REACH + width, data, :] = near_part[...]
     short = packed.shape[0]
     vel_s[short : 2 * short] = packed[...]
+
+    def put(block, high):
+        outer = pl.ds(high * (width + REACH), REACH)
+        first_s[pl.ds(high * (width + REACH) + REACH, REACH), data, :] = block[0:REACH]
+        cur_s[outer] = block[REACH : 2 * REACH]
+        vel_s[pl.ds(high * 2 * short, short)] = block[4 * REACH + 1 :].reshape(short, size_z)
+
+    put(one, 1 - odd)
+    put(masked(two, inner), odd)
+    fill_courant(c2_s, vel_s[...], size_z)
+    cross(first_s, c2_s, size_y, wide, 0, False, lambda j: cur_s[REACH + j])
+    cross(first_s, c2_s, size_y, wide, 0, True, lambda j: cur_s[REACH - 1 - j])
+    cross(first_s, c2_s, size_y, wide + width, 0, False, lambda j: cur_s[REACH + width + j])
+    cross(first_s, c2_s, size_y, wide + width, 0, True, lambda j: cur_s[REACH + width - 1 - j])
 
     cell = src_cell[0]
     now = src_step[0]
     src_layer = cell // plane - place * width
-    same_column = rec[...] % plane == cell % plane
-
-    ticks = lax.broadcasted_iota(jnp.int32, wavelet.shape, 1)
-
-    def pulse(ahead):
-        return jnp.sum(jnp.where(ticks == now + ahead, wavelet[...], 0.0), axis=1, keepdims=True)
-
-    pulse_one = pulse(1)
 
     def inject(ref, start, layers, offset, pulse):
         layer = src_layer + start
@@ -233,18 +260,72 @@
         at = pl.ds(offset + cell % plane // size_z, 1)
         ref[layer, at, :] = ref[layer, at, :] + jnp.where(lane == cell % size_z, value, 0.0)
 
+    inject(first_s.at[pl.ds(REACH, width + wide)], REACH, width + wide, 8, pulse_of(wavelet, now + 1))
+    for ch in range(0, width + 2 * REACH, STEP):
+        centre, total = laplace(first_s, ch + REACH, size_y, weights)
+        factor = courant(c2_s, ch + REACH, STEP, size_y)
+        sec_s[ch : ch + STEP] = 2.0 * centre - cur_s[ch : ch + STEP] + factor * total
+    inject(sec_s, REACH, width + wide, 0, pulse_of(wavelet, now + 2))
+
+    region = (width + 2 * REACH) * size_y
+    row = (rec[...] - (place * width - REACH) * plane) // size_z
+    hot = row == lax.broadcasted_iota(jnp.int32, (region, receivers), 0)
+    hot = jnp.where(hot, 1.0, 0.0).astype(jnp.bfloat16)
+    hot_out[...] = hot
+    lanes = lanes_in[...].astype(f32) > 0.5
+    lo = REACH * size_y
+    hi = lo + width * size_y
+
+    def read(field, marks):
+        turned = field.T
+        total = sum(jnp.dot(part, marks, preferred_element_type=f32) for part in split3(turned))
+        return jnp.sum(jnp.where(lanes, total, 0.0), axis=0, keepdims=True)
+
+    first_own = first_s[wide : wide + width, data, :].reshape(width * size_y, size_z)
+    read_one = read(first_own, hot[lo:hi])
+    read_two = read(sec_s[...].reshape(region, size_z), hot)
+    values[0:1, :] = read_one
+    values[1:2, :] = read_two
+    samples[0:1, :] = read_one
+    samples[1:2, :] = jnp.where((row >= lo) & (row < hi), read_two, 0.0)
+
+
+def adjoint_kernel(
+    src_cell, src_step, prev, cur, near, packed, near_part, lanes_in, rec, wavelet, obs, one, two,
+    values, first_s, sec_s, c2_s, hot_in, *rest, n_far, with_models
+):
+    fars = rest[:n_far]
+    rest = rest[n_far:]
+    if with_models:
+        model_one, rest = rest[0], rest[1:]
+    pay, near_s, two_s, img_s = rest
+    width, size_y, size_z = prev.shape
+    short = packed.shape[0]
+    rows = 2 * short
+    receivers = rec.shape[1]
+    plane = size_y * size_z
+    place, odd, inner = place_of_slab()
+    f32 = jnp.float32
+    data = pl.ds(8, size_y)
+    lane = lax.broadcasted_iota(jnp.int32, (1, size_z), 1)
+    weights = lane_weights(size_z)
+    wide = 2 * REACH
+    clear_margins(two_s, size_y)
+    near_s[REACH : REACH + width] = near[...]
+    two_s[REACH : REACH + width, data, :] = near_part[...]
+    cell = src_cell[0]
+    src_layer = cell // plane - place * width
+    same_column = rec[...] % plane == cell % plane
+    pulse_one = pulse_of(wavelet, src_step[0] + 1)
     far_high = 1 - (place % 4) // 2
     hops = [unfold(block[0:1], receivers) for block in fars]
 
-    def put(block, model, high):
+    def put(block, high):
         outer = pl.ds(high * (width + REACH), REACH)
-        first_s[pl.ds(high * (width + REACH) + REACH, REACH), data, :] = block[0:REACH]
-        cur_s[outer] = block[REACH : 2 * REACH]
         two_s[outer, data, :] = block[2 * REACH : 3 * REACH]
         near_s[outer] = block[3 * REACH : 4 * REACH]
-        vel_s[pl.ds(high * 2 * short, short)] = model
         up = high == 1
-        columns = unfold(block[4 * REACH :], receivers)
+        columns = unfold(block[4 * REACH : 4 * REACH + 1], receivers)
         half = columns.shape[0] - REACH
         deep = [jnp.where(up, columns[j : j + 1], columns[3 - j : 4 - j]) for j in range(REACH)]
         factor = [
@@ -269,50 +350,17 @@
             for depth in range(REACH)
         ]
 
-    gains_one = put(one, model_one[...], 1 - odd)
-    inner = (place > 0) & (place < lax.axis_size("slab") - 1)
-    if with_models:
-        model_two = fars[0][2:].reshape(short, size_z)
-    gains_two = put(jnp.where(inner, two[...], 0.0), jnp.where(inner, model_two[...], 0.0), odd)
-    fill_courant(c2_s, vel_s[...], size_z)
-
-    def crossing(sources, depth):
-        terms = [STENCIL_WEIGHTS[depth + 1 + j] * sources[j] for j in range(REACH - depth)]
-        return sum(terms[1:], terms[0])
-
-    def cross(ref, at, shift, upward, read):
-        for depth in range(REACH):
-            layer = at + depth if upward else at - 1 - depth
-            sources = [read(j) for j in range(REACH - depth)]
-            fine = (layer + shift) // 2 * size_y
-            factor = c2_s[fine : fine + size_y, :]
-            ref[layer, data, :] = ref[layer, data, :] + factor * crossing(sources, depth)
-
-    cross(first_s, wide, 0, False, lambda j: cur_s[REACH + j])
-    cross(first_s, wide, 0, True, lambda j: cur_s[REACH - 1 - j])
-    cross(first_s, wide + width, 0, False, lambda j: cur_s[REACH + width + j])
-    cross(first_s, wide + width, 0, True, lambda j: cur_s[REACH + width - 1 - j])
-    cross(two_s, REACH, REACH, False, lambda j: near_s[REACH + j])
-    cross(two_s, REACH, REACH, True, lambda j: near_s[REACH - 1 - j])
-    cross(two_s, REACH + width, REACH, False, lambda j: near_s[REACH + width + j])
-    cross(two_s, REACH + width, REACH, True, lambda j: near_s[REACH + width - 1 - j])
-
-    inject(first_s.at[pl.ds(REACH, width + wide)], REACH, width + wide, 8, pulse_one)
-    for ch in range(0, width + 2 * REACH, STEP):
-        centre, total = laplace(first_s, ch + REACH, size_y, weights)
-        factor = courant(c2_s, ch + REACH, STEP, size_y)
-        sec_s[ch : ch + STEP] = 2.0 * centre - cur_s[ch : ch + STEP] + factor * total
-    inject(sec_s, REACH, width + wide, 0, pulse(2))
-
-    region = (width + 2 * REACH) * size_y
-    row = (rec[...] - (place * width - REACH) * plane) // size_z
-    hot = row == lax.broadcasted_iota(jnp.int32, (region, receivers), 0)
-    hot = jnp.where(hot, 1.0, 0.0).astype(jnp.bfloat16)
+    gains_one = put(one, 1 - odd)
+    gains_two = put(masked(two, inner), odd)
+    cross(two_s, c2_s, size_y, REACH, REACH, False, lambda j: near_s[REACH + j])
+    cross(two_s, c2_s, size_y, REACH, REACH, True, lambda j: near_s[REACH - 1 - j])
+    cross(two_s, c2_s, size_y, REACH + width, REACH, False, lambda j: near_s[REACH + width + j])
+    cross(two_s, c2_s, size_y, REACH + width, REACH, True, lambda j: near_s[REACH + width - 1 - j])
+
     lanes = lanes_in[...].astype(f32) > 0.5
     lo = REACH * size_y
     hi = lo + width * size_y
-    own = (row >= lo) & (row < hi)
-    layer = row // size_y
+    layer = (rec[...] - (place * width - REACH) * plane) // plane
     gain = jnp.zeros((1, receivers), f32)
     for depth in range(REACH):
         low_layer = REACH - 1 - depth
@@ -321,24 +369,14 @@
         two_side = layer == low_layer + odd * (high_layer - low_layer)
         gain = jnp.where(one_side, gains_one[depth], jnp.where(two_side, gains_two[depth], gain))
 
-    def read(field, marks):
-        turned = field.T
-        total = sum(jnp.dot(part, marks, preferred_element_type=f32) for part in split3(turned))
-        return jnp.sum(jnp.where(lanes, total, 0.0), axis=0, keepdims=True)
-
-    def spread_out(values, marks):
-        placed = jnp.where(lanes, values, 0.0)
+    def spread_out(value, marks):
+        placed = jnp.where(lanes, value, 0.0)
         dims = (((1,), (1,)), ((), ()))
         return sum(lax.dot_general(marks, part, dims, preferred_element_type=f32) for part in split3(placed))
 
-    first_own = first_s[wide : wide + width, data, :].reshape(width * size_y, size_z)
-    read_one = read(first_own, hot[lo:hi])
-    read_two = read(sec_s[...].reshape(region, size_z), hot) + gain
-    samples[0:1, :] = read_one
-    samples[1:2, :] = jnp.where(own, read_two, 0.0)
-    add_one = spread_out(read_one - obs[0:1, :], hot[lo:hi])
-    add_two = spread_out(read_two - obs[1:2, :], hot)
-
+    hot = hot_in[...]
+    add_one = spread_out(values[0:1, :] - obs[0:1, :], hot[lo:hi])
+    add_two = spread_out(values[1:2, :] + gain - obs[1:2, :], hot)
     for ch in range(0, width + 2 * REACH, STEP):
         extra = add_two[ch * size_y : (ch + STEP) * size_y].reshape(STEP, size_y, size_z)
         two_s[ch : ch + STEP, data, :] = two_s[ch : ch + STEP, data, :] + extra
@@ -360,9 +398,13 @@
     gather = jnp.where(grid_r // 2 == grid_c, 1.0, 0.0).astype(f32)
     folded = img_s[pl.ds(0, rows, stride=2), :] + img_s[pl.ds(1, rows, stride=2), :]
     blocks = jnp.dot(folded, gather, precision=HIGHEST, preferred_element_type=f32)
-    own_vel = twice(vel[...])
+    left = lane < size_z // 2
+    turned = pltpu.roll(packed[...], size_z // 2, 1)
+    own_vel = jnp.concatenate(
+        [jnp.where(left, packed[...], turned), jnp.where(left, turned, packed[...])], axis=0
+    )
     factor = 2.0 / (own_vel * own_vel * own_vel)
-    pay[0:rows, :] = jnp.where(lane < size_z // 2, factor * blocks, own_vel)
+    pay[0:rows, :] = jnp.where(left, factor * blocks, own_vel)
     if with_models:
         pay[rows : rows + short, :] = model_one[...]
         pay[rows + short :, :] = fars[0][1:].reshape(2 * short, size_z)
@@ -430,7 +472,7 @@
     half, coarse_y, coarse_z = model.shape
     rows = half * coarse_y
     short = rows // 2
-    near_layers = 4 * REACH + 1
+    near_layers = 4 * REACH + 1 + short // size_y
     far_layers = 1 + short // size_y
     receivers = rec_cell.shape[0]
     in_vmem = pl.BlockSpec(memory_space=pltpu.VMEM)
@@ -454,56 +496,67 @@
         scratch_shapes=[padded, padded, pltpu.VMEM((2 * rows, size_z), f32)],
         name="start_steps",
     )
+    even = [(i, i + 1) for i in range(0, slabs - 1, 2)]
+    if fast:
+        model_one = swap(model, "slab", even)
     to_one, to_two, to_far, packed, *kept, obs = start(
         prev, cur, far, near, model, rec_cell[None], observed, wavelet[None]
     )
-    even = [(i, i + 1) for i in range(0, slabs - 1, 2)]
-    model_one = swap(packed, "slab", even)
     one = swap(to_one, "slab", even)
     two = swap_uneven(to_two, slabs, count)
     if fast:
-        to_far = pl.pallas_call(
-            join_kernel,
-            out_shape=pltpu.VMEM((far_layers + short // size_y, size_y, size_z), f32),
+        to_far, model_one = pl.pallas_call(
+            far_kernel,
+            out_shape=(
+                pltpu.VMEM((far_layers + short // size_y, size_y, size_z), f32),
+                pltpu.VMEM((short, size_z), f32),
+            ),
             in_specs=[in_vmem] * 2,
-            out_specs=in_vmem,
+            out_specs=(in_vmem, in_vmem),
             name="join_messages",
         )(resident(to_far), resident(model_one))
     fars = [swap(to_far, "slab", [(i, i + 2) for i in range(slabs - 2) if i % 4 < 2])]
-    models = [model_one]
-    if not fast:
-        models.append(swap_uneven(packed, slabs, count))
-        others = [(i, i + 2) for i in range(slabs - 2) if i % 4 >= 2]
-        if others:
-            fars.append(swap(to_far, "slab", others))
+    others = [(i, i + 2) for i in range(slabs - 2) if i % 4 >= 2]
+    if others:
+        fars.append(swap(to_far, "slab", others))
     wide = 2 * REACH
-    pay_rows = rows + 3 * short if fast else rows
-    own_part, near_part, *small = kept
-    operands = (
-        prev, cur, near, model, own_part, near_part, packed, *small, obs,
-        one, two, *models, *fars,
-    )
-    plain = pltpu.VMEM((width + 2 * REACH, size_y, size_z), f32)
-    pay, samples = pl.pallas_call(
-        lambda *refs: wave_kernel(*refs, n_far=len(fars), with_models=fast),
+    region = (width + wide) * size_y
+    own_part, near_part, lanes, rec, pulses = kept
+    in_smem = pl.BlockSpec(memory_space=pltpu.SMEM)
+    plain = pltpu.VMEM((width + wide, size_y, size_z), f32)
+    operands = (cur, own_part, packed, lanes, rec, pulses, one, two)
+    forward = pl.pallas_call(
+        forward_kernel,
         out_shape=(
-            pltpu.VMEM((pay_rows, size_z), f32),
             pltpu.VMEM((2, receivers), f32),
-        ),
-        in_specs=[pl.BlockSpec(memory_space=pltpu.SMEM)] * 2 + [in_vmem] * len(operands),
-        out_specs=(in_vmem, in_vmem),
-        scratch_shapes=[
-            plain,
-            plain,
+            pltpu.VMEM((2, receivers), f32),
             pltpu.VMEM((width + 2 * wide, PITCH, size_z), f32),
             plain,
-            padded,
-            pltpu.VMEM((3 * short, size_z), f32),
             pltpu.VMEM((6 * rows, size_z), f32),
-            pltpu.VMEM((2 * rows, size_z), f32),
-        ],
-        name="wave_steps",
-    )(src_cell, src_step, *[resident(block) for block in operands])
+            pltpu.VMEM((region, receivers), jnp.bfloat16),
+        ),
+        in_specs=[in_smem] * 2 + [in_vmem] * len(operands),
+        out_specs=(in_vmem,) * 6,
+        scratch_shapes=[plain, pltpu.VMEM((3 * short, size_z), f32)],
+        name="forward_steps",
+    )
+    samples, *waves = forward(src_cell, src_step, *[resident(block) for block in operands])
+    if fast:
+        part = samples + swap(samples, "slab", [(0, 1), (2, 3)])
+    pay_rows = rows + 3 * short if fast else rows
+    operands = (
+        prev, cur, near, packed, near_part, lanes, rec, pulses, obs, one, two, *waves, *fars,
+        *([model_one] if fast else []),
+    )
+    adjoint = pl.pallas_call(
+        lambda *refs: adjoint_kernel(*refs, n_far=len(fars), with_models=fast),
+        out_shape=pltpu.VMEM((pay_rows, size_z), f32),
+        in_specs=[in_smem] * 2 + [in_vmem] * len(operands),
+        out_specs=in_vmem,
+        scratch_shapes=[plain, padded, pltpu.VMEM((2 * rows, size_z), f32)],
+        name="adjoint_steps",
+    )
+    pay = adjoint(src_cell, src_step, *[resident(block) for block in operands])
     cells_coarse = rows * slabs * coarse_z
     if not fast:
         residual = lax.psum(samples, "slab") - observed
@@ -526,7 +579,6 @@
     for flip in (0, 6, 4, 2):
         pairs = [(i, i ^ 1) for i in range(0, count, 2)]
         blocks[flip + 1] = swap(blocks[flip], "particle", pairs)
-    part = samples + swap(samples, "slab", [(0, 1), (2, 3)])
     other = swap(part, "slab", [(0, 2), (1, 3)])
     update, residual = pl.pallas_call(
         lambda *refs: mix_kernel(*refs, cells=cells_coarse),

time: 33.9 us -> 32.1 us (0.947)
  waiting for transfers between devices: 11.9 us -> 9.44 us
  starting transfers between devices: 15.5 us -> 16 us
    ppermute x13, waiting for transfers between devices: 11.9 us -> 9.44 us  [swap(): return lax.ppermute(block, axis, both)]
    ppermute x13, starting transfers between devices: 15.5 us -> 16 us  [swap(): return lax.ppermute(block, axis, both)]
    pallas_call x2 -> x3, Pallas kernels: 1.79 us -> 1.92 us  [the longest x1 1.02 us: device_step(): forward(src_cell, src_step, *[resident(block) for block in operands])]
  transfers between devices with their start and end apart: 13 -> 13, of which waited for: 7 -> 7; matrix products, arithmetic and copies ran while one was open for 0% -> 0% of each run, Pallas kernels for 0% -> 3%
where the time goes in v6:
time: 32.1 us; the launch traced here: 31.9 us
  starting transfers between devices  16 us (50%)
  waiting for transfers between devices  9.44 us (29%)
  Pallas kernels  4.47 us (14%)
  between operations  2.03 us (6%)
    ppermute x13, starting transfers between devices, swap(): return lax.ppermute(block, axis, both)  16 us
    ppermute x13, waiting for transfers between devices, swap(): return lax.ppermute(block, axis, both)  9.44 us
    pallas_call x1, Pallas kernels, device_step(): start(prev, cur, far, near, model, rec_cell[None], observed, wavelet[None])  1.67 us
    pallas_call x1, Pallas kernels, device_step(): forward(src_cell, src_step, *[resident(block) for block in operands])  1.02 us
    pallas_call x1, Pallas kernels, device_step(): pl.pallas_call(lambda *refs: mix_kernel(*refs, cells=cells_coarse), out_s...  0.88 us
    pallas_call x1, Pallas kernels, device_step(): pay = adjoint(src_cell, src_step, *[resident(block) for block in operands])  0.83 us
  transfers between devices with their start and end apart: 13, of which 7 were waited for; matrix products, arithmetic and copies ran while one was open for 0% of the time, Pallas kernels for 3%

profile of v6, /device:TPU:0, one launch (start us, length us, event | category | flops | bytes accessed | tf_op | source)
XLA Modules:
  0.0 31.9 jit_solution(173700200182883985)
XLA Ops:
  0.7 1.7 %start_steps.1 = (f32[18,16,128]{2,1,0:T(8,128)S(1)}, f32[18,16,128]{2,1,0:T(8,128)S(1)}, f32[2,16,128]{2,1,0:T(8,128)S(1)}, f32[16,128]{1,0:T(8,128)S(1)}, f32[...) custom-call(f32[8,16,128]{2,1,0:T(8,128)} %bitcast.12, ...), custom_call_target="tpu_custom_call" | custom-call | tf_op jit(solution)/shard_map/start_steps/pallas_call | solution.py:502
  2.3 3.1 %collective-permute-start = (f32[18,16,128]{2,1,0:T(8,128)S(1)}, f32[18,16,128]{2,1,0:T(8,128)S(1)}, u32[]{:S(2)}, u32[]{:S(2)}) collective-permute-start(f32[18,16,128]{2,1,0:T(8,128)S(1)} %get-tuple-element.28), channel_id=1, source_target_pairs={{0,1},{2,3},{1,0},{3,2},{4,5},{6,7},{5,4},{7,6},{8,9},{10,11},{9,8... | collective-permute-start | bytes 442376 | tf_op jit(solution)/shard_map/ppermute | solution.py:37
  5.4 0.0 collective-permute-start.1
  5.5 3.1 %collective-permute-start.2 = (f32[4,8,64]{2,1,0:T(8,128)S(1)}, f32[4,8,64]{2,1,0:T(8,128)S(1)}, u32[]{:S(2)}, u32[]{:S(2)}) collective-permute-start(f32[4,8,64]{2,1,0:T(8,128)S(1)} %bitcast.18), channel_id=1, source_target_pairs={{0,1},{2,3},{1,0},{3,2},{4,5},{6,7},{5,4},{7,6},{8,9},{10,11},{9,8... | collective-permute-start | bytes 24584 | tf_op jit(solution)/shard_map/ppermute | solution.py:37
  8.6 1.7 %collective-permute-done.2.model = f32[4,8,64]{2,1,0:T(8,128)S(1)} collective-permute-done((f32[4,8,64]{2,1,0:T(8,128)S(1)}, f32[4,8,64]{2,1,0:T(8,128)S(1)}, u32[]{:S(2)}, u32[]{:S(2)}) %collective-permute-start.2) | collective-permute-done | bytes 8224 | tf_op jit(solution)/shard_map/ppermute | solution.py:37
  10.3 0.1 join_messages.1
  10.4 2.1 %collective-permute-start.3 = (f32[3,16,128]{2,1,0:T(8,128)S(1)}, f32[3,16,128]{2,1,0:T(8,128)S(1)}, u32[]{:S(2)}, u32[]{:S(2)}) collective-permute-start(f32[3,16,128]{2,1,0:T(8,128)S(1)} %get-tuple-element.37), channel_id=1, source_target_pairs={{0,2},{1,3},{2,0},{3,1},{4,6},{5,7},{6,4},{7,5},{8,10},{9,11},{10,... | collective-permute-start | bytes 73736 | tf_op jit(solution)/shard_map/ppermute | solution.py:37
  13.8 0.0 collective-permute-done.one.refs_11_
  13.8 0.0 copy-start.1
  13.8 0.0 copy-start.2
  13.8 1.0 %forward_steps.1 = (f32[2,256]{1,0:T(2,128)S(1)}, f32[2,256]{1,0:T(2,128)S(1)}, f32[24,32,128]{2,1,0:T(8,128)S(1)}, f32[16,16,128]{2,1,0:T(8,128)S(1)}, f32[192,...) custom-call(s32[1]{0:T(128)S(6)} %copy.12.src_cell.refs_0_, s32[1]{0:T(128)S(6)} %copy.13.src_step.refs_1_, ...), custom_call_target="tpu_custom_call" | custom-call | tf_op jit(solution)/shard_map/forward_steps/pallas_call | solution.py:543
  14.9 0.3 collective-permute-done.3.refs_18_
  15.1 0.8 %adjoint_steps.1.refs_0_ = f32[80,128]{1,0:T(8,128)S(1)} custom-call(s32[1]{0:T(128)S(6)} %copy.12.src_cell.refs_0_, s32[1]{0:T(128)S(6)} %copy.13.src_step.refs_1_, f32[8,16,128]{2,1,0:T(8,128)S(1)} %bitcast.13, f32[8,16,128]{2,1,0:T(8,128)S(1)} %bitcast.11, f32[8,16,128]{2,1,0:T(8,128)S(1)} %bitcast.15, f32[16,128]{1,0:T(8,128)S(1)} %get-tuple-element.22.packed.refs_5_, ...), custom_call_target="tpu_custom_call" | custom-call | tf_op jit(solution)/shard_map/adjoint_steps/pallas_call | solution.py:559
  16.0 2.5 %collective-permute-start.9 = (f32[80,128]{1,0:T(8,128)S(1)}, f32[80,128]{1,0:T(8,128)S(1)}, u32[]{:S(2)}, u32[]{:S(2)}) collective-permute-start(f32[80,128]{1,0:T(8,128)S(1)} %adjoint_steps.1.refs_0_), channel_id=1, source_target_pairs={{0,24},{4,28},{8,16},{12,20},{24,0},{28,4},{16,8},{20,12},{1,25},{... | collective-permute-start | bytes 122888 | tf_op jit(solution)/shard_map/ppermute | solution.py:37
  18.4 0.5 %collective-permute-start.5 = (f32[80,128]{1,0:T(8,128)S(1)}, f32[80,128]{1,0:T(8,128)S(1)}, u32[]{:S(2)}, u32[]{:S(2)}) collective-permute-start(f32[80,128]{1,0:T(8,128)S(1)} %adjoint_steps.1.refs_0_), channel_id=1, source_target_pairs={{0,8},{4,12},{16,24},{20,28},{8,0},{12,4},{24,16},{28,20},{1,9},{5... | collective-permute-start | bytes 122888 | tf_op jit(solution)/shard_map/ppermute | solution.py:37
  18.9 0.5 %collective-permute-start.7 = (f32[80,128]{1,0:T(8,128)S(1)}, f32[80,128]{1,0:T(8,128)S(1)}, u32[]{:S(2)}, u32[]{:S(2)}) collective-permute-start(f32[80,128]{1,0:T(8,128)S(1)} %adjoint_steps.1.refs_0_), channel_id=1, source_target_pairs={{0,16},{4,20},{8,24},{12,28},{16,0},{20,4},{24,8},{28,12},{1,17},{... | collective-permute-start | bytes 122888 | tf_op jit(solution)/shard_map/ppermute | solution.py:37
  19.5 1.4 %collective-permute-done.9.refs_6_ = f32[80,128]{1,0:T(8,128)S(1)} collective-permute-done((f32[80,128]{1,0:T(8,128)S(1)}, f32[80,128]{1,0:T(8,128)S(1)}, u32[]{:S(2)}, u32[]{:S(2)}) %collective-permute-start.9) | collective-permute-done | bytes 40992 | tf_op jit(solution)/shard_map/ppermute | solution.py:37
  20.9 1.6 %collective-permute-done.5.refs_2_ = f32[80,128]{1,0:T(8,128)S(1)} collective-permute-done((f32[80,128]{1,0:T(8,128)S(1)}, f32[80,128]{1,0:T(8,128)S(1)}, u32[]{:S(2)}, u32[]{:S(2)}) %collective-permute-start.5) | collective-permute-done | bytes 40992 | tf_op jit(solution)/shard_map/ppermute | solution.py:37
  22.4 0.5 %collective-permute-done.7.refs_4_ = f32[80,128]{1,0:T(8,128)S(1)} collective-permute-done((f32[80,128]{1,0:T(8,128)S(1)}, f32[80,128]{1,0:T(8,128)S(1)}, u32[]{:S(2)}, u32[]{:S(2)}) %collective-permute-start.7) | collective-permute-done | bytes 40992 | tf_op jit(solution)/shard_map/ppermute | solution.py:37
  23.0 2.0 %collective-permute-start.11 = (f32[2,256]{1,0:T(2,128)S(1)}, f32[2,256]{1,0:T(2,128)S(1)}, u32[]{:S(2)}, u32[]{:S(2)}) collective-permute-start(f32[2,256]{1,0:T(2,128)S(1)} %get-tuple-element.39), channel_id=1, source_target_pairs={{0,1},{2,3},{1,0},{3,2},{4,5},{6,7},{5,4},{7,6},{8,9},{10,11},{9,8... | collective-permute-start | bytes 6152 | tf_op jit(solution)/shard_map/ppermute | solution.py:37
  25.0 1.6 %collective-permute-done.11 = f32[2,256]{1,0:T(2,128)S(1)} collective-permute-done((f32[2,256]{1,0:T(2,128)S(1)}, f32[2,256]{1,0:T(2,128)S(1)}, u32[]{:S(2)}, u32[]{:S(2)}) %collective-permute-start.11) | collective-permute-done | bytes 2080 | tf_op jit(solution)/shard_map/ppermute | solution.py:37
  26.5 2.1 %collective-permute-start.12 = (f32[2,256]{1,0:T(2,128)S(1)}, f32[2,256]{1,0:T(2,128)S(1)}, u32[]{:S(2)}, u32[]{:S(2)}) collective-permute-start(f32[2,256]{1,0:T(2,128)S(1)} %add.3.refs_8_), channel_id=1, source_target_pairs={{0,2},{1,3},{2,0},{3,1},{4,6},{5,7},{6,4},{7,5},{8,10},{9,11},{10,... | collective-permute-start | bytes 6152 | tf_op jit(solution)/shard_map/ppermute | solution.py:37
  28.6 2.4 %collective-permute-done.12.refs_9_ = f32[2,256]{1,0:T(2,128)S(1)} collective-permute-done((f32[2,256]{1,0:T(2,128)S(1)}, f32[2,256]{1,0:T(2,128)S(1)}, u32[]{:S(2)}, u32[]{:S(2)}) %collective-permute-start.12) | collective-permute-done | bytes 2080 | tf_op jit(solution)/shard_map/ppermute | solution.py:37
  31.1 0.9 %mix_particles.1 = (f32[4,8,64]{2,1,0:T(8,128)}, f32[2,256]{1,0:T(2,128)}) custom-call(f32[80,128]{1,0:T(8,128)S(1)} %adjoint_steps.1.refs_0_, f32[80,128]{1,0:T(8,128)S(1)} %collective-permute-done.4.refs_1_, f32[80,128]{1,0:T(8,128)S(1)} %collective-permute-done.5.refs_2_, f32[80,128]{1,0:T(8,128)S(1)} %collective-permute-done.6.refs_3_, ...), custom_call_target="tpu_custom_call" | custom-call | tf_op jit(solution)/shard_map/mix_particles/pallas_call | solution.py:583
  (16 shorter events, 0.0 us)
Async XLA Ops:
  0.6 4.8 %copy-start.3 = (f32[1,4,8,64]{3,2,1,0:T(8,128)S(1)}, f32[1,4,8,64]{3,2,1,0:T(8,128)}, u32[]{:S(2)}) copy-start(f32[1,4,8,64]{3,2,1,0:T(8,128)} %param.10) | copy-start | bytes 24580
  0.6 13.2 %copy-start = (f32[1,8,16,128]{3,2,1,0:T(8,128)S(1)}, f32[1,8,16,128]{3,2,1,0:T(8,128)}, u32[]{:S(2)}) copy-start(f32[1,8,16,128]{3,2,1,0:T(8,128)} %param.12) | copy-start | bytes 196612
  2.3 11.4 %collective-permute-start = (f32[18,16,128]{2,1,0:T(8,128)S(1)}, f32[18,16,128]{2,1,0:T(8,128)S(1)}, u32[]{:S(2)}, u32[]{:S(2)}) collective-permute-start(f32[18,16,128]{2,1,0:T(8,128)S(1)} %get-tuple-element.28), channel_id=1, source_target_pairs={{0,1},{2,3},{1,0},{3,2},{4,5},{6,7},{5,4},{7,6},{8,9},{10,11},{9,8... | collective-permute-start | bytes 442376 | tf_op jit(solution)/shard_map/ppermute | solution.py:37
  5.4 8.3 %collective-permute-start.1 = (f32[18,16,128]{2,1,0:T(8,128)S(1)}, f32[18,16,128]{2,1,0:T(8,128)S(1)}, u32[]{:S(2)}, u32[]{:S(2)}) collective-permute-start(f32[18,16,128]{2,1,0:T(8,128)S(1)} %get-tuple-element.29), channel_id=1, source_target_pairs={{1,2},{0,4},{3,7},{5,6},{9,10},{8,12},{11,15},{13,14},{17,18},{16,... | collective-permute-start | bytes 442376 | tf_op jit(solution)/shard_map/ppermute | solution.py:37
  5.5 4.9 %collective-permute-start.2 = (f32[4,8,64]{2,1,0:T(8,128)S(1)}, f32[4,8,64]{2,1,0:T(8,128)S(1)}, u32[]{:S(2)}, u32[]{:S(2)}) collective-permute-start(f32[4,8,64]{2,1,0:T(8,128)S(1)} %bitcast.18), channel_id=1, source_target_pairs={{0,1},{2,3},{1,0},{3,2},{4,5},{6,7},{5,4},{7,6},{8,9},{10,11},{9,8... | collective-permute-start | bytes 24584 | tf_op jit(solution)/shard_map/ppermute | solution.py:37
  10.4 4.7 %collective-permute-start.3 = (f32[3,16,128]{2,1,0:T(8,128)S(1)}, f32[3,16,128]{2,1,0:T(8,128)S(1)}, u32[]{:S(2)}, u32[]{:S(2)}) collective-permute-start(f32[3,16,128]{2,1,0:T(8,128)S(1)} %get-tuple-element.37), channel_id=1, source_target_pairs={{0,2},{1,3},{2,0},{3,1},{4,6},{5,7},{6,4},{7,5},{8,10},{9,11},{10,... | collective-permute-start | bytes 73736 | tf_op jit(solution)/shard_map/ppermute | solution.py:37
  13.8 1.3 %copy-start.1 = (f32[1,8,16,128]{3,2,1,0:T(8,128)S(1)}, f32[1,8,16,128]{3,2,1,0:T(8,128)}, u32[]{:S(2)}) copy-start(f32[1,8,16,128]{3,2,1,0:T(8,128)} %param.11) | copy-start | bytes 196612
  13.8 1.3 %copy-start.2 = (f32[1,8,16,128]{3,2,1,0:T(8,128)S(1)}, f32[1,8,16,128]{3,2,1,0:T(8,128)}, u32[]{:S(2)}) copy-start(f32[1,8,16,128]{3,2,1,0:T(8,128)} %param.14) | copy-start | bytes 196612
  16.0 4.9 %collective-permute-start.9 = (f32[80,128]{1,0:T(8,128)S(1)}, f32[80,128]{1,0:T(8,128)S(1)}, u32[]{:S(2)}, u32[]{:S(2)}) collective-permute-start(f32[80,128]{1,0:T(8,128)S(1)} %adjoint_steps.1.refs_0_), channel_id=1, source_target_pairs={{0,24},{4,28},{8,16},{12,20},{24,0},{28,4},{16,8},{20,12},{1,25},{... | collective-permute-start | bytes 122888 | tf_op jit(solution)/shard_map/ppermute | solution.py:37
  18.4 4.0 %collective-permute-start.5 = (f32[80,128]{1,0:T(8,128)S(1)}, f32[80,128]{1,0:T(8,128)S(1)}, u32[]{:S(2)}, u32[]{:S(2)}) collective-permute-start(f32[80,128]{1,0:T(8,128)S(1)} %adjoint_steps.1.refs_0_), channel_id=1, source_target_pairs={{0,8},{4,12},{16,24},{20,28},{8,0},{12,4},{24,16},{28,20},{1,9},{5... | collective-permute-start | bytes 122888 | tf_op jit(solution)/shard_map/ppermute | solution.py:37
  18.9 4.0 %collective-permute-start.7 = (f32[80,128]{1,0:T(8,128)S(1)}, f32[80,128]{1,0:T(8,128)S(1)}, u32[]{:S(2)}, u32[]{:S(2)}) collective-permute-start(f32[80,128]{1,0:T(8,128)S(1)} %adjoint_steps.1.refs_0_), channel_id=1, source_target_pairs={{0,16},{4,20},{8,24},{12,28},{16,0},{20,4},{24,8},{28,12},{1,17},{... | collective-permute-start | bytes 122888 | tf_op jit(solution)/shard_map/ppermute | solution.py:37
  19.5 11.6 %collective-permute-start.4 = (f32[80,128]{1,0:T(8,128)S(1)}, f32[80,128]{1,0:T(8,128)S(1)}, u32[]{:S(2)}, u32[]{:S(2)}) collective-permute-start(f32[80,128]{1,0:T(8,128)S(1)} %adjoint_steps.1.refs_0_), channel_id=1, source_target_pairs={{0,4},{8,12},{16,20},{24,28},{4,0},{12,8},{20,16},{28,24},{1,5},{9... | collective-permute-start | bytes 122888 | tf_op jit(solution)/shard_map/ppermute | solution.py:37
  20.9 10.2 %collective-permute-start.10 = (f32[80,128]{1,0:T(8,128)S(1)}, f32[80,128]{1,0:T(8,128)S(1)}, u32[]{:S(2)}, u32[]{:S(2)}) collective-permute-start(f32[80,128]{1,0:T(8,128)S(1)} %collective-permute-done.9.refs_6_), channel_id=1, source_target_pairs={{0,4},{8,12},{16,20},{24,28},{4,0},{12,8},{20,16},{28,24},{1,5},{9... | collective-permute-start | bytes 122888 | tf_op jit(solution)/shard_map/ppermute | solution.py:37
  22.4 8.6 %collective-permute-start.6 = (f32[80,128]{1,0:T(8,128)S(1)}, f32[80,128]{1,0:T(8,128)S(1)}, u32[]{:S(2)}, u32[]{:S(2)}) collective-permute-start(f32[80,128]{1,0:T(8,128)S(1)} %collective-permute-done.5.refs_2_), channel_id=1, source_target_pairs={{0,4},{8,12},{16,20},{24,28},{4,0},{12,8},{20,16},{28,24},{1,5},{9... | collective-permute-start | bytes 122888 | tf_op jit(solution)/shard_map/ppermute | solution.py:37
  22.9 8.1 %collective-permute-start.8 = (f32[80,128]{1,0:T(8,128)S(1)}, f32[80,128]{1,0:T(8,128)S(1)}, u32[]{:S(2)}, u32[]{:S(2)}) collective-permute-start(f32[80,128]{1,0:T(8,128)S(1)} %collective-permute-done.7.refs_4_), channel_id=1, source_target_pairs={{0,4},{8,12},{16,20},{24,28},{4,0},{12,8},{20,16},{28,24},{1,5},{9... | collective-permute-start | bytes 122888 | tf_op jit(solution)/shard_map/ppermute | solution.py:37
  23.0 3.6 %collective-permute-start.11 = (f32[2,256]{1,0:T(2,128)S(1)}, f32[2,256]{1,0:T(2,128)S(1)}, u32[]{:S(2)}, u32[]{:S(2)}) collective-permute-start(f32[2,256]{1,0:T(2,128)S(1)} %get-tuple-element.39), channel_id=1, source_target_pairs={{0,1},{2,3},{1,0},{3,2},{4,5},{6,7},{5,4},{7,6},{8,9},{10,11},{9,8... | collective-permute-start | bytes 6152 | tf_op jit(solution)/shard_map/ppermute | solution.py:37
  26.5 4.5 %collective-permute-start.12 = (f32[2,256]{1,0:T(2,128)S(1)}, f32[2,256]{1,0:T(2,128)S(1)}, u32[]{:S(2)}, u32[]{:S(2)}) collective-permute-start(f32[2,256]{1,0:T(2,128)S(1)} %add.3.refs_8_), channel_id=1, source_target_pairs={{0,2},{1,3},{2,0},{3,1},{4,6},{5,7},{6,4},{7,5},{8,10},{9,11},{10,... | collective-permute-start | bytes 6152 | tf_op jit(solution)/shard_map/ppermute | solution.py:37

commit v7 on v6

--- a/solution.py
+++ b/solution.py
@@ -172,6 +172,11 @@
     out[message.shape[0] :] = packed[...].reshape(-1, *out.shape[1:])
 
 
+def join_kernel(first, second, out):
+    out[0 : first.shape[0]] = first[...]
+    out[first.shape[0] :] = second[...].reshape(-1, *out.shape[1:])
+
+
 def fold(block, size_y, size_z):
     pieces = [block[:, at : at + size_z] for at in range(0, block.shape[1], size_z)]
     return jnp.concatenate(pieces, axis=0).reshape(-1, size_y, size_z)
@@ -411,16 +416,16 @@
 
 
 def mix_kernel(*refs, cells):
-    count = len(refs) - 5
-    pays = refs[:count]
-    part, other, obs, update, misfit = refs[count:]
+    part, other, obs, update, misfit = refs[-5:]
+    total = refs[0].shape[0]
+    pays = [ref.at[at : at + total] for ref in refs[:-5] for at in range(0, ref.shape[0], total)]
+    count = len(pays)
     f32 = jnp.float32
     misfit[...] = part[...] + other[...] - obs[...]
     rows = update.shape[0] * update.shape[1]
     lane = lax.broadcasted_iota(jnp.int32, (1, pays[0].shape[1]), 1)
     half = update.shape[2]
     model_lane = lane >= half
-    total = pays[0].shape[0]
     mean = sum(ref[...] for ref in pays[1:]) + pays[0][...]
     mean = mean * (1.0 / count)
 
@@ -573,12 +578,19 @@
         update = (mixed[:, :coarse_z] + pull) / count
         return (update.reshape(model.shape)[None], residual[None])
 
-    blocks = {0: pay}
-    for flip in (6, 4, 2):
-        blocks[flip] = swap(pay, "particle", [(i, i ^ flip) for i in range(count) if i < i ^ flip])
-    for flip in (0, 6, 4, 2):
-        pairs = [(i, i ^ 1) for i in range(0, count, 2)]
-        blocks[flip + 1] = swap(blocks[flip], "particle", pairs)
+    cores = [(i, i ^ 1) for i in range(0, count, 2)]
+    beside = swap(pay, "particle", cores)
+    corner = swap(pay, "particle", [(i, i ^ 6) for i in range(count) if i < i ^ 6])
+    both = pl.pallas_call(
+        join_kernel,
+        out_shape=pltpu.VMEM((2 * pay_rows, size_z), f32),
+        in_specs=[in_vmem] * 2,
+        out_specs=in_vmem,
+        name="join_blocks",
+    )(resident(pay), resident(beside))
+    sides = [(i, i ^ 4) for i in (0, 2)] + [(i, i ^ 2) for i in (1, 5)]
+    side = swap(both, "particle", sides)
+    blocks = [pay, beside, corner, swap(corner, "particle", cores), side, swap(side, "particle", cores)]
     other = swap(part, "slab", [(0, 2), (1, 3)])
     update, residual = pl.pallas_call(
         lambda *refs: mix_kernel(*refs, cells=cells_coarse),
@@ -586,10 +598,10 @@
             jax.ShapeDtypeStruct(model.shape, f32),
             jax.ShapeDtypeStruct((2, receivers), f32),
         ),
-        in_specs=[in_vmem] * 11,
+        in_specs=[in_vmem] * (len(blocks) + 3),
         out_specs=(in_vmem, in_vmem),
         name="mix_particles",
-    )(*[resident(blocks[i]) for i in range(count)], resident(part), resident(other), resident(obs))
+    )(*[resident(block) for block in blocks], resident(part), resident(other), resident(obs))
     return (update[None], residual[None])
 
 

time: 32.1 us -> 32.8 us (1.022)
  waiting for transfers between devices: 9.44 us -> 10.6 us
  starting transfers between devices: 16 us -> 15.4 us
    ppermute x13 -> x11, waiting for transfers between devices: 9.44 us -> 10.6 us  [swap(): return lax.ppermute(block, axis, both)]
    ppermute x13 -> x11, starting transfers between devices: 16 us -> 15.4 us  [swap(): return lax.ppermute(block, axis, both)]
  transfers between devices with their start and end apart: 13 -> 11, of which waited for: 7 -> 7; matrix products, arithmetic and copies ran while one was open for 0% -> 0% of each run, Pallas kernels for 3% -> 3%
where the time goes in v7:
time: 32.8 us; the launch traced here: 32.6 us
  starting transfers between devices  15.4 us (47%)
  waiting for transfers between devices  10.6 us (32%)
  Pallas kernels  4.48 us (14%)
  between operations  2.01 us (6%)
    ppermute x11, starting transfers between devices, swap(): return lax.ppermute(block, axis, both)  15.4 us
    ppermute x11, waiting for transfers between devices, swap(): return lax.ppermute(block, axis, both)  10.6 us
    pallas_call x1, Pallas kernels, device_step(): start(prev, cur, far, near, model, rec_cell[None], observed, wavelet[None])  1.67 us
    pallas_call x1, Pallas kernels, device_step(): forward(src_cell, src_step, *[resident(block) for block in operands])  1.02 us
    pallas_call x1, Pallas kernels, device_step(): pl.pallas_call(lambda *refs: mix_kernel(*refs, cells=cells_coarse), out_s...  0.88 us
    pallas_call x1, Pallas kernels, device_step(): pay = adjoint(src_cell, src_step, *[resident(block) for block in operands])  0.83 us
  transfers between devices with their start and end apart: 11, of which 7 were waited for; matrix products, arithmetic and copies ran while one was open for 0% of the time, Pallas kernels for 3%

profile of v7, /device:TPU:0, one launch (start us, length us, event | category | flops | bytes accessed | tf_op | source)
XLA Modules:
  0.0 32.6 jit_solution(736895693037512378)
XLA Ops:
  0.7 1.7 %start_steps.1 = (f32[18,16,128]{2,1,0:T(8,128)S(1)}, f32[18,16,128]{2,1,0:T(8,128)S(1)}, f32[2,16,128]{2,1,0:T(8,128)S(1)}, f32[16,128]{1,0:T(8,128)S(1)}, f32[...) custom-call(f32[8,16,128]{2,1,0:T(8,128)} %bitcast.12, ...), custom_call_target="tpu_custom_call" | custom-call | tf_op jit(solution)/shard_map/start_steps/pallas_call | solution.py:507
  2.3 3.1 %collective-permute-start = (f32[18,16,128]{2,1,0:T(8,128)S(1)}, f32[18,16,128]{2,1,0:T(8,128)S(1)}, u32[]{:S(2)}, u32[]{:S(2)}) collective-permute-start(f32[18,16,128]{2,1,0:T(8,128)S(1)} %get-tuple-element.28), channel_id=1, source_target_pairs={{0,1},{2,3},{1,0},{3,2},{4,5},{6,7},{5,4},{7,6},{8,9},{10,11},{9,8... | collective-permute-start | bytes 442376 | tf_op jit(solution)/shard_map/ppermute | solution.py:37
  5.4 0.0 collective-permute-start.1
  5.5 3.1 %collective-permute-start.2 = (f32[4,8,64]{2,1,0:T(8,128)S(1)}, f32[4,8,64]{2,1,0:T(8,128)S(1)}, u32[]{:S(2)}, u32[]{:S(2)}) collective-permute-start(f32[4,8,64]{2,1,0:T(8,128)S(1)} %bitcast.18), channel_id=1, source_target_pairs={{0,1},{2,3},{1,0},{3,2},{4,5},{6,7},{5,4},{7,6},{8,9},{10,11},{9,8... | collective-permute-start | bytes 24584 | tf_op jit(solution)/shard_map/ppermute | solution.py:37
  8.6 1.7 %collective-permute-done.2.model = f32[4,8,64]{2,1,0:T(8,128)S(1)} collective-permute-done((f32[4,8,64]{2,1,0:T(8,128)S(1)}, f32[4,8,64]{2,1,0:T(8,128)S(1)}, u32[]{:S(2)}, u32[]{:S(2)}) %collective-permute-start.2) | collective-permute-done | bytes 8224 | tf_op jit(solution)/shard_map/ppermute | solution.py:37
  10.3 0.1 join_messages.1
  10.4 2.1 %collective-permute-start.3 = (f32[3,16,128]{2,1,0:T(8,128)S(1)}, f32[3,16,128]{2,1,0:T(8,128)S(1)}, u32[]{:S(2)}, u32[]{:S(2)}) collective-permute-start(f32[3,16,128]{2,1,0:T(8,128)S(1)} %get-tuple-element.37), channel_id=1, source_target_pairs={{0,2},{1,3},{2,0},{3,1},{4,6},{5,7},{6,4},{7,5},{8,10},{9,11},{10,... | collective-permute-start | bytes 73736 | tf_op jit(solution)/shard_map/ppermute | solution.py:37
  13.8 0.0 collective-permute-done.one.refs_11_
  13.8 0.0 collective-permute-done.1.two.refs_12_
  13.8 0.0 copy-start.1
  13.8 0.0 copy-start.2
  13.8 1.0 %forward_steps.1 = (f32[2,256]{1,0:T(2,128)S(1)}, f32[2,256]{1,0:T(2,128)S(1)}, f32[24,32,128]{2,1,0:T(8,128)S(1)}, f32[16,16,128]{2,1,0:T(8,128)S(1)}, f32[192,...) custom-call(s32[1]{0:T(128)S(6)} %copy.12.src_cell.refs_0_, s32[1]{0:T(128)S(6)} %copy.13.src_step.refs_1_, ...), custom_call_target="tpu_custom_call" | custom-call | tf_op jit(solution)/shard_map/forward_steps/pallas_call | solution.py:548
  14.9 0.3 collective-permute-done.3.refs_18_
  15.1 0.8 %adjoint_steps.1.first.refs_0_ = f32[80,128]{1,0:T(8,128)S(1)} custom-call(s32[1]{0:T(128)S(6)} %copy.12.src_cell.refs_0_, s32[1]{0:T(128)S(6)} %copy.13.src_step.refs_1_, f32[8,16,128]{2,1,0:T(8,128)S(1)} %bitcast.13, f32[8,16,128]{2,1,0:T(8,128)S(1)} %bitcast.11, f32[8,16,128]{2,1,0:T(8,128)S(1)} %bitcast.15, ...), custom_call_target="tpu_custom_call" | custom-call | tf_op jit(solution)/shard_map/adjoint_steps/pallas_call | solution.py:564
  16.0 1.2 %collective-permute-done.4.second.refs_1_ = f32[80,128]{1,0:T(8,128)S(1)} collective-permute-done((f32[80,128]{1,0:T(8,128)S(1)}, f32[80,128]{1,0:T(8,128)S(1)}, u32[]{:S(2)}, u32[]{:S(2)}) %collective-permute-start.4) | collective-permute-done | bytes 40992 | tf_op jit(solution)/shard_map/ppermute | solution.py:37
  17.2 1.5 %collective-permute-start.7 = (f32[160,128]{1,0:T(8,128)S(1)}, f32[160,128]{1,0:T(8,128)S(1)}, u32[]{:S(2)}, u32[]{:S(2)}) collective-permute-start(f32[160,128]{1,0:T(8,128)S(1)} %join_blocks.1), channel_id=1, source_target_pairs={{0,16},{8,24},{4,12},{20,28},{16,0},{24,8},{12,4},{28,20},{1,17},{... | collective-permute-start | bytes 245768 | tf_op jit(solution)/shard_map/ppermute | solution.py:37
  18.7 1.4 %collective-permute-start.5 = (f32[80,128]{1,0:T(8,128)S(1)}, f32[80,128]{1,0:T(8,128)S(1)}, u32[]{:S(2)}, u32[]{:S(2)}) collective-permute-start(f32[80,128]{1,0:T(8,128)S(1)} %adjoint_steps.1.first.refs_0_), channel_id=1, source_target_pairs={{0,24},{4,28},{8,16},{12,20},{24,0},{28,4},{16,8},{20,12},{1,25},{... | collective-permute-start | bytes 122888 | tf_op jit(solution)/shard_map/ppermute | solution.py:37
  20.1 1.5 %collective-permute-done.7.refs_4_ = f32[160,128]{1,0:T(8,128)S(1)} collective-permute-done((f32[160,128]{1,0:T(8,128)S(1)}, f32[160,128]{1,0:T(8,128)S(1)}, u32[]{:S(2)}, u32[]{:S(2)}) %collective-permute-start.7) | collective-permute-done | bytes 81952 | tf_op jit(solution)/shard_map/ppermute | solution.py:37
  21.6 2.0 %collective-permute-done.5.refs_2_ = f32[80,128]{1,0:T(8,128)S(1)} collective-permute-done((f32[80,128]{1,0:T(8,128)S(1)}, f32[80,128]{1,0:T(8,128)S(1)}, u32[]{:S(2)}, u32[]{:S(2)}) %collective-permute-start.5) | collective-permute-done | bytes 40992 | tf_op jit(solution)/shard_map/ppermute | solution.py:37
  23.6 2.0 %collective-permute-start.9 = (f32[2,256]{1,0:T(2,128)S(1)}, f32[2,256]{1,0:T(2,128)S(1)}, u32[]{:S(2)}, u32[]{:S(2)}) collective-permute-start(f32[2,256]{1,0:T(2,128)S(1)} %get-tuple-element.39), channel_id=1, source_target_pairs={{0,1},{2,3},{1,0},{3,2},{4,5},{6,7},{5,4},{7,6},{8,9},{10,11},{9,8... | collective-permute-start | bytes 6152 | tf_op jit(solution)/shard_map/ppermute | solution.py:37
  25.6 1.6 %collective-permute-done.9 = f32[2,256]{1,0:T(2,128)S(1)} collective-permute-done((f32[2,256]{1,0:T(2,128)S(1)}, f32[2,256]{1,0:T(2,128)S(1)}, u32[]{:S(2)}, u32[]{:S(2)}) %collective-permute-start.9) | collective-permute-done | bytes 2080 | tf_op jit(solution)/shard_map/ppermute | solution.py:37
  27.2 2.1 %collective-permute-start.10 = (f32[2,256]{1,0:T(2,128)S(1)}, f32[2,256]{1,0:T(2,128)S(1)}, u32[]{:S(2)}, u32[]{:S(2)}) collective-permute-start(f32[2,256]{1,0:T(2,128)S(1)} %add.3.refs_6_), channel_id=1, source_target_pairs={{0,2},{1,3},{2,0},{3,1},{4,6},{5,7},{6,4},{7,5},{8,10},{9,11},{10,... | collective-permute-start | bytes 6152 | tf_op jit(solution)/shard_map/ppermute | solution.py:37
  29.3 2.4 %collective-permute-done.10.refs_7_ = f32[2,256]{1,0:T(2,128)S(1)} collective-permute-done((f32[2,256]{1,0:T(2,128)S(1)}, f32[2,256]{1,0:T(2,128)S(1)}, u32[]{:S(2)}, u32[]{:S(2)}) %collective-permute-start.10) | collective-permute-done | bytes 2080 | tf_op jit(solution)/shard_map/ppermute | solution.py:37
  31.7 0.9 %mix_particles.1 = (f32[4,8,64]{2,1,0:T(8,128)}, f32[2,256]{1,0:T(2,128)}) custom-call(f32[80,128]{1,0:T(8,128)S(1)} %adjoint_steps.1.first.refs_0_, f32[80,128]{1,0:T(8,128)S(1)} %collective-permute-done.4.second.refs_1_, f32[80,128]{1,0:T(8,128)S(1)} %collective-permute-done.5.refs_2_, f32[80,128]{1,0:T(8,128)S(1)} %collective-permute-done.6.refs_3_, ...), custom_call_target="tpu_custom_call" | custom-call | tf_op jit(solution)/shard_map/mix_particles/pallas_call | solution.py:595
  (13 shorter events, 0.0 us)
Async XLA Ops:
  0.6 4.8 %copy-start.3 = (f32[1,4,8,64]{3,2,1,0:T(8,128)S(1)}, f32[1,4,8,64]{3,2,1,0:T(8,128)}, u32[]{:S(2)}) copy-start(f32[1,4,8,64]{3,2,1,0:T(8,128)} %param.10) | copy-start | bytes 24580
  0.6 13.2 %copy-start = (f32[1,8,16,128]{3,2,1,0:T(8,128)S(1)}, f32[1,8,16,128]{3,2,1,0:T(8,128)}, u32[]{:S(2)}) copy-start(f32[1,8,16,128]{3,2,1,0:T(8,128)} %param.12) | copy-start | bytes 196612
  2.3 11.4 %collective-permute-start = (f32[18,16,128]{2,1,0:T(8,128)S(1)}, f32[18,16,128]{2,1,0:T(8,128)S(1)}, u32[]{:S(2)}, u32[]{:S(2)}) collective-permute-start(f32[18,16,128]{2,1,0:T(8,128)S(1)} %get-tuple-element.28), channel_id=1, source_target_pairs={{0,1},{2,3},{1,0},{3,2},{4,5},{6,7},{5,4},{7,6},{8,9},{10,11},{9,8... | collective-permute-start | bytes 442376 | tf_op jit(solution)/shard_map/ppermute | solution.py:37
  5.4 8.3 %collective-permute-start.1 = (f32[18,16,128]{2,1,0:T(8,128)S(1)}, f32[18,16,128]{2,1,0:T(8,128)S(1)}, u32[]{:S(2)}, u32[]{:S(2)}) collective-permute-start(f32[18,16,128]{2,1,0:T(8,128)S(1)} %get-tuple-element.29), channel_id=1, source_target_pairs={{1,2},{0,4},{3,7},{5,6},{9,10},{8,12},{11,15},{13,14},{17,18},{16,... | collective-permute-start | bytes 442376 | tf_op jit(solution)/shard_map/ppermute | solution.py:37
  5.5 4.9 %collective-permute-start.2 = (f32[4,8,64]{2,1,0:T(8,128)S(1)}, f32[4,8,64]{2,1,0:T(8,128)S(1)}, u32[]{:S(2)}, u32[]{:S(2)}) collective-permute-start(f32[4,8,64]{2,1,0:T(8,128)S(1)} %bitcast.18), channel_id=1, source_target_pairs={{0,1},{2,3},{1,0},{3,2},{4,5},{6,7},{5,4},{7,6},{8,9},{10,11},{9,8... | collective-permute-start | bytes 24584 | tf_op jit(solution)/shard_map/ppermute | solution.py:37
  10.4 4.7 %collective-permute-start.3 = (f32[3,16,128]{2,1,0:T(8,128)S(1)}, f32[3,16,128]{2,1,0:T(8,128)S(1)}, u32[]{:S(2)}, u32[]{:S(2)}) collective-permute-start(f32[3,16,128]{2,1,0:T(8,128)S(1)} %get-tuple-element.37), channel_id=1, source_target_pairs={{0,2},{1,3},{2,0},{3,1},{4,6},{5,7},{6,4},{7,5},{8,10},{9,11},{10,... | collective-permute-start | bytes 73736 | tf_op jit(solution)/shard_map/ppermute | solution.py:37
  13.8 1.3 %copy-start.1 = (f32[1,8,16,128]{3,2,1,0:T(8,128)S(1)}, f32[1,8,16,128]{3,2,1,0:T(8,128)}, u32[]{:S(2)}) copy-start(f32[1,8,16,128]{3,2,1,0:T(8,128)} %param.11) | copy-start | bytes 196612
  13.8 1.3 %copy-start.2 = (f32[1,8,16,128]{3,2,1,0:T(8,128)S(1)}, f32[1,8,16,128]{3,2,1,0:T(8,128)}, u32[]{:S(2)}) copy-start(f32[1,8,16,128]{3,2,1,0:T(8,128)} %param.14) | copy-start | bytes 196612
  16.0 1.2 %collective-permute-start.4 = (f32[80,128]{1,0:T(8,128)S(1)}, f32[80,128]{1,0:T(8,128)S(1)}, u32[]{:S(2)}, u32[]{:S(2)}) collective-permute-start(f32[80,128]{1,0:T(8,128)S(1)} %adjoint_steps.1.first.refs_0_), channel_id=1, source_target_pairs={{0,4},{8,12},{16,20},{24,28},{4,0},{12,8},{20,16},{28,24},{1,5},{9... | collective-permute-start | bytes 122888 | tf_op jit(solution)/shard_map/ppermute | solution.py:37
  17.2 4.4 %collective-permute-start.7 = (f32[160,128]{1,0:T(8,128)S(1)}, f32[160,128]{1,0:T(8,128)S(1)}, u32[]{:S(2)}, u32[]{:S(2)}) collective-permute-start(f32[160,128]{1,0:T(8,128)S(1)} %join_blocks.1), channel_id=1, source_target_pairs={{0,16},{8,24},{4,12},{20,28},{16,0},{24,8},{12,4},{28,20},{1,17},{... | collective-permute-start | bytes 245768 | tf_op jit(solution)/shard_map/ppermute | solution.py:37
  18.7 4.9 %collective-permute-start.5 = (f32[80,128]{1,0:T(8,128)S(1)}, f32[80,128]{1,0:T(8,128)S(1)}, u32[]{:S(2)}, u32[]{:S(2)}) collective-permute-start(f32[80,128]{1,0:T(8,128)S(1)} %adjoint_steps.1.first.refs_0_), channel_id=1, source_target_pairs={{0,24},{4,28},{8,16},{12,20},{24,0},{28,4},{16,8},{20,12},{1,25},{... | collective-permute-start | bytes 122888 | tf_op jit(solution)/shard_map/ppermute | solution.py:37
  21.6 10.1 %collective-permute-start.8 = (f32[160,128]{1,0:T(8,128)S(1)}, f32[160,128]{1,0:T(8,128)S(1)}, u32[]{:S(2)}, u32[]{:S(2)}) collective-permute-start(f32[160,128]{1,0:T(8,128)S(1)} %collective-permute-done.7.refs_4_), channel_id=1, source_target_pairs={{0,4},{8,12},{16,20},{24,28},{4,0},{12,8},{20,16},{28,24},{1,5},{9... | collective-permute-start | bytes 245768 | tf_op jit(solution)/shard_map/ppermute | solution.py:37
  23.6 8.1 %collective-permute-start.6 = (f32[80,128]{1,0:T(8,128)S(1)}, f32[80,128]{1,0:T(8,128)S(1)}, u32[]{:S(2)}, u32[]{:S(2)}) collective-permute-start(f32[80,128]{1,0:T(8,128)S(1)} %collective-permute-done.5.refs_2_), channel_id=1, source_target_pairs={{0,4},{8,12},{16,20},{24,28},{4,0},{12,8},{20,16},{28,24},{1,5},{9... | collective-permute-start | bytes 122888 | tf_op jit(solution)/shard_map/ppermute | solution.py:37
  23.6 3.6 %collective-permute-start.9 = (f32[2,256]{1,0:T(2,128)S(1)}, f32[2,256]{1,0:T(2,128)S(1)}, u32[]{:S(2)}, u32[]{:S(2)}) collective-permute-start(f32[2,256]{1,0:T(2,128)S(1)} %get-tuple-element.39), channel_id=1, source_target_pairs={{0,1},{2,3},{1,0},{3,2},{4,5},{6,7},{5,4},{7,6},{8,9},{10,11},{9,8... | collective-permute-start | bytes 6152 | tf_op jit(solution)/shard_map/ppermute | solution.py:37
  27.2 4.5 %collective-permute-start.10 = (f32[2,256]{1,0:T(2,128)S(1)}, f32[2,256]{1,0:T(2,128)S(1)}, u32[]{:S(2)}, u32[]{:S(2)}) collective-permute-start(f32[2,256]{1,0:T(2,128)S(1)} %add.3.refs_6_), channel_id=1, source_target_pairs={{0,2},{1,3},{2,0},{3,1},{4,6},{5,7},{6,4},{7,5},{8,10},{9,11},{10,... | collective-permute-start | bytes 6152 | tf_op jit(solution)/shard_map/ppermute | solution.py:37

commit v8 on v6

--- a/solution.py
+++ b/solution.py
@@ -73,9 +73,10 @@
 def fill_courant(c2_ref, packed, size_z):
     grid_r = lax.broadcasted_iota(jnp.int32, (size_z, 2 * size_z), 0)
     grid_c = lax.broadcasted_iota(jnp.int32, (size_z, 2 * size_z), 1)
-    spread = jnp.where(grid_r == grid_c // 2, 1.0, 0.0).astype(jnp.float32)
+    spread = jnp.where(grid_r == grid_c // 2, 1.0, 0.0).astype(jnp.bfloat16)
     scaled = COURANT_FACTOR * packed
-    fine = jnp.dot(scaled * scaled, spread, precision=HIGHEST, preferred_element_type=jnp.float32)
+    parts = split3(scaled * scaled)
+    fine = sum(jnp.dot(part, spread, preferred_element_type=jnp.float32) for part in parts)
     count = packed.shape[0]
     part = count if count < 16 else 16
     for start in range(0, count, part):
@@ -395,9 +396,9 @@
         img_s[ch // 2 * size_y : (ch + STEP) // 2 * size_y, :] = image.reshape(STEP // 2 * size_y, size_z)
     grid_r = lax.broadcasted_iota(jnp.int32, (size_z, size_z), 0)
     grid_c = lax.broadcasted_iota(jnp.int32, (size_z, size_z), 1)
-    gather = jnp.where(grid_r // 2 == grid_c, 1.0, 0.0).astype(f32)
+    gather = jnp.where(grid_r // 2 == grid_c, 1.0, 0.0).astype(jnp.bfloat16)
     folded = img_s[pl.ds(0, rows, stride=2), :] + img_s[pl.ds(1, rows, stride=2), :]
-    blocks = jnp.dot(folded, gather, precision=HIGHEST, preferred_element_type=f32)
+    blocks = sum(jnp.dot(part, gather, preferred_element_type=f32) for part in split3(folded))
     left = lane < size_z // 2
     turned = pltpu.roll(packed[...], size_z // 2, 1)
     own_vel = jnp.concatenate(

time: 32.1 us -> 32 us (level)
  no operation moved by 1% of the time
where the time goes in v8:
time: 32 us; the launch traced here: 31.8 us
  starting transfers between devices  16 us (50%)
  waiting for transfers between devices  9.49 us (30%)
  Pallas kernels  4.26 us (13%)
  between operations  2.03 us (6%)
    ppermute x13, starting transfers between devices, swap(): return lax.ppermute(block, axis, both)  16 us
    ppermute x13, waiting for transfers between devices, swap(): return lax.ppermute(block, axis, both)  9.49 us
    pallas_call x1, Pallas kernels, device_step(): start(prev, cur, far, near, model, rec_cell[None], observed, wavelet[None])  1.57 us
    pallas_call x1, Pallas kernels, device_step(): forward(src_cell, src_step, *[resident(block) for block in operands])  0.96 us
    pallas_call x1, Pallas kernels, device_step(): pl.pallas_call(lambda *refs: mix_kernel(*refs, cells=cells_coarse), out_s...  0.88 us
    pallas_call x1, Pallas kernels, device_step(): pay = adjoint(src_cell, src_step, *[resident(block) for block in operands])  0.77 us
  transfers between devices with their start and end apart: 13, of which 7 were waited for; matrix products, arithmetic and copies ran while one was open for 0% of the time, Pallas kernels for 3%

profile of v8, /device:TPU:0, one launch (start us, length us, event | category | flops | bytes accessed | tf_op | source)
XLA Modules:
  0.0 31.8 jit_solution(12470318800504480634)
XLA Ops:
  0.7 1.6 %start_steps.1 = (f32[18,16,128]{2,1,0:T(8,128)S(1)}, f32[18,16,128]{2,1,0:T(8,128)S(1)}, f32[2,16,128]{2,1,0:T(8,128)S(1)}, f32[16,128]{1,0:T(8,128)S(1)}, f32[...) custom-call(f32[8,16,128]{2,1,0:T(8,128)} %bitcast.12, ...), custom_call_target="tpu_custom_call" | custom-call | tf_op jit(solution)/shard_map/start_steps/pallas_call | solution.py:503
  2.2 3.1 %collective-permute-start = (f32[18,16,128]{2,1,0:T(8,128)S(1)}, f32[18,16,128]{2,1,0:T(8,128)S(1)}, u32[]{:S(2)}, u32[]{:S(2)}) collective-permute-start(f32[18,16,128]{2,1,0:T(8,128)S(1)} %get-tuple-element.28), channel_id=1, source_target_pairs={{0,1},{2,3},{1,0},{3,2},{4,5},{6,7},{5,4},{7,6},{8,9},{10,11},{9,8... | collective-permute-start | bytes 442376 | tf_op jit(solution)/shard_map/ppermute | solution.py:37
  5.3 0.0 collective-permute-start.1
  5.4 3.1 %collective-permute-start.2 = (f32[4,8,64]{2,1,0:T(8,128)S(1)}, f32[4,8,64]{2,1,0:T(8,128)S(1)}, u32[]{:S(2)}, u32[]{:S(2)}) collective-permute-start(f32[4,8,64]{2,1,0:T(8,128)S(1)} %bitcast.18), channel_id=1, source_target_pairs={{0,1},{2,3},{1,0},{3,2},{4,5},{6,7},{5,4},{7,6},{8,9},{10,11},{9,8... | collective-permute-start | bytes 24584 | tf_op jit(solution)/shard_map/ppermute | solution.py:37
  8.5 1.7 %collective-permute-done.2.model = f32[4,8,64]{2,1,0:T(8,128)S(1)} collective-permute-done((f32[4,8,64]{2,1,0:T(8,128)S(1)}, f32[4,8,64]{2,1,0:T(8,128)S(1)}, u32[]{:S(2)}, u32[]{:S(2)}) %collective-permute-start.2) | collective-permute-done | bytes 8224 | tf_op jit(solution)/shard_map/ppermute | solution.py:37
  10.2 0.1 join_messages.1
  10.3 2.1 %collective-permute-start.3 = (f32[3,16,128]{2,1,0:T(8,128)S(1)}, f32[3,16,128]{2,1,0:T(8,128)S(1)}, u32[]{:S(2)}, u32[]{:S(2)}) collective-permute-start(f32[3,16,128]{2,1,0:T(8,128)S(1)} %get-tuple-element.37), channel_id=1, source_target_pairs={{0,2},{1,3},{2,0},{3,1},{4,6},{5,7},{6,4},{7,5},{8,10},{9,11},{10,... | collective-permute-start | bytes 73736 | tf_op jit(solution)/shard_map/ppermute | solution.py:37
  13.7 0.0 collective-permute-done.1.two.refs_12_
  13.7 0.0 copy-start.1
  13.7 0.0 copy-start.2
  13.7 1.0 %forward_steps.1 = (f32[2,256]{1,0:T(2,128)S(1)}, f32[2,256]{1,0:T(2,128)S(1)}, f32[24,32,128]{2,1,0:T(8,128)S(1)}, f32[16,16,128]{2,1,0:T(8,128)S(1)}, f32[192,...) custom-call(s32[1]{0:T(128)S(6)} %copy.12.src_cell.refs_0_, s32[1]{0:T(128)S(6)} %copy.13.src_step.refs_1_, ...), custom_call_target="tpu_custom_call" | custom-call | tf_op jit(solution)/shard_map/forward_steps/pallas_call | solution.py:544
  14.7 0.3 %collective-permute-done.3.refs_18_ = f32[3,16,128]{2,1,0:T(8,128)S(1)} collective-permute-done((f32[3,16,128]{2,1,0:T(8,128)S(1)}, f32[3,16,128]{2,1,0:T(8,128)S(1)}, u32[]{:S(2)}, u32[]{:S(2)}) %collective-permute-start.3) | collective-permute-done | bytes 24608 | tf_op jit(solution)/shard_map/ppermute | solution.py:37
  15.0 0.8 %adjoint_steps.1.refs_0_ = f32[80,128]{1,0:T(8,128)S(1)} custom-call(s32[1]{0:T(128)S(6)} %copy.12.src_cell.refs_0_, s32[1]{0:T(128)S(6)} %copy.13.src_step.refs_1_, f32[8,16,128]{2,1,0:T(8,128)S(1)} %bitcast.13, f32[8,16,128]{2,1,0:T(8,128)S(1)} %bitcast.11, f32[8,16,128]{2,1,0:T(8,128)S(1)} %bitcast.15, f32[16,128]{1,0:T(8,128)S(1)} %get-tuple-element.22.packed.refs_5_, ...), custom_call_target="tpu_custom_call" | custom-call | tf_op jit(solution)/shard_map/adjoint_steps/pallas_call | solution.py:560
  15.8 2.5 %collective-permute-start.9 = (f32[80,128]{1,0:T(8,128)S(1)}, f32[80,128]{1,0:T(8,128)S(1)}, u32[]{:S(2)}, u32[]{:S(2)}) collective-permute-start(f32[80,128]{1,0:T(8,128)S(1)} %adjoint_steps.1.refs_0_), channel_id=1, source_target_pairs={{0,24},{4,28},{8,16},{12,20},{24,0},{28,4},{16,8},{20,12},{1,25},{... | collective-permute-start | bytes 122888 | tf_op jit(solution)/shard_map/ppermute | solution.py:37
  18.3 0.5 %collective-permute-start.5 = (f32[80,128]{1,0:T(8,128)S(1)}, f32[80,128]{1,0:T(8,128)S(1)}, u32[]{:S(2)}, u32[]{:S(2)}) collective-permute-start(f32[80,128]{1,0:T(8,128)S(1)} %adjoint_steps.1.refs_0_), channel_id=1, source_target_pairs={{0,8},{4,12},{16,24},{20,28},{8,0},{12,4},{24,16},{28,20},{1,9},{5... | collective-permute-start | bytes 122888 | tf_op jit(solution)/shard_map/ppermute | solution.py:37
  18.8 0.5 %collective-permute-start.7 = (f32[80,128]{1,0:T(8,128)S(1)}, f32[80,128]{1,0:T(8,128)S(1)}, u32[]{:S(2)}, u32[]{:S(2)}) collective-permute-start(f32[80,128]{1,0:T(8,128)S(1)} %adjoint_steps.1.refs_0_), channel_id=1, source_target_pairs={{0,16},{4,20},{8,24},{12,28},{16,0},{20,4},{24,8},{28,12},{1,17},{... | collective-permute-start | bytes 122888 | tf_op jit(solution)/shard_map/ppermute | solution.py:37
  19.3 1.4 %collective-permute-done.9.refs_6_ = f32[80,128]{1,0:T(8,128)S(1)} collective-permute-done((f32[80,128]{1,0:T(8,128)S(1)}, f32[80,128]{1,0:T(8,128)S(1)}, u32[]{:S(2)}, u32[]{:S(2)}) %collective-permute-start.9) | collective-permute-done | bytes 40992 | tf_op jit(solution)/shard_map/ppermute | solution.py:37
  20.7 1.5 %collective-permute-done.5.refs_2_ = f32[80,128]{1,0:T(8,128)S(1)} collective-permute-done((f32[80,128]{1,0:T(8,128)S(1)}, f32[80,128]{1,0:T(8,128)S(1)}, u32[]{:S(2)}, u32[]{:S(2)}) %collective-permute-start.5) | collective-permute-done | bytes 40992 | tf_op jit(solution)/shard_map/ppermute | solution.py:37
  22.3 0.5 %collective-permute-done.7.refs_4_ = f32[80,128]{1,0:T(8,128)S(1)} collective-permute-done((f32[80,128]{1,0:T(8,128)S(1)}, f32[80,128]{1,0:T(8,128)S(1)}, u32[]{:S(2)}, u32[]{:S(2)}) %collective-permute-start.7) | collective-permute-done | bytes 40992 | tf_op jit(solution)/shard_map/ppermute | solution.py:37
  22.8 2.0 %collective-permute-start.11 = (f32[2,256]{1,0:T(2,128)S(1)}, f32[2,256]{1,0:T(2,128)S(1)}, u32[]{:S(2)}, u32[]{:S(2)}) collective-permute-start(f32[2,256]{1,0:T(2,128)S(1)} %get-tuple-element.39), channel_id=1, source_target_pairs={{0,1},{2,3},{1,0},{3,2},{4,5},{6,7},{5,4},{7,6},{8,9},{10,11},{9,8... | collective-permute-start | bytes 6152 | tf_op jit(solution)/shard_map/ppermute | solution.py:37
  24.8 1.6 %collective-permute-done.11 = f32[2,256]{1,0:T(2,128)S(1)} collective-permute-done((f32[2,256]{1,0:T(2,128)S(1)}, f32[2,256]{1,0:T(2,128)S(1)}, u32[]{:S(2)}, u32[]{:S(2)}) %collective-permute-start.11) | collective-permute-done | bytes 2080 | tf_op jit(solution)/shard_map/ppermute | solution.py:37
  26.4 2.1 %collective-permute-start.12 = (f32[2,256]{1,0:T(2,128)S(1)}, f32[2,256]{1,0:T(2,128)S(1)}, u32[]{:S(2)}, u32[]{:S(2)}) collective-permute-start(f32[2,256]{1,0:T(2,128)S(1)} %add.3.refs_8_), channel_id=1, source_target_pairs={{0,2},{1,3},{2,0},{3,1},{4,6},{5,7},{6,4},{7,5},{8,10},{9,11},{10,... | collective-permute-start | bytes 6152 | tf_op jit(solution)/shard_map/ppermute | solution.py:37
  28.5 2.4 %collective-permute-done.12.refs_9_ = f32[2,256]{1,0:T(2,128)S(1)} collective-permute-done((f32[2,256]{1,0:T(2,128)S(1)}, f32[2,256]{1,0:T(2,128)S(1)}, u32[]{:S(2)}, u32[]{:S(2)}) %collective-permute-start.12) | collective-permute-done | bytes 2080 | tf_op jit(solution)/shard_map/ppermute | solution.py:37
  30.9 0.9 %mix_particles.1 = (f32[4,8,64]{2,1,0:T(8,128)}, f32[2,256]{1,0:T(2,128)}) custom-call(f32[80,128]{1,0:T(8,128)S(1)} %adjoint_steps.1.refs_0_, f32[80,128]{1,0:T(8,128)S(1)} %collective-permute-done.4.refs_1_, f32[80,128]{1,0:T(8,128)S(1)} %collective-permute-done.5.refs_2_, f32[80,128]{1,0:T(8,128)S(1)} %collective-permute-done.6.refs_3_, ...), custom_call_target="tpu_custom_call" | custom-call | tf_op jit(solution)/shard_map/mix_particles/pallas_call | solution.py:584
  (16 shorter events, 0.0 us)
Async XLA Ops:
  0.6 4.7 %copy-start.3 = (f32[1,4,8,64]{3,2,1,0:T(8,128)S(1)}, f32[1,4,8,64]{3,2,1,0:T(8,128)}, u32[]{:S(2)}) copy-start(f32[1,4,8,64]{3,2,1,0:T(8,128)} %param.10) | copy-start | bytes 24580
  0.6 13.1 %copy-start = (f32[1,8,16,128]{3,2,1,0:T(8,128)S(1)}, f32[1,8,16,128]{3,2,1,0:T(8,128)}, u32[]{:S(2)}) copy-start(f32[1,8,16,128]{3,2,1,0:T(8,128)} %param.12) | copy-start | bytes 196612
  2.2 11.4 %collective-permute-start = (f32[18,16,128]{2,1,0:T(8,128)S(1)}, f32[18,16,128]{2,1,0:T(8,128)S(1)}, u32[]{:S(2)}, u32[]{:S(2)}) collective-permute-start(f32[18,16,128]{2,1,0:T(8,128)S(1)} %get-tuple-element.28), channel_id=1, source_target_pairs={{0,1},{2,3},{1,0},{3,2},{4,5},{6,7},{5,4},{7,6},{8,9},{10,11},{9,8... | collective-permute-start | bytes 442376 | tf_op jit(solution)/shard_map/ppermute | solution.py:37
  5.3 8.3 %collective-permute-start.1 = (f32[18,16,128]{2,1,0:T(8,128)S(1)}, f32[18,16,128]{2,1,0:T(8,128)S(1)}, u32[]{:S(2)}, u32[]{:S(2)}) collective-permute-start(f32[18,16,128]{2,1,0:T(8,128)S(1)} %get-tuple-element.29), channel_id=1, source_target_pairs={{1,2},{0,4},{3,7},{5,6},{9,10},{8,12},{11,15},{13,14},{17,18},{16,... | collective-permute-start | bytes 442376 | tf_op jit(solution)/shard_map/ppermute | solution.py:37
  5.4 4.9 %collective-permute-start.2 = (f32[4,8,64]{2,1,0:T(8,128)S(1)}, f32[4,8,64]{2,1,0:T(8,128)S(1)}, u32[]{:S(2)}, u32[]{:S(2)}) collective-permute-start(f32[4,8,64]{2,1,0:T(8,128)S(1)} %bitcast.18), channel_id=1, source_target_pairs={{0,1},{2,3},{1,0},{3,2},{4,5},{6,7},{5,4},{7,6},{8,9},{10,11},{9,8... | collective-permute-start | bytes 24584 | tf_op jit(solution)/shard_map/ppermute | solution.py:37
  10.3 4.7 %collective-permute-start.3 = (f32[3,16,128]{2,1,0:T(8,128)S(1)}, f32[3,16,128]{2,1,0:T(8,128)S(1)}, u32[]{:S(2)}, u32[]{:S(2)}) collective-permute-start(f32[3,16,128]{2,1,0:T(8,128)S(1)} %get-tuple-element.37), channel_id=1, source_target_pairs={{0,2},{1,3},{2,0},{3,1},{4,6},{5,7},{6,4},{7,5},{8,10},{9,11},{10,... | collective-permute-start | bytes 73736 | tf_op jit(solution)/shard_map/ppermute | solution.py:37
  13.7 1.3 %copy-start.1 = (f32[1,8,16,128]{3,2,1,0:T(8,128)S(1)}, f32[1,8,16,128]{3,2,1,0:T(8,128)}, u32[]{:S(2)}) copy-start(f32[1,8,16,128]{3,2,1,0:T(8,128)} %param.11) | copy-start | bytes 196612
  13.7 1.3 %copy-start.2 = (f32[1,8,16,128]{3,2,1,0:T(8,128)S(1)}, f32[1,8,16,128]{3,2,1,0:T(8,128)}, u32[]{:S(2)}) copy-start(f32[1,8,16,128]{3,2,1,0:T(8,128)} %param.14) | copy-start | bytes 196612
  15.8 4.9 %collective-permute-start.9 = (f32[80,128]{1,0:T(8,128)S(1)}, f32[80,128]{1,0:T(8,128)S(1)}, u32[]{:S(2)}, u32[]{:S(2)}) collective-permute-start(f32[80,128]{1,0:T(8,128)S(1)} %adjoint_steps.1.refs_0_), channel_id=1, source_target_pairs={{0,24},{4,28},{8,16},{12,20},{24,0},{28,4},{16,8},{20,12},{1,25},{... | collective-permute-start | bytes 122888 | tf_op jit(solution)/shard_map/ppermute | solution.py:37
  18.3 4.0 %collective-permute-start.5 = (f32[80,128]{1,0:T(8,128)S(1)}, f32[80,128]{1,0:T(8,128)S(1)}, u32[]{:S(2)}, u32[]{:S(2)}) collective-permute-start(f32[80,128]{1,0:T(8,128)S(1)} %adjoint_steps.1.refs_0_), channel_id=1, source_target_pairs={{0,8},{4,12},{16,24},{20,28},{8,0},{12,4},{24,16},{28,20},{1,9},{5... | collective-permute-start | bytes 122888 | tf_op jit(solution)/shard_map/ppermute | solution.py:37
  18.8 4.0 %collective-permute-start.7 = (f32[80,128]{1,0:T(8,128)S(1)}, f32[80,128]{1,0:T(8,128)S(1)}, u32[]{:S(2)}, u32[]{:S(2)}) collective-permute-start(f32[80,128]{1,0:T(8,128)S(1)} %adjoint_steps.1.refs_0_), channel_id=1, source_target_pairs={{0,16},{4,20},{8,24},{12,28},{16,0},{20,4},{24,8},{28,12},{1,17},{... | collective-permute-start | bytes 122888 | tf_op jit(solution)/shard_map/ppermute | solution.py:37
  19.3 11.6 %collective-permute-start.4 = (f32[80,128]{1,0:T(8,128)S(1)}, f32[80,128]{1,0:T(8,128)S(1)}, u32[]{:S(2)}, u32[]{:S(2)}) collective-permute-start(f32[80,128]{1,0:T(8,128)S(1)} %adjoint_steps.1.refs_0_), channel_id=1, source_target_pairs={{0,4},{8,12},{16,20},{24,28},{4,0},{12,8},{20,16},{28,24},{1,5},{9... | collective-permute-start | bytes 122888 | tf_op jit(solution)/shard_map/ppermute | solution.py:37
  20.7 10.2 %collective-permute-start.10 = (f32[80,128]{1,0:T(8,128)S(1)}, f32[80,128]{1,0:T(8,128)S(1)}, u32[]{:S(2)}, u32[]{:S(2)}) collective-permute-start(f32[80,128]{1,0:T(8,128)S(1)} %collective-permute-done.9.refs_6_), channel_id=1, source_target_pairs={{0,4},{8,12},{16,20},{24,28},{4,0},{12,8},{20,16},{28,24},{1,5},{9... | collective-permute-start | bytes 122888 | tf_op jit(solution)/shard_map/ppermute | solution.py:37
  22.3 8.6 %collective-permute-start.6 = (f32[80,128]{1,0:T(8,128)S(1)}, f32[80,128]{1,0:T(8,128)S(1)}, u32[]{:S(2)}, u32[]{:S(2)}) collective-permute-start(f32[80,128]{1,0:T(8,128)S(1)} %collective-permute-done.5.refs_2_), channel_id=1, source_target_pairs={{0,4},{8,12},{16,20},{24,28},{4,0},{12,8},{20,16},{28,24},{1,5},{9... | collective-permute-start | bytes 122888 | tf_op jit(solution)/shard_map/ppermute | solution.py:37
  22.8 8.1 %collective-permute-start.8 = (f32[80,128]{1,0:T(8,128)S(1)}, f32[80,128]{1,0:T(8,128)S(1)}, u32[]{:S(2)}, u32[]{:S(2)}) collective-permute-start(f32[80,128]{1,0:T(8,128)S(1)} %collective-permute-done.7.refs_4_), channel_id=1, source_target_pairs={{0,4},{8,12},{16,20},{24,28},{4,0},{12,8},{20,16},{28,24},{1,5},{9... | collective-permute-start | bytes 122888 | tf_op jit(solution)/shard_map/ppermute | solution.py:37
  22.8 3.6 %collective-permute-start.11 = (f32[2,256]{1,0:T(2,128)S(1)}, f32[2,256]{1,0:T(2,128)S(1)}, u32[]{:S(2)}, u32[]{:S(2)}) collective-permute-start(f32[2,256]{1,0:T(2,128)S(1)} %get-tuple-element.39), channel_id=1, source_target_pairs={{0,1},{2,3},{1,0},{3,2},{4,5},{6,7},{5,4},{7,6},{8,9},{10,11},{9,8... | collective-permute-start | bytes 6152 | tf_op jit(solution)/shard_map/ppermute | solution.py:37
  26.4 4.5 %collective-permute-start.12 = (f32[2,256]{1,0:T(2,128)S(1)}, f32[2,256]{1,0:T(2,128)S(1)}, u32[]{:S(2)}, u32[]{:S(2)}) collective-permute-start(f32[2,256]{1,0:T(2,128)S(1)} %add.3.refs_8_), channel_id=1, source_target_pairs={{0,2},{1,3},{2,0},{3,1},{4,6},{5,7},{6,4},{7,5},{8,10},{9,11},{10,... | collective-permute-start | bytes 6152 | tf_op jit(solution)/shard_map/ppermute | solution.py:37
